TPU v7x, 32 devices: a whole 2x2x4 slice. The times are simulated.
32 devices in a mesh: seq: 8 (over z, y), tensor: 4 (over x, core).
Axes of the slice: x: 2, y: 2, z: 4, core: 2. Of those that a mesh axis runs over, the one named last changes fastest.
Arguments:
- block_input: bfloat16 [8192, 1024], P('seq', 'tensor'), may hold values from -8 to 8
- cotangent: bfloat16 [8192, 1024], P('seq', 'tensor'), may hold values from -6 to 6
- image_ids: int32 [8192], replicated, may hold values from -1 to 4, as said below
- qkv_weight: bfloat16 [1024, 3072], P('tensor', 'seq'), may hold values from -7 to 7
- proj_weight: bfloat16 [1024, 1024], P('tensor', 'seq'), may hold values from -1.5 to 1.5
- fc1_weight: bfloat16 [4096, 1024], P('tensor', 'seq'), may hold values from -0.1875 to 0.1875
- fc2_weight: bfloat16 [4096, 1024], P('tensor', 'seq'), may hold values from -0.09375 to 0.09375
- norm1_gain: float32 [1024], P('tensor'), may hold values from 0.25 to 1.75
- norm1_shift: float32 [1024], P('tensor'), may hold values from -3 to 3
- q_bias: float32 [1024], P('tensor'), may hold values from -3 to 3
- v_bias: float32 [1024], P('tensor'), may hold values from -3 to 3
- proj_bias: float32 [1024], P('tensor'), may hold values from -3 to 3
- scale_attn: float32 [1024], P('tensor'), may hold values from 0.5 to 2
- norm2_gain: float32 [1024], P('tensor'), may hold values from 0.25 to 1.75
- norm2_shift: float32 [1024], P('tensor'), may hold values from -3 to 3
- fc1_bias: float32 [4096], P('tensor'), may hold values from -3 to 3
- fc2_bias: float32 [1024], P('tensor'), may hold values from -3 to 3
- scale_mlp: float32 [1024], P('tensor'), may hold values from 0.5 to 2
Outputs:
- block_output: bfloat16 [8192, 1024], P('seq', 'tensor')
- input_grad: bfloat16 [8192, 1024], P('seq', 'tensor')
- qkv_weight_grad: float32 [1024, 3072], P('tensor', 'seq')
- proj_weight_grad: float32 [1024, 1024], P('tensor', 'seq')
- fc1_weight_grad: float32 [4096, 1024], P('tensor', 'seq')
- fc2_weight_grad: float32 [4096, 1024], P('tensor', 'seq')
- norm1_gain_grad: float32 [1024], P('tensor')
- norm1_shift_grad: float32 [1024], P('tensor')
- q_bias_grad: float32 [1024], P('tensor')
- v_bias_grad: float32 [1024], P('tensor')
- proj_bias_grad: float32 [1024], P('tensor')
- scale_attn_grad: float32 [1024], P('tensor')
- norm2_gain_grad: float32 [1024], P('tensor')
- norm2_shift_grad: float32 [1024], P('tensor')
- fc1_bias_grad: float32 [4096], P('tensor')
- fc2_bias_grad: float32 [1024], P('tensor')
- scale_mlp_grad: float32 [1024], P('tensor')
Inputs may be any that keep to these rules, and one draw needn't show every extreme that they name: `image_ids`: tokens of one image are consecutive; there are exactly (5) images, numbered 0, 1, 2 in order of position; each has 686 to 1370 tokens and image 0 has exactly 1370; the tokens after the last image, at least one, are padding with id -1.
All inputs are finite; a program needn't handle non-finite values.
Results may differ from a plain program's by a relative error of at most 0.0095.
The roundings to bfloat16 on the way count: a program that leaves them out, or rounds other values in their place, can miss the bound.
Values may be sent and summed in bfloat16 or wider, within the bound.
No kernel may reach another device: no remote copies, remote signals or barrier semaphores. Data moves between devices by JAX's collectives and lax.ppermute only.
A program may use at most 256 MiB of HBM per device.

v0:
```python
import jax
import jax.numpy as jnp
from jax import lax
from jax.sharding import PartitionSpec as P

HEAD_DIM = 64
IMG = 1370


EPS = 1e-06
NEG = -1e30


def passed_along(block, axis, distance):
    devices = range(lax.axis_size(axis))
    route = [(i - distance, i) for i in devices if i - distance in devices]
    return lax.ppermute(block, axis, route)


def times_t(left, right):
    return lax.dot_general(
        left, right, (((1,), (1,)), ((), ())), preferred_element_type=jnp.float32
    )


def outer_sum(left, right):
    return lax.dot_general(
        left, right, (((0,), (0,)), ((), ())), preferred_element_type=jnp.float32
    )


def plain(left, right):
    return jnp.dot(left, right, preferred_element_type=jnp.float32)


def widen(piece):
    return lax.all_gather(piece, "tensor", axis=1, tiled=True)


def narrow(term):
    return lax.psum_scatter(term, "tensor", scatter_dimension=1, tiled=True)


def row_pair(first, second):
    return lax.psum((jnp.sum(first, axis=1), jnp.sum(second, axis=1)), "tensor")


def normalize(value, gain, shift, width):
    total, square = row_pair(value, value * value)
    mean = total[:, None] / width
    rstd = lax.rsqrt(square[:, None] / width - mean * mean + EPS)
    scaled = (value - mean) * rstd
    return (scaled, rstd, scaled * gain + shift)


def norm_back(grad_normed, scaled, rstd, gain, width):
    grad_scaled = grad_normed * gain
    total, cross = row_pair(grad_scaled, grad_scaled * scaled)
    return rstd * (grad_scaled - total[:, None] / width - scaled * (cross[:, None] / width))


def gelu_exact(inner):
    return jax.nn.gelu(inner, approximate=False)


def column_sum(values):
    return jnp.sum(values.astype(jnp.float32), axis=0)


def per_device(
    block_input,
    cotangent,
    image_ids,
    qkv_weight,
    proj_weight,
    fc1_weight,
    fc2_weight,
    norm1_gain,
    norm1_shift,
    q_bias,
    v_bias,
    proj_bias,
    scale_attn,
    norm2_gain,
    norm2_shift,
    fc1_bias,
    fc2_bias,
    scale_mlp,
):
    row_count = block_input.shape[0]
    width = block_input.shape[1] * lax.axis_size("tensor")
    features = qkv_weight.shape[0]
    heads_here = features // HEAD_DIM
    reach = (IMG - 1 + row_count - 1) // row_count
    places = 2 * reach + 1
    scale = HEAD_DIM ** (-0.5)
    seq_rank = lax.axis_index("seq")
    tile_rows = min(128, row_count)
    qkv_full, proj_full, fc1_full, fc2_full = (
        lax.all_gather(qkv_weight, "seq", axis=1, tiled=True),
        lax.all_gather(proj_weight, "seq", axis=1, tiled=True),
        lax.all_gather(fc1_weight, "seq", axis=1, tiled=True),
        lax.all_gather(fc2_weight, "seq", axis=1, tiled=True),
    )
    qkv_parts = qkv_full.reshape(features, 3, width)
    query_w = qkv_parts[:, 0]
    key_w = qkv_parts[:, 1]
    value_w = qkv_parts[:, 2]
    input_f = block_input.astype(jnp.float32)
    scaled1, rstd1, normal1 = normalize(input_f, norm1_gain, norm1_shift, width)
    normed1 = widen(normal1.astype(jnp.bfloat16))
    query = (times_t(normed1, query_w) + q_bias).astype(jnp.bfloat16)
    own_key = times_t(normed1, key_w).astype(jnp.bfloat16)
    own_value = (times_t(normed1, value_w) + v_bias).astype(jnp.bfloat16)
    own_pair = jnp.stack([own_key, own_value])
    margin_ids = -jnp.ones((reach * row_count,), jnp.int32)
    padded_ids = jnp.concatenate([margin_ids, image_ids, margin_ids])
    first_row = seq_rank * row_count
    query_ids = lax.dynamic_slice_in_dim(image_ids, first_row, row_count, 0)
    pieces = []
    id_pieces = []
    counts = []
    for place in range(places):
        offset = reach - place
        start = first_row + place * row_count
        if offset == 0:
            pieces.append(own_pair)
            id_pieces.append(lax.dynamic_slice_in_dim(padded_ids, start, row_count, 0))
            counts.append(row_count)
        else:
            need = IMG - 1 - (abs(offset) - 1) * row_count
            count = min(row_count, -(-need // tile_rows) * tile_rows)
            if offset > 0:
                sent = own_pair[:, row_count - count :]
                start = start + row_count - count
            else:
                sent = own_pair[:, :count]
            pieces.append(passed_along(sent, "seq", offset))
            id_pieces.append(lax.dynamic_slice_in_dim(padded_ids, start, count, 0))
            counts.append(count)
    near_pair = jnp.concatenate(pieces, axis=1)
    near_key = near_pair[0]
    near_value = near_pair[1]
    key_ids = jnp.concatenate(id_pieces)
    valid_row = (query_ids >= 0)[:, None]
    allowed = (query_ids[:, None] == key_ids[None, :]) & valid_row
    contexts = []
    peaks = []
    totals = []
    for head_index in range(heads_here):
        low_col = head_index * HEAD_DIM
        high_col = low_col + HEAD_DIM
        masked = jnp.where(
            allowed, times_t(query[:, low_col:high_col], near_key[:, low_col:high_col]) * scale, NEG
        )
        peak = jnp.max(masked, axis=1, keepdims=True)
        expon = jnp.where(allowed, jnp.exp(masked - peak), 0.0)
        total = jnp.where(valid_row, jnp.sum(expon, axis=1, keepdims=True), 1.0)
        prob = (expon / total).astype(jnp.bfloat16)
        contexts.append(plain(prob, near_value[:, low_col:high_col]))
        peaks.append(peak)
        totals.append(total)
    context = jnp.concatenate(contexts, axis=1).astype(jnp.bfloat16)
    branch = narrow(plain(context, proj_full))
    branch_total = branch + proj_bias
    middle = input_f + scale_attn * branch_total
    scaled2, rstd2, normal2 = normalize(middle, norm2_gain, norm2_shift, width)
    normed2 = widen(normal2.astype(jnp.bfloat16))
    before = times_t(normed2, fc1_full) + fc1_bias
    hidden = gelu_exact(before).astype(jnp.bfloat16)
    second = narrow(plain(hidden, fc2_full))
    second_total = second + fc2_bias
    block_output = (middle + scale_mlp * second_total).astype(jnp.bfloat16)
    qkv_full, proj_full, fc1_full, fc2_full = (
        lax.all_gather(qkv_weight, "seq", axis=1, tiled=True),
        lax.all_gather(proj_weight, "seq", axis=1, tiled=True),
        lax.all_gather(fc1_weight, "seq", axis=1, tiled=True),
        lax.all_gather(fc2_weight, "seq", axis=1, tiled=True),
    )
    qkv_parts = qkv_full.reshape(features, 3, width)
    query_w = qkv_parts[:, 0]
    key_w = qkv_parts[:, 1]
    value_w = qkv_parts[:, 2]
    grad_out = cotangent.astype(jnp.float32)
    grad_second = grad_out * scale_mlp
    scale_mlp_grad = jnp.sum(grad_out * second_total, axis=0)
    fc2_bias_grad = jnp.sum(grad_second, axis=0)
    second_full = widen(grad_second.astype(jnp.bfloat16))
    grad_hidden = times_t(second_full, fc2_full)
    fc2_grad = outer_sum(hidden, second_full)
    _, gelu_pull = jax.vjp(gelu_exact, before)
    grad_before = gelu_pull(grad_hidden)[0].astype(jnp.bfloat16)
    fc1_bias_grad = column_sum(grad_before)
    fc1_grad = outer_sum(grad_before, normed2)
    grad_normed2 = narrow(plain(grad_before, fc1_full))
    norm2_gain_grad = jnp.sum(grad_normed2 * scaled2, axis=0)
    norm2_shift_grad = jnp.sum(grad_normed2, axis=0)
    grad_middle = grad_out + norm_back(grad_normed2, scaled2, rstd2, norm2_gain, width)
    grad_branch = grad_middle * scale_attn
    scale_attn_grad = jnp.sum(grad_middle * branch_total, axis=0)
    proj_bias_grad = jnp.sum(grad_branch, axis=0)
    branch_full = widen(grad_branch.astype(jnp.bfloat16))
    grad_context = times_t(branch_full, proj_full).astype(jnp.bfloat16)
    proj_grad = outer_sum(context, branch_full)
    query_terms = []
    key_terms = []
    value_terms = []
    for head_index in range(heads_here):
        low_col = head_index * HEAD_DIM
        high_col = low_col + HEAD_DIM
        query_head = query[:, low_col:high_col]
        masked = jnp.where(allowed, times_t(query_head, near_key[:, low_col:high_col]) * scale, NEG)
        weight = jnp.where(allowed, jnp.exp(masked - peaks[head_index]), 0.0) / totals[head_index]
        prob = weight.astype(jnp.bfloat16)
        grad_head = grad_context[:, low_col:high_col]
        grad_prob = times_t(grad_head, near_value[:, low_col:high_col])
        value_terms.append(outer_sum(prob, grad_head))
        rowdot = jnp.sum(weight * grad_prob, axis=1, keepdims=True)
        grad_score = (weight * (grad_prob - rowdot)).astype(jnp.bfloat16)
        query_terms.append(plain(grad_score, near_key[:, low_col:high_col]) * scale)
        key_terms.append(outer_sum(grad_score, query_head) * scale)
    grads_near = jnp.stack(
        [jnp.concatenate(key_terms, axis=1), jnp.concatenate(value_terms, axis=1)]
    )
    returned = jnp.zeros((2, row_count, features), jnp.float32)
    position = 0
    for place in range(places):
        offset = reach - place
        count = counts[place]
        segment = grads_near[:, position : position + count]
        position = position + count
        if offset == 0:
            returned = returned + segment
        else:
            back = passed_along(segment, "seq", -offset)
            if offset > 0:
                back = jnp.pad(back, ((0, 0), (row_count - count, 0), (0, 0)))
            else:
                back = jnp.pad(back, ((0, 0), (0, row_count - count), (0, 0)))
            returned = returned + back
    grad_query = jnp.concatenate(query_terms, axis=1).astype(jnp.bfloat16)
    grad_key = returned[0].astype(jnp.bfloat16)
    grad_value = returned[1].astype(jnp.bfloat16)
    q_bias_grad = column_sum(grad_query)
    v_bias_grad = column_sum(grad_value)
    qkv_grad = jnp.stack(
        [
            outer_sum(grad_query, normed1),
            outer_sum(grad_key, normed1),
            outer_sum(grad_value, normed1),
        ],
        axis=1,
    ).reshape(features, 3 * width)
    grad_normed1 = narrow(
        plain(grad_query, query_w) + plain(grad_key, key_w) + plain(grad_value, value_w)
    )
    norm1_gain_grad = jnp.sum(grad_normed1 * scaled1, axis=0)
    norm1_shift_grad = jnp.sum(grad_normed1, axis=0)
    input_grad = (grad_middle + norm_back(grad_normed1, scaled1, rstd1, norm1_gain, width)).astype(
        jnp.bfloat16
    )
    qkv_out, proj_out, fc1_out, fc2_out = (
        lax.psum_scatter(qkv_grad, "seq", scatter_dimension=1, tiled=True),
        lax.psum_scatter(proj_grad, "seq", scatter_dimension=1, tiled=True),
        lax.psum_scatter(fc1_grad, "seq", scatter_dimension=1, tiled=True),
        lax.psum_scatter(fc2_grad, "seq", scatter_dimension=1, tiled=True),
    )
    vectors = lax.psum(
        (
            norm1_gain_grad,
            norm1_shift_grad,
            q_bias_grad,
            v_bias_grad,
            proj_bias_grad,
            scale_attn_grad,
            norm2_gain_grad,
            norm2_shift_grad,
            fc1_bias_grad,
            fc2_bias_grad,
            scale_mlp_grad,
        ),
        "seq",
    )
    return (
        block_output,
        input_grad,
        qkv_out,
        proj_out,
        fc1_out,
        fc2_out,
        vectors[0],
        vectors[1],
        vectors[2],
        vectors[3],
        vectors[4],
        vectors[5],
        vectors[6],
        vectors[7],
        vectors[8],
        vectors[9],
        vectors[10],
    )


def solution(mesh):
    in_specs = (
        P("seq", "tensor"),
        P("seq", "tensor"),
        P(),
        P("tensor", "seq"),
        P("tensor", "seq"),
        P("tensor", "seq"),
        P("tensor", "seq"),
        P("tensor"),
        P("tensor"),
        P("tensor"),
        P("tensor"),
        P("tensor"),
        P("tensor"),
        P("tensor"),
        P("tensor"),
        P("tensor"),
        P("tensor"),
        P("tensor"),
    )
    out_specs = (
        P("seq", "tensor"),
        P("seq", "tensor"),
        P("tensor", "seq"),
        P("tensor", "seq"),
        P("tensor", "seq"),
        P("tensor", "seq"),
        P("tensor"),
        P("tensor"),
        P("tensor"),
        P("tensor"),
        P("tensor"),
        P("tensor"),
        P("tensor"),
        P("tensor"),
        P("tensor"),
        P("tensor"),
        P("tensor"),
    )
    return jax.shard_map(
        per_device, mesh=mesh, in_specs=in_specs, out_specs=out_specs, check_vma=False
    )
```

profile of v0, /device:TPU:0, one launch (start us, length us, event | category | flops | bytes accessed | tf_op | source)
XLA Modules:
  0.0 1273.1 jit_solution(3247334891451056319)
XLA Ops:
  10.5 8.5 all-reduce.6
  23.5 34.3 %all-gather.10.cloned.1.call-done = bf16[256,3072]{0,1:T(8,128)(2,1)} async-done(((bf16[256,384]{0,1:T(8,128)(2,1)}), bf16[256,3072]{0,1:T(8,128)(2,1)}) %all-gather.10.cloned.1.call-update) | async-done | bytes 1572880 | tf_op jit(solution)/shard_map/all_gather | solution.py:100
  57.8 23.3 %all-gather.8.cloned.1.call-done = bf16[1024,1024]{1,0:T(8,128)(2,1)} async-done(((bf16[1024,256]{1,0:T(8,128)(2,1)}), bf16[1024,1024]{1,0:T(8,128)(2,1)}) %all-gather.8.cloned.1.call-update) | async-done | bytes 2097168 | tf_op jit(solution)/shard_map/all_gather | solution.py:37
  90.9 48.6 %all_gather.30 = bf16[256,1024]{1,0:T(8,128)(2,1)} all-gather(bf16[256,128]{1,0:T(8,128)(2,1)S(1)} %copy-done.46), channel_id=1, replica_groups=mesh['seq'=8,'tensor'=4] {'seq'}, dimensions={1}, use_global_device_ids=true | all-gather | bytes 589824 | tf_op jit(solution)/shard_map/all_gather | solution.py:101
  152.0 10.1 collective-permute-done.2
  162.2 8.6 collective-permute-done.3
  173.5 8.2 fusion.79
  189.7 20.5 %fusion = (f32[1024]{0:T(1024)S(1)}, f32[1024]{0:T(1024)S(1)}, f32[1024]{0:T(1024)S(1)}, f32[1024]{0:T(1024)S(1)}, f32[1024,3840]{1,0:T(8,128)}) fusion(s32[3840]{0:T(1024)S(1)} %constant_dynamic-update-slice_fusion.6, s32[1024]{0:T(1024)S(1)} %get-tuple-element.83, pred[1024]{0:T(1024)(128)(4,1)S(1)} %get-tuple-element.82, f32[1024,3840]{1,0:T(8,128)S(1)} %fusion.73, ...), kind=kOutput, calls=%fused_computation.17 | convolution fusion | flops 558362624 | bytes 64066560 | tf_op jit(solution)/shard_map/dot_general | solution.py:21
  210.2 25.5 %fusion.123 = (f32[1024]{0:T(1024)S(1)}, f32[1024]{0:T(1024)S(1)}, f32[1024]{0:T(1024)S(1)}, f32[1024]{0:T(1024)S(1)}) fusion(f32[1024]{0:T(1024)S(1)} %get-tuple-element.54, f32[1024,3840]{1,0:T(8,128)} %get-tuple-element.108, pred[1024]{0:T(1024)(128)(4,1)S(1)} %get-tuple-element.82, s32[3840]{0:T(1024)S(1)} %constant_dynamic-update-slice_fusion.6, ...), kind=kLoop, calls=%fused_computation.229 | loop fusion | flops 86503424 | bytes 62967808 | tf_op jit(solution)/shard_map/reduce_sum | solution.py:158
  235.7 48.3 %broadcast_divide_fusion.3 = (f32[1024,3840]{1,0:T(8,128)}, f32[1024,3840]{1,0:T(8,128)}, f32[1024,3840]{1,0:T(8,128)}, f32[1024,3840]{1,0:T(8,128)}) fusion(f32[1024]{0:T(1024)S(1)} %get-tuple-element.104, f32[1024]{0:T(1024)S(1)} %get-tuple-element.54, f32[1024,3840]{1,0:T(8,128)} %get-tuple-element.108, pred[1024]{0:T(1024)(128)(4,1)S(1)} %get-tuple-element.82, ...), kind=kLoop, calls=%fused_computation.30 | loop fusion | flops 86507520 | bytes 125882368 | tf_op jit(solution)/shard_map/div | solution.py:159
  315.2 41.6 %reduce-scatter.9.cloned.1.call-done = f32[1024,256]{1,0:T(8,128)} async-done(((f32[1024,1024]{1,0:T(8,128)}), f32[1024,256]{1,0:T(8,128)}) %reduce-scatter.9.cloned.1.call-update) | async-done | bytes 1048592 | tf_op jit(solution)/shard_map/reduce_scatter | solution.py:41
  367.6 41.4 %all-gather.14.cloned.1.call-done = bf16[1024,1024]{1,0:T(8,128)(2,1)} async-done(((bf16[1024,128]{1,0:T(8,128)(2,1)}), bf16[1024,1024]{1,0:T(8,128)(2,1)}) %all-gather.14.cloned.1.call-update) | async-done | bytes 2097168 | tf_op jit(solution)/shard_map/all_gather | solution.py:102
  409.0 23.0 %all-gather.12.cloned.1.call-done = bf16[1024,1024]{1,0:T(8,128)(2,1)} async-done(((bf16[1024,256]{1,0:T(8,128)(2,1)}), bf16[1024,1024]{1,0:T(8,128)(2,1)}) %all-gather.12.cloned.1.call-update) | async-done | bytes 2097168 | tf_op jit(solution)/shard_map/all_gather | solution.py:37
  438.6 18.2 %all-gather.18.cloned.1.call-done = bf16[1024,1024]{1,0:T(8,128)(2,1)} async-done(((bf16[1024,256]{1,0:T(8,128)(2,1)}), bf16[1024,1024]{1,0:T(8,128)(2,1)}) %all-gather.18.cloned.1.call-update) | async-done | bytes 2097168 | tf_op jit(solution)/shard_map/all_gather | solution.py:37
  456.8 52.4 %all-gather.16.cloned.1.call-done = bf16[1024,1024]{1,0:T(8,128)(2,1)} async-done(((bf16[1024,128]{1,0:T(8,128)(2,1)}), bf16[1024,1024]{1,0:T(8,128)(2,1)}) %all-gather.16.cloned.1.call-update) | async-done | bytes 2097168 | tf_op jit(solution)/shard_map/all_gather | solution.py:103
  509.3 16.1 %convert_reduce_fusion = (f32[1024]{0:T(1024)}, bf16[1024,1024]{1,0:T(8,128)(2,1)S(1)}, f32[1024,1024]{1,0:T(8,128)}) fusion(f32[1024,1024]{1,0:T(8,128)} %fusion.129, f32[1024]{0:T(1024)S(1)} %copy-done.50, bf16[1024,1024]{1,0:T(8,128)(2,1)} %all-gather.18.cloned.1.call-done, bf16[1024,1024]{1,0:T(8,128)(2,1)} %all-gather.16.cloned.1.call-done), kind=kOutput, calls=%fused_computation.37 | convolution fusion | flops 2226125824 | bytes 14688256 | tf_op jit(solution)/shard_map/dot_general | solution.py:21
  541.6 32.2 %reduce-scatter.13.cloned.1.call-done = f32[1024,256]{1,0:T(8,128)} async-done(((f32[1024,1024]{1,0:T(8,128)}), f32[1024,256]{1,0:T(8,128)}) %reduce-scatter.13.cloned.1.call-update) | async-done | bytes 1048592 | tf_op jit(solution)/shard_map/reduce_scatter | solution.py:41
  582.3 38.5 %reduce-scatter.11.cloned.1.call-done = f32[1024,256]{1,0:T(8,128)} async-done(((f32[1024,1024]{1,0:T(8,128)}), f32[1024,256]{1,0:T(8,128)}) %reduce-scatter.11.cloned.1.call-update) | async-done | bytes 1048592 | tf_op jit(solution)/shard_map/reduce_scatter | solution.py:41
  626.1 22.9 %all-gather.20.cloned.1.call-done = bf16[1024,1024]{1,0:T(8,128)(2,1)} async-done(((bf16[1024,256]{1,0:T(8,128)(2,1)}), bf16[1024,1024]{1,0:T(8,128)(2,1)}) %all-gather.20.cloned.1.call-update) | async-done | bytes 2097168 | tf_op jit(solution)/shard_map/all_gather | solution.py:37
  659.5 8.8 fusion.18
  680.9 12.6 multiply_reduce_fusion.1
  693.4 12.6 multiply_reduce_fusion.2
  713.3 23.9 %multiply_convert_fusion = (bf16[1024,3840]{1,0:T(8,128)(2,1)}, bf16[1024,3840]{1,0:T(8,128)(2,1)S(1)}) fusion(f32[1024,3840]{1,0:T(8,128)} %get-tuple-element.98, f32[1024,3840]{1,0:T(8,128)} %get-tuple-element.110, f32[1024]{0:T(1024)S(1)} %get-tuple-element.109, f32[1024,3840]{1,0:T(8,128)} %get-tuple-element.97, f32[1024,3840]{1,0:T(8,128)} %get-tuple-element.112, ...), kind=kLoop, calls=%fused_computation | loop fusion | flops 23592960 | bytes 78651392 | tf_op jit(solution)/shard_map/convert_element_type | solution.py:219
  744.4 27.0 %multiply_convert_fusion.2 = (bf16[1024,3840]{1,0:T(8,128)(2,1)}, bf16[1024,3840]{1,0:T(8,128)(2,1)}) fusion(f32[1024,3840]{1,0:T(8,128)} %get-tuple-element.99, f32[1024,3840]{1,0:T(8,128)} %get-tuple-element.114, f32[1024]{0:T(1024)S(1)} %get-tuple-element.113, f32[1024,3840]{1,0:T(8,128)} %get-tuple-element.96, f32[1024,3840]{1,0:T(8,128)} %get-tuple-element.116, ...), kind=kLoop, calls=%fused_computation.4 | loop fusion | flops 23592960 | bytes 78651392 | tf_op jit(solution)/shard_map/convert_element_type | solution.py:219
  818.6 36.2 %collective-permute-done.4 = f32[2,384,256]{1,2,0:T(8,128)S(1)} collective-permute-done((f32[2,384,256]{1,2,0:T(8,128)}, f32[2,384,256]{1,2,0:T(8,128)S(1)}, u32[]{:S(2)}, u32[]{:S(2)}) %collective-permute-start.4) | collective-permute-done | bytes 786464 | tf_op jit(solution)/shard_map/ppermute | solution.py:17
  855.7 26.2 %collective-permute-done.6 = f32[2,1024,256]{1,2,0:T(8,128)} collective-permute-done((f32[2,1024,256]{1,2,0:T(8,128)}, f32[2,1024,256]{1,2,0:T(8,128)}, u32[]{:S(2)}, u32[]{:S(2)}) %collective-permute-start.6) | collective-permute-done | bytes 2097184 | tf_op jit(solution)/shard_map/ppermute | solution.py:17
  917.0 49.6 %reduce-scatter.17.cloned.1.call-done = f32[256,384]{0,1:T(8,128)} async-done(((f32[256,3072]{0,1:T(8,128)}), f32[256,384]{0,1:T(8,128)}) %reduce-scatter.17.cloned.1.call-update) | async-done | bytes 393232 | tf_op jit(solution)/shard_map/reduce_scatter | solution.py:263
  968.6 44.0 %reduce-scatter.15.cloned.1.call-done = f32[1024,256]{1,0:T(8,128)} async-done(((f32[1024,1024]{1,0:T(8,128)}), f32[1024,256]{1,0:T(8,128)}) %reduce-scatter.15.cloned.1.call-update) | async-done | bytes 1048592 | tf_op jit(solution)/shard_map/reduce_scatter | solution.py:41
  1014.6 39.2 %all-reduce.2 = (f32[256]{0:T(256)}, f32[256]{0:T(256)}, f32[256]{0:T(256)}, f32[256]{0:T(256)}, f32[256]{0:T(256)}, /*index=5*/f32[256]{0:T(256)}, f32[256]{0:T...) all-reduce(f32[256]{0:T(256)S(1)} %get-tuple-element.36, ...), channel_id=1, replica_groups=mesh['seq'=8,'tensor'=4] {'seq'}, use_global_device_ids=true, to_apply=%region_37.38 | all-reduce | flops 3584 | bytes 28672 | tf_op jit(solution)/shard_map/psum | solution.py:268
  1062.5 43.3 %reduce-scatter.23.cloned.1.call-done = f32[1024,128]{1,0:T(8,128)} async-done(((f32[1024,1024]{1,0:T(8,128)}), f32[1024,128]{1,0:T(8,128)}) %reduce-scatter.23.cloned.1.call-update) | async-done | bytes 524304 | tf_op jit(solution)/shard_map/reduce_scatter | solution.py:266
  1105.8 92.4 %reduce-scatter.21.cloned.1.call-done = f32[1024,128]{1,0:T(8,128)} async-done(((f32[1024,1024]{1,0:T(8,128)}), f32[1024,128]{1,0:T(8,128)}) %reduce-scatter.21.cloned.1.call-update) | async-done | bytes 524304 | tf_op jit(solution)/shard_map/reduce_scatter | solution.py:265
  1198.3 68.2 %reduce-scatter.19.cloned.1.call-done = f32[256,128]{1,0:T(8,128)} async-done(((f32[256,1024]{1,0:T(8,128)}), f32[256,128]{1,0:T(8,128)}) %reduce-scatter.19.cloned.1.call-update) | async-done | bytes 131088 | tf_op jit(solution)/shard_map/reduce_scatter | solution.py:264
  (309 shorter events, 251.6 us)
Async XLA Ops:
  7.2 50.6 %all-gather.10.cloned.1.call-start = ((), (), s32[]{:S(2)}) async-start(), calls=%async_computation.9 | async-start | bytes 1769472 | tf_op jit(solution)/shard_map/all_gather | solution.py:100
  9.0 72.1 %all-gather.8.cloned.1.call-start = ((), (), s32[]{:S(2)}) async-start(), calls=%async_computation.8 | async-start | bytes 2621440 | tf_op jit(solution)/shard_map/all_gather | solution.py:37
  21.8 334.9 %reduce-scatter.9.cloned.1.call-start = ((), (), s32[]{:S(2)}) async-start(), calls=%async_computation.10 | async-start | bytes 5242880 | tf_op jit(solution)/shard_map/reduce_scatter | solution.py:41
  86.6 64.0 %collective-permute-start.1 = (bf16[2,1024,256]{2,1,0:T(8,128)(2,1)}, bf16[2,1024,256]{2,1,0:T(8,128)(2,1)}, u32[]{:S(2)}, u32[]{:S(2)}) collective-permute-start(bf16[2,1024,256]{2,1,0:T(8,128)(2,1)} %pad_maximum_fusion.1), channel_id=1, source_target_pairs={{0,4},{4,8},{8,12},{12,16},{16,20},{20,24},{24,28},{1,5},{5,9},{9,... | collective-permute-start | bytes 3145736 | tf_op jit(solution)/shard_map/ppermute | solution.py:17
  139.5 22.6 %collective-permute-start.2 = (bf16[2,1024,256]{2,1,0:T(8,128)(2,1)}, bf16[2,1024,256]{2,1,0:T(8,128)(2,1)S(1)}, u32[]{:S(2)}, u32[]{:S(2)}) collective-permute-start(bf16[2,1024,256]{2,1,0:T(8,128)(2,1)} %pad_maximum_fusion.1), channel_id=1, source_target_pairs={{4,0},{8,4},{12,8},{16,12},{20,16},{24,20},{28,24},{5,1},{9,5},{13... | collective-permute-start | bytes 3145736 | tf_op jit(solution)/shard_map/ppermute | solution.py:17
  140.9 9.7 collective-permute-start
  145.4 25.4 %collective-permute-start.3 = (bf16[2,384,256]{2,1,0:T(8,128)(2,1)S(1)}, bf16[2,384,256]{2,1,0:T(8,128)(2,1)S(1)}, u32[]{:S(2)}, u32[]{:S(2)}) collective-permute-start(bf16[2,384,256]{2,1,0:T(8,128)(2,1)S(1)} %get-tuple-element.94), channel_id=1, source_target_pairs={{8,0},{12,4},{16,8},{20,12},{24,16},{28,20},{9,1},{13,5},{17,9},{2... | collective-permute-start | bytes 1179656 | tf_op jit(solution)/shard_map/ppermute | solution.py:17
  171.1 137.3 %copy-start.3 = (bf16[3840,256]{1,0:T(8,128)(2,1)}, bf16[3840,256]{1,0:T(8,128)(2,1)S(1)}, u32[]{:S(2)}) copy-start(bf16[3840,256]{1,0:T(8,128)(2,1)S(1)} %get-tuple-element.88) | copy-start | bytes 5898244
  314.5 94.5 %all-gather.14.cloned.1.call-start = ((), (), s32[]{:S(2)}) async-start(), calls=%async_computation.12 | async-start | bytes 2359296 | tf_op jit(solution)/shard_map/all_gather | solution.py:102
  315.1 116.9 %all-gather.12.cloned.1.call-start = ((), (), s32[]{:S(2)}) async-start(), calls=%async_computation.11 | async-start | bytes 2621440 | tf_op jit(solution)/shard_map/all_gather | solution.py:37
  365.8 91.0 %all-gather.18.cloned.1.call-start = ((), (), s32[]{:S(2)}) async-start(), calls=%async_computation.15 | async-start | bytes 2621440 | tf_op jit(solution)/shard_map/all_gather | solution.py:37
  366.8 142.5 %all-gather.16.cloned.1.call-start = ((), (), s32[]{:S(2)}) async-start(), calls=%async_computation.13 | async-start | bytes 2359296 | tf_op jit(solution)/shard_map/all_gather | solution.py:103
  367.6 141.7 %copy-start.50 = (f32[1024]{0:T(1024)S(1)}, f32[1024]{0:T(1024)}, u32[]{:S(2)}) copy-start(f32[1024]{0:T(1024)} %param.33) | copy-start | bytes 12292
  367.6 206.2 %reduce-scatter.13.cloned.1.call-start = ((), (), s32[]{:S(2)}) async-start(), calls=%async_computation.16 | async-start | bytes 5242880 | tf_op jit(solution)/shard_map/reduce_scatter | solution.py:41
  531.1 89.7 %reduce-scatter.11.cloned.1.call-start = ((), (), s32[]{:S(2)}) async-start(), calls=%async_computation.14 | async-start | bytes 5242880 | tf_op jit(solution)/shard_map/reduce_scatter | solution.py:41
  541.6 107.5 %all-gather.20.cloned.1.call-start = ((), (), s32[]{:S(2)}) async-start(), calls=%async_computation.17 | async-start | bytes 2621440 | tf_op jit(solution)/shard_map/all_gather | solution.py:37
  626.1 340.6 %reduce-scatter.17.cloned.1.call-start = ((), (), s32[]{:S(2)}) async-start(), calls=%async_computation.19 | async-start | bytes 3538944 | tf_op jit(solution)/shard_map/reduce_scatter | solution.py:263
  787.1 67.7 %collective-permute-start.5 = (f32[2,1024,256]{1,2,0:T(8,128)}, f32[2,1024,256]{1,2,0:T(8,128)}, u32[]{:S(2)}, u32[]{:S(2)}) collective-permute-start(f32[2,1024,256]{1,2,0:T(8,128)} %get-tuple-element.86), channel_id=1, source_target_pairs={{4,0},{8,4},{12,8},{16,12},{20,16},{24,20},{28,24},{5,1},{9,5},{13... | collective-permute-start | bytes 6291464 | tf_op jit(solution)/shard_map/ppermute | solution.py:17
  788.4 93.5 %collective-permute-start.6 = (f32[2,1024,256]{1,2,0:T(8,128)}, f32[2,1024,256]{1,2,0:T(8,128)}, u32[]{:S(2)}, u32[]{:S(2)}) collective-permute-start(f32[2,1024,256]{1,2,0:T(8,128)} %get-tuple-element.87), channel_id=1, source_target_pairs={{0,4},{4,8},{8,12},{12,16},{16,20},{20,24},{24,28},{1,5},{5,9},{9,... | collective-permute-start | bytes 6291464 | tf_op jit(solution)/shard_map/ppermute | solution.py:17
  800.6 54.2 %collective-permute-start.4 = (f32[2,384,256]{1,2,0:T(8,128)}, f32[2,384,256]{1,2,0:T(8,128)S(1)}, u32[]{:S(2)}, u32[]{:S(2)}) collective-permute-start(f32[2,384,256]{1,2,0:T(8,128)} %get-tuple-element.84), channel_id=1, source_target_pairs={{8,0},{12,4},{16,8},{20,12},{24,16},{28,20},{9,1},{13,5},{17,9},{2... | collective-permute-start | bytes 2359304 | tf_op jit(solution)/shard_map/ppermute | solution.py:17
  801.9 52.9 %collective-permute-start.7 = (f32[2,384,256]{1,2,0:T(8,128)}, f32[2,384,256]{1,2,0:T(8,128)}, u32[]{:S(2)}, u32[]{:S(2)}) collective-permute-start(f32[2,384,256]{1,2,0:T(8,128)} %get-tuple-element.85), channel_id=1, source_target_pairs={{0,8},{4,12},{8,16},{12,20},{16,24},{20,28},{1,9},{5,13},{9,17},{1... | collective-permute-start | bytes 2359304 | tf_op jit(solution)/shard_map/ppermute | solution.py:17
  892.2 120.4 %reduce-scatter.15.cloned.1.call-start = ((), (), s32[]{:S(2)}) async-start(), calls=%async_computation.18 | async-start | bytes 5242880 | tf_op jit(solution)/shard_map/reduce_scatter | solution.py:41
  896.8 209.1 %reduce-scatter.23.cloned.1.call-start = ((), (), s32[]{:S(2)}) async-start(), calls=%async_computation.22 | async-start | bytes 4718592 | tf_op jit(solution)/shard_map/reduce_scatter | solution.py:266
  904.6 293.7 %reduce-scatter.21.cloned.1.call-start = ((), (), s32[]{:S(2)}) async-start(), calls=%async_computation.21 | async-start | bytes 4718592 | tf_op jit(solution)/shard_map/reduce_scatter | solution.py:265
  912.3 102.2 %copy-start.51 = (f32[256]{0:T(256)S(1)}, f32[256]{0:T(256)}, u32[]{:S(2)}) copy-start(f32[256]{0:T(256)} %get-tuple-element.34) | copy-start | bytes 3076
  912.3 102.2 %copy-start.52 = (f32[256]{0:T(256)S(1)}, f32[256]{0:T(256)}, u32[]{:S(2)}) copy-start(f32[256]{0:T(256)} %get-tuple-element.40) | copy-start | bytes 3076
  912.3 102.2 %copy-start.53 = (f32[1024]{0:T(1024)S(1)}, f32[1024]{0:T(1024)}, u32[]{:S(2)}) copy-start(f32[1024]{0:T(1024)} %get-tuple-element.77) | copy-start | bytes 12292
  912.3 102.2 %copy-start.56 = (f32[256]{0:T(256)S(1)}, f32[256]{0:T(256)}, u32[]{:S(2)}) copy-start(f32[256]{0:T(256)} %get-tuple-element.46) | copy-start | bytes 3076
  912.3 102.2 %copy-start.57 = (f32[256]{0:T(256)S(1)}, f32[256]{0:T(256)}, u32[]{:S(2)}) copy-start(f32[256]{0:T(256)} %get-tuple-element.47) | copy-start | bytes 3076
  912.3 102.2 %copy-start.58 = (f32[256]{0:T(256)S(1)}, f32[256]{0:T(256)}, u32[]{:S(2)}) copy-start(f32[256]{0:T(256)} %get-tuple-element.91) | copy-start | bytes 3076
  912.4 147.6 %copy-start.11 = (f32[1024,256]{1,0:T(8,128)S(1)}, f32[1024,256]{1,0:T(8,128)}, u32[]{:S(2)}) copy-start(f32[1024,256]{1,0:T(8,128)} %copy-done.10) | copy-start | bytes 3145732
  912.4 354.1 %reduce-scatter.19.cloned.1.call-start = ((), (), s32[]{:S(2)}) async-start(), calls=%async_computation.20 | async-start | bytes 1179648 | tf_op jit(solution)/shard_map/reduce_scatter | solution.py:264
  (79 other events, 1812.0 us)
Sparse Core Ops, SparseCore 0:
  10.8 46.9 all-gather.9
  59.9 21.1 all-gather.7
  314.7 42.0 reduce-scatter.8
  358.6 50.3 all-gather.13
  411.0 20.9 all-gather.11
  434.0 22.8 all-gather.17
  458.9 50.3 all-gather.15
  531.2 42.5 reduce-scatter.12
  576.3 44.3 reduce-scatter.10
  626.2 22.8 all-gather.19
  892.3 74.3 reduce-scatter.16
  969.0 43.4 reduce-scatter.14
  1016.8 89.0 reduce-scatter.22
  1109.9 88.3 reduce-scatter.20
  1202.1 64.2 reduce-scatter.18
where the time goes:
time: 1280 us; the launch traced here: 1270 us
  waiting for transfers between devices  710 us (55%)
  matrix products  218 us (17%)
  other arithmetic  166 us (13%)
  blocking collectives  115 us (9%)
  starting transfers between devices  26.2 us (2%)
  local copies, waits for them, and re-layouts  22.7 us (2%)
  between operations  15.3 us (1%)
    reduce_scatter x4, waiting for transfers between devices, narrow(): return lax.psum_scatter(term, 'tensor', scatter_dimension=1, tiled=True)  156 us
    dot_general x14, matrix products, times_t(): lax.dot_general(left, right, (((1,), (1,)), ((), ())), preferred_element_...  109 us
    reduce_scatter x1, waiting for transfers between devices, per_device(): lax.psum_scatter(fc1_grad, 'seq', scatter_dimension=1, tiled=True)  92.4 us
    all_gather x4, waiting for transfers between devices, widen(): return lax.all_gather(piece, 'tensor', axis=1, tiled=True)  87.5 us
    ppermute x8, waiting for transfers between devices, passed_along(): return lax.ppermute(block, axis, route)  83.2 us
    reduce_scatter x1, waiting for transfers between devices, per_device(): lax.psum_scatter(proj_grad, 'seq', scatter_dimension=1, tiled=True)  68.2 us
    dot_general x14, matrix products, plain(): return jnp.dot(left, right, preferred_element_type=jnp.float32)  56.5 us
    dot_general x14, matrix products, outer_sum(): lax.dot_general(left, right, (((0,), (0,)), ((), ())), preferred_element_...  53.2 us
  transfers between devices with their start and end apart: 23, of which 20 were waited for; matrix products, arithmetic and copies ran while one was open for 6% of the time, Pallas kernels for 0%

commit v1 on v0

v1 whole, which is shorter than its diff:
```python
import functools

import jax
import jax.numpy as jnp
from jax import lax
from jax.experimental import pallas as pl
from jax.experimental.pallas import tpu as pltpu
from jax.sharding import PartitionSpec as P

HEAD_DIM = 64
IMG = 1370
IMG_LEAST = 686
EPS = 1e-06
NEG = -1e30
BF = jnp.bfloat16
F32 = jnp.float32
TILE = 256
PAIR = 2 * HEAD_DIM
SCALE = HEAD_DIM ** (-0.5)
INV_SQRT2 = 0.7071067811865476
INV_SQRT2PI = 0.3989422804014327


def px(value, bits):
    pairs = [(i, i ^ bits) for i in range(lax.axis_size("tensor"))]
    return lax.ppermute(value, "tensor", pairs)


def ps(value, bits):
    pairs = [(i, i ^ bits) for i in range(lax.axis_size("seq"))]
    return lax.ppermute(value, "seq", pairs)


def passed_along(block, distance):
    devices = range(lax.axis_size("seq"))
    route = [(i - distance, i) for i in devices if i - distance in devices]
    return lax.ppermute(block, "seq", route)


def gather4(value):
    across = px(value, 2)
    return [value, px(value, 1), across, px(across, 1)]


def swap4(pieces):
    return [pieces[0]] + [px(pieces[r], r) for r in range(1, 4)]


def rows_at(value, index, size):
    return lax.dynamic_slice_in_dim(value, index * size, size, 0)


def unxor(pieces, t):
    low = (t & 1) == 1
    high = (t & 2) == 2
    first = [jnp.where(low, pieces[r ^ 1], pieces[r]) for r in range(4)]
    return [jnp.where(high, first[r ^ 2], first[r]) for r in range(4)]


def nt(left, right):
    return lax.dot_general(left, right, (((1,), (1,)), ((), ())), preferred_element_type=F32)


def nn(left, right):
    return lax.dot_general(left, right, (((1,), (0,)), ((), ())), preferred_element_type=F32)


def tn(left, right):
    return lax.dot_general(left, right, (((0,), (0,)), ((), ())), preferred_element_type=F32)


def params(n=1, limit=56):
    return pltpu.CompilerParams(
        dimension_semantics=("arbitrary",) * n, vmem_limit_bytes=limit * 1024 * 1024
    )


def stats_of(chunks, width):
    total = sum(jnp.sum(c, axis=1, keepdims=True) for c in chunks)
    square = sum(jnp.sum(c * c, axis=1, keepdims=True) for c in chunks)
    mean = total / width
    rstd = lax.rsqrt(square / width - mean * mean + EPS)
    return mean, rstd


def qkv_kernel(sc, x0, x1, x2, x3, w_ref, vec, qb, vb, n1_ref, q_ref, kv0_ref, kv1_ref, wout, wscr):
    groups = w_ref.shape[0]
    part = w_ref.shape[2]
    features = w_ref.shape[1]

    @pl.when(pl.program_id(0) == 0)
    def _():
        for g in range(groups):
            wscr[:, g * part : (g + 1) * part] = w_ref[g]
        wout[...] = wscr[...]

    t = sc[0]
    chunks = unxor([r[...].astype(F32) for r in (x0, x1, x2, x3)], t)
    fw = x0.shape[1]
    width = 4 * fw
    mean, rstd = stats_of(chunks, width)
    for a in range(4):
        lo = a * fw
        scaled = (chunks[a] - mean) * rstd
        n1_ref[:, lo : lo + fw] = (
            scaled * vec[0:1, lo : lo + fw] + vec[1:2, lo : lo + fw]
        ).astype(BF)
    normed = n1_ref[...]
    query = nt(normed, wscr[:, 0:width]) + qb[...]
    q_ref[...] = query.astype(BF)
    key = nt(normed, wscr[:, width : 2 * width]).astype(BF)
    value = (nt(normed, wscr[:, 2 * width : 3 * width]) + vb[...]).astype(BF)
    for p, ref in enumerate((kv0_ref, kv1_ref)):
        ref[:, 0:PAIR] = key[:, p * PAIR : (p + 1) * PAIR]
        ref[:, PAIR : 2 * PAIR] = value[:, p * PAIR : (p + 1) * PAIR]


def qkv_call(sc, xs, w, vec, qb, vb):
    rows, fw = xs[0].shape
    groups, features, part = w.shape
    width = 4 * fw
    tile = TILE

    def full(shape):
        return pl.BlockSpec(shape, lambda i, sc: (0,) * len(shape))

    def row(n):
        return pl.BlockSpec((tile, n), lambda i, sc: (i, 0))

    return pl.pallas_call(
        qkv_kernel,
        grid_spec=pltpu.PrefetchScalarGridSpec(
            num_scalar_prefetch=1,
            grid=(rows // tile,),
            in_specs=[row(fw)] * 4
            + [full(w.shape), full(vec.shape), full(qb.shape), full(vb.shape)],
            out_specs=[
                row(width),
                row(features),
                row(2 * PAIR),
                row(2 * PAIR),
                full((features, groups * part)),
            ],
            scratch_shapes=[pltpu.VMEM((features, groups * part), BF)],
        ),
        out_shape=[
            jax.ShapeDtypeStruct((rows, width), BF),
            jax.ShapeDtypeStruct((rows, features), BF),
            jax.ShapeDtypeStruct((rows, 2 * PAIR), BF),
            jax.ShapeDtypeStruct((rows, 2 * PAIR), BF),
            jax.ShapeDtypeStruct((features, groups * part), BF),
        ],
        compiler_params=params(),
        name="qkv",
    )(sc, *xs, w, vec, qb, vb)


def load_pieces(pieces, target, sem, offsets, counts):
    copies = [
        pltpu.make_async_copy(ref, target.at[pl.ds(offset, count), :], sem.at[k])
        for k, (ref, offset, count) in enumerate(zip(pieces, offsets, counts))
    ]
    for copy in copies:
        copy.start()
    for copy in copies:
        copy.wait()


def head_lanes(shape, head):
    lane = lax.broadcasted_iota(jnp.int32, shape, 1)
    return (lane >= head * HEAD_DIM) & (lane < (head + 1) * HEAD_DIM)


def scores_of(kv, head_query, j, start, end):
    raw = nt(kv[pl.ds(pl.multiple_of(j * TILE, TILE), TILE), 0:PAIR], head_query)
    place = lax.broadcasted_iota(jnp.int32, raw.shape, 0) + j * TILE
    return jnp.where((place >= start) & (place < end), raw, NEG)


def fold8(values, how):
    return how(values.reshape(values.shape[0] // 8, 8, values.shape[1]), axis=0)


def fwd_kernel(offsets, counts, sc, q_ref, se_ref, *refs):
    n = len(counts)
    pieces = refs[:n]
    ctx_ref, st_ref, kv, s_scr, acc, sem = refs[n:]
    i = pl.program_id(0)

    @pl.when(i == 0)
    def _():
        load_pieces(pieces, kv, sem, offsets, counts)

    lo = sc[1 + 2 * i]
    hi = sc[2 + 2 * i]
    start = se_ref[0:1, :]
    end = se_ref[1:2, :]
    query = q_ref[...].astype(F32) * SCALE
    for head in range(2):
        head_query = jnp.where(head_lanes(query.shape, head), query, 0.0).astype(BF)

        def first(j, peak):
            score = scores_of(kv, head_query, j, start, end)
            s_scr[j - lo] = score
            return jnp.maximum(peak, fold8(score, jnp.max))

        peak8 = lax.fori_loop(lo, hi, first, jnp.full((8, TILE), NEG, F32))
        peak = jnp.max(peak8, axis=0, keepdims=True)
        peak = jnp.maximum(peak, 0.1 * NEG)

        def second(j, total):
            expon = jnp.exp(s_scr[j - lo] - peak)
            s_scr[j - lo] = expon
            return total + fold8(expon, jnp.sum)

        total8 = lax.fori_loop(lo, hi, second, jnp.zeros((8, TILE), F32))
        total = jnp.sum(total8, axis=0, keepdims=True)
        inverse = 1.0 / jnp.where(end > start, total, 1.0)
        acc[head] = jnp.zeros(acc.shape[1:], F32)

        def third(j, carry):
            prob = (s_scr[j - lo] * inverse).astype(BF)
            vals = kv[pl.ds(pl.multiple_of(j * TILE, TILE), TILE), PAIR : 2 * PAIR]
            acc[head] += tn(vals, prob)
            return carry

        lax.fori_loop(lo, hi, third, 0)
        st_ref[head : head + 1, :] = peak
        st_ref[2 + head : 3 + head, :] = inverse
    both = jnp.concatenate([acc[0, 0:HEAD_DIM, :], acc[1, HEAD_DIM:PAIR, :]], axis=0)
    ctx_ref[...] = both.T.astype(BF)


def fwd_call(pair, sc, query, spans, pieces, offsets, counts):
    rows = query.shape[0]
    near = sum(counts)
    return pl.pallas_call(
        functools.partial(fwd_kernel, offsets, counts),
        grid_spec=pltpu.PrefetchScalarGridSpec(
            num_scalar_prefetch=1,
            grid=(rows // TILE,),
            in_specs=[
                pl.BlockSpec((TILE, PAIR), lambda i, sc: (i, pair)),
                pl.BlockSpec((8, TILE), lambda i, sc: (0, i)),
            ]
            + [pl.BlockSpec(memory_space=pl.ANY)] * len(pieces),
            out_specs=[
                pl.BlockSpec((TILE, PAIR), lambda i, sc: (i, 0)),
                pl.BlockSpec((8, TILE), lambda i, sc: (0, i)),
            ],
            scratch_shapes=[
                pltpu.VMEM((near, 2 * PAIR), BF),
                pltpu.VMEM((near // TILE, TILE, TILE), F32),
                pltpu.VMEM((2, PAIR, TILE), F32),
                pltpu.SemaphoreType.DMA((len(pieces),)),
            ],
        ),
        out_shape=[
            jax.ShapeDtypeStruct((rows, PAIR), BF),
            jax.ShapeDtypeStruct((8, rows), F32),
        ],
        compiler_params=params(),
        name="attn_fwd",
    )(sc, query, spans, *pieces)


def bwd_kernel(offsets, counts, own, sc, q_ref, se_ref, st_ref, g_ref, *refs):
    n = len(counts)
    pieces = refs[:n]
    dq_ref = refs[n]
    outs = refs[n + 1 : 2 * n + 1]
    kv, w_scr, g_scr, acc, dq_scr, sem = refs[2 * n + 1 :]
    r = pl.program_id(0)

    @pl.when(r == 0)
    def _():
        load_pieces(pieces, kv, sem, offsets, counts)
        acc[...] = jnp.zeros(acc.shape, F32)

    i = sc[0] ^ r
    lo = sc[1 + 2 * i]
    hi = sc[2 + 2 * i]
    start = se_ref[0:1, :]
    end = se_ref[1:2, :]
    query = q_ref[...].astype(F32) * SCALE
    grad = g_ref[0].astype(F32)
    for head in range(2):
        lanes = head_lanes(query.shape, head)
        head_query = jnp.where(lanes, query, 0.0).astype(BF)
        head_grad = jnp.where(lanes, grad, 0.0).astype(BF)
        peak = st_ref[head : head + 1, :]
        inverse = st_ref[2 + head : 3 + head, :]

        def first(j, dot8):
            score = scores_of(kv, head_query, j, start, end)
            weight = jnp.exp(score - peak) * inverse
            vals = kv[pl.ds(pl.multiple_of(j * TILE, TILE), TILE), PAIR : 2 * PAIR]
            grad_prob = nt(vals, head_grad)
            w_scr[j - lo] = weight
            g_scr[j - lo] = grad_prob
            return dot8 + fold8(weight * grad_prob, jnp.sum)

        dot8 = lax.fori_loop(lo, hi, first, jnp.zeros((8, TILE), F32))
        rowdot = jnp.sum(dot8, axis=0, keepdims=True)
        dq_scr[head] = jnp.zeros(dq_scr.shape[1:], F32)

        def second(j, carry):
            weight = w_scr[j - lo]
            grad_score = (weight * (g_scr[j - lo] - rowdot)).astype(BF)
            prob = weight.astype(BF)
            at = pl.ds(pl.multiple_of(j * TILE, TILE), TILE)
            acc[at, 0:PAIR] += nn(grad_score, head_query)
            acc[at, PAIR : 2 * PAIR] += nn(prob, head_grad)
            dq_scr[head] += tn(kv[at, 0:PAIR], grad_score)
            return carry

        lax.fori_loop(lo, hi, second, 0)
    both = jnp.concatenate([dq_scr[0, 0:HEAD_DIM, :], dq_scr[1, HEAD_DIM:PAIR, :]], axis=0)
    dq_ref[...] = (both.T * SCALE).astype(BF)

    @pl.when(r == pl.num_programs(0) - 1)
    def _():
        for k in range(n):
            piece = acc[offsets[k] : offsets[k] + counts[k], :]
            outs[k][...] = piece.astype(outs[k].dtype)


def bwd_call(pair, sc, query, spans, stats, grads, pieces, offsets, counts, own):
    rows = query.shape[0]
    near = sum(counts)

    def whole(count):
        return pl.BlockSpec((count, 2 * PAIR), lambda r, sc: (0, 0))

    return pl.pallas_call(
        functools.partial(bwd_kernel, offsets, counts, own),
        grid_spec=pltpu.PrefetchScalarGridSpec(
            num_scalar_prefetch=1,
            grid=(rows // TILE,),
            in_specs=[
                pl.BlockSpec((TILE, PAIR), lambda r, sc: (sc[0] ^ r, pair)),
                pl.BlockSpec((8, TILE), lambda r, sc: (0, sc[0] ^ r)),
                pl.BlockSpec((8, TILE), lambda r, sc: (0, sc[0] ^ r)),
                pl.BlockSpec((1, TILE, PAIR), lambda r, sc: (r, 0, pair)),
            ]
            + [pl.BlockSpec(memory_space=pl.ANY)] * len(pieces),
            out_specs=[pl.BlockSpec((TILE, PAIR), lambda r, sc: (sc[0] ^ r, 0))]
            + [whole(c) for c in counts],
            scratch_shapes=[
                pltpu.VMEM((near, 2 * PAIR), BF),
                pltpu.VMEM((near // TILE, TILE, TILE), F32),
                pltpu.VMEM((near // TILE, TILE, TILE), F32),
                pltpu.VMEM((near, 2 * PAIR), F32),
                pltpu.VMEM((2, PAIR, TILE), F32),
                pltpu.SemaphoreType.DMA((len(pieces),)),
            ],
        ),
        out_shape=[jax.ShapeDtypeStruct((rows, PAIR), BF)]
        + [
            jax.ShapeDtypeStruct((c, 2 * PAIR), F32 if k == own else BF)
            for k, c in enumerate(counts)
        ],
        compiler_params=params(),
        name="attn_bwd",
    )(sc, query, spans, stats, grads, *pieces)


def whole_spec(shape):
    return pl.BlockSpec(shape, lambda i, sc: (0,) * len(shape))


def proj_kernel(sc, c0, c1, c2, c3, w0, w1, w2, w3, x0, x1, x2, x3, vec, bt_ref, mid_ref, n2_ref):
    t = sc[0]
    fw = x0.shape[1]
    branch = vec[4:5, :] + sum(
        nn(c[...], w[...]) for c, w in ((c0, w0), (c1, w1), (c2, w2), (c3, w3))
    )
    bt_ref[...] = branch
    chunks = unxor([x[...].astype(F32) for x in (x0, x1, x2, x3)], t)
    for a in range(4):
        at = slice(a * fw, (a + 1) * fw)
        mid_ref[:, at] = chunks[a] + vec[5:6, at] * branch[:, at]
    middle = mid_ref[...]
    mean, rstd = stats_of([middle], 4 * fw)
    n2_ref[...] = ((middle - mean) * rstd * vec[2:3, :] + vec[3:4, :]).astype(BF)


def proj_call(sc, contexts, ws, xs, vec):
    rows, fw = contexts[0].shape
    width = ws[0].shape[1]
    tile = rows // 2

    def row(n):
        return pl.BlockSpec((tile, n), lambda i, sc: (i, 0))

    def mine(n):
        return pl.BlockSpec((tile, n), lambda i, sc: (sc[0] * 2 + i, 0))

    return pl.pallas_call(
        proj_kernel,
        grid_spec=pltpu.PrefetchScalarGridSpec(
            num_scalar_prefetch=1,
            grid=(2,),
            in_specs=[row(fw)] * 4
            + [whole_spec(ws[0].shape)] * 4
            + [mine(fw)] * 4
            + [whole_spec(vec.shape)],
            out_specs=[row(width)] * 3,
        ),
        out_shape=[
            jax.ShapeDtypeStruct((rows, width), F32),
            jax.ShapeDtypeStruct((rows, width), F32),
            jax.ShapeDtypeStruct((rows, width), BF),
        ],
        compiler_params=params(),
        name="proj",
    )(sc, *contexts, *ws, *xs, vec)


def mlp_kernel(n0, n1, g0, g1, fc1, fc2, bias, h_ref, gb_ref, s0, s1, d0, d1, fb_ref):
    i = pl.program_id(0)
    step = 256
    hidden_units = fc1.shape[0]

    @pl.when(i == 0)
    def _():
        fb_ref[...] = jnp.zeros(fb_ref.shape, F32)

    def work(n_ref, g_ref, s_ref, d_ref):
        normed = n_ref[...]
        grads = g_ref[...]
        for u in range(hidden_units // step):
            at = slice(u * step, (u + 1) * step)
            before = nt(normed, fc1[at, :]) + bias[:, at]
            phi = 0.5 * (1.0 + lax.erf(before * INV_SQRT2))
            h_ref[:, at] = (before * phi).astype(BF)
            slope = phi + before * (jnp.exp(-0.5 * before * before) * INV_SQRT2PI)
            grad_before = (slope * nt(grads, fc2[at, :])).astype(BF)
            gb_ref[:, at] = grad_before
            wide = grad_before.astype(F32)
            fb_ref[0:1, at] += jnp.sum(wide, axis=0, keepdims=True)
        d_ref[...] = nn(gb_ref[...], fc1[...]).astype(BF)
        s_ref[...] = nn(h_ref[...], fc2[...]).astype(BF)

    @pl.when(i == 0)
    def _():
        work(n0, g0, s0, d0)

    @pl.when(i == 1)
    def _():
        work(n1, g1, s1, d1)


def mlp_call(normed, grads, weights, bias):
    rows, width = normed[0].shape
    hidden_units = bias.shape[1]

    def full(shape):
        return pl.BlockSpec(shape, lambda i: (0,) * len(shape))

    piece = jax.ShapeDtypeStruct((rows, width), BF)
    return pl.pallas_call(
        mlp_kernel,
        grid=(2,),
        in_specs=[full((rows, width))] * 4
        + [
            pl.BlockSpec((hidden_units, width), lambda i: (0, 0)),
            pl.BlockSpec((hidden_units, width), lambda i: (1, 0)),
            full(bias.shape),
        ],
        out_specs=[pl.BlockSpec((rows, hidden_units), lambda i: (i, 0))] * 2
        + [full((rows, width))] * 4
        + [full((8, hidden_units))],
        out_shape=[jax.ShapeDtypeStruct((2 * rows, hidden_units), BF)] * 2
        + [piece] * 4
        + [jax.ShapeDtypeStruct((8, hidden_units), F32)],
        compiler_params=params(),
        name="mlp",
    )(*normed, *grads, weights, weights, bias)


def mid_kernel(
    sc, a0, a1, a2, k0, k1, k2, k3, mid, bt, w0, w1, w2, w3, vec, gm_ref, gb_ref, gc_ref, sums
):
    t = sc[0]
    fw = k0.shape[1]
    width = 4 * fw

    @pl.when(pl.program_id(0) == 0)
    def _():
        sums[...] = jnp.zeros(sums.shape, F32)

    grad_normed = a0[...].astype(F32) + a1[...].astype(F32) + a2[...].astype(F32)
    middle = mid[...]
    mean, rstd = stats_of([middle], width)
    scaled = (middle - mean) * rstd
    inner = grad_normed * vec[2:3, :]
    mean_a = jnp.sum(inner, axis=1, keepdims=True) / width
    mean_b = jnp.sum(inner * scaled, axis=1, keepdims=True) / width
    chunks = unxor([k[...].astype(F32) for k in (k0, k1, k2, k3)], t)
    back = rstd * (inner - mean_a - scaled * mean_b)
    for a in range(4):
        at = slice(a * fw, (a + 1) * fw)
        gm_ref[:, at] = chunks[a] + back[:, at]
    grad_middle = gm_ref[...]
    grad_branch = grad_middle * vec[5:6, :]
    small = grad_branch.astype(BF)
    gb_ref[...] = small
    for r, w in enumerate((w0, w1, w2, w3)):
        gc_ref[r] = nt(small, w[...]).astype(BF)

    def add(k, values):
        sums[k : k + 1, :] += jnp.sum(values, axis=0, keepdims=True)

    add(0, grad_normed * scaled)
    add(1, grad_normed)
    add(2, grad_middle * bt[...])
    add(3, grad_branch)


def mid_call(sc, parts, cots, middle, branch, ws, vec):
    rows, width = middle.shape
    fw = width // 4
    tile = rows // 2

    def row(n):
        return pl.BlockSpec((tile, n), lambda i, sc: (i, 0))

    return pl.pallas_call(
        mid_kernel,
        grid_spec=pltpu.PrefetchScalarGridSpec(
            num_scalar_prefetch=1,
            grid=(2,),
            in_specs=[row(width)] * 3
            + [row(fw)] * 4
            + [row(width)] * 2
            + [whole_spec(ws[0].shape)] * 4
            + [whole_spec(vec.shape)],
            out_specs=[
                row(width),
                row(width),
                pl.BlockSpec((4, tile, fw), lambda i, sc: (0, i, 0)),
                whole_spec((8, width)),
            ],
        ),
        out_shape=[
            jax.ShapeDtypeStruct((rows, width), F32),
            jax.ShapeDtypeStruct((rows, width), BF),
            jax.ShapeDtypeStruct((4, rows, fw), BF),
            jax.ShapeDtypeStruct((8, width), F32),
        ],
        compiler_params=params(),
        name="mid",
    )(sc, *parts, *cots, middle, branch, *ws, vec)


def gn1_kernel(sc, gq0, gq1, gk, gv, w_ref, o0, o1, o2, o3):
    width = w_ref.shape[1] // 3
    query = jnp.concatenate([gq0[...], gq1[...]], axis=1)
    total = (
        nn(query, w_ref[:, 0:width])
        + nn(gk[...], w_ref[:, width : 2 * width])
        + nn(gv[...], w_ref[:, 2 * width : 3 * width])
    ).astype(BF)
    for r, ref in enumerate((o0, o1, o2, o3)):

        @pl.when(pl.program_id(0) == r)
        def _():
            ref[...] = total


def gn1_call(sc, gq0, gq1, gk, gv, w):
    rows = gk.shape[0]
    features, wide = w.shape
    sub = rows // 4

    def row(n):
        return pl.BlockSpec((sub, n), lambda r, sc: (sc[0] ^ r, 0))

    return pl.pallas_call(
        gn1_kernel,
        grid_spec=pltpu.PrefetchScalarGridSpec(
            num_scalar_prefetch=1,
            grid=(4,),
            in_specs=[row(PAIR), row(PAIR), row(features), row(features), whole_spec(w.shape)],
            out_specs=[whole_spec((sub, wide // 3))] * 4,
        ),
        out_shape=[jax.ShapeDtypeStruct((sub, wide // 3), BF)] * 4,
        compiler_params=params(),
        name="gn1",
    )(sc, gq0, gq1, gk, gv, w)


def last_kernel(sc, a0, a1, a2, x0, x1, x2, x3, gm, vec, o0, o1, o2, o3, sums, scr):
    t = sc[0]
    fw = x0.shape[1]
    width = 4 * fw

    @pl.when(pl.program_id(0) == 0)
    def _():
        sums[...] = jnp.zeros(sums.shape, F32)

    grad_normed = a0[...].astype(F32) + a1[...].astype(F32) + a2[...].astype(F32)
    chunks = unxor([x[...].astype(F32) for x in (x0, x1, x2, x3)], t)
    value = jnp.concatenate(chunks, axis=1)
    mean, rstd = stats_of([value], width)
    scaled = (value - mean) * rstd
    inner = grad_normed * vec[0:1, :]
    mean_a = jnp.sum(inner, axis=1, keepdims=True) / width
    mean_b = jnp.sum(inner * scaled, axis=1, keepdims=True) / width
    scr[...] = (gm[...] + rstd * (inner - mean_a - scaled * mean_b)).astype(BF)
    for r, ref in enumerate((o0, o1, o2, o3)):
        ref[...] = scr[:, pl.ds(pl.multiple_of((t ^ r) * fw, fw), fw)]
    sums[0:1, :] += jnp.sum(grad_normed * scaled, axis=0, keepdims=True)
    sums[1:2, :] += jnp.sum(grad_normed, axis=0, keepdims=True)


def last_call(sc, parts, xs, grad_middle, vec):
    rows, width = grad_middle.shape
    fw = width // 4
    tile = rows // 2

    def row(n):
        return pl.BlockSpec((tile, n), lambda i, sc: (i, 0))

    def mine(n):
        return pl.BlockSpec((tile, n), lambda i, sc: (sc[0] * 2 + i, 0))

    return pl.pallas_call(
        last_kernel,
        grid_spec=pltpu.PrefetchScalarGridSpec(
            num_scalar_prefetch=1,
            grid=(2,),
            in_specs=[row(width)] * 3 + [mine(fw)] * 4 + [row(width), whole_spec(vec.shape)],
            out_specs=[row(fw)] * 4 + [whole_spec((8, width))],
            scratch_shapes=[pltpu.VMEM((tile, width), BF)],
        ),
        out_shape=[jax.ShapeDtypeStruct((rows, fw), BF)] * 4
        + [jax.ShapeDtypeStruct((8, width), F32)],
        compiler_params=params(),
        name="last",
    )(sc, *parts, *xs, grad_middle, vec)


def out_kernel(sc, a0, a1, a2, k0, k1, k2, k3, mid, vec, o0, o1, o2, o3, sums, scr):
    t = sc[0]
    fw = k0.shape[1]

    @pl.when(pl.program_id(0) == 0)
    def _():
        sums[...] = jnp.zeros(sums.shape, F32)

    total = a0[...].astype(F32) + a1[...].astype(F32) + a2[...].astype(F32) + vec[6:7, :]
    scr[...] = (mid[...] + vec[7:8, :] * total).astype(BF)
    for r, ref in enumerate((o0, o1, o2, o3)):
        ref[...] = scr[:, pl.ds(pl.multiple_of((t ^ r) * fw, fw), fw)]
    grad = jnp.concatenate(unxor([k[...].astype(F32) for k in (k0, k1, k2, k3)], t), axis=1)
    sums[0:1, :] += jnp.sum(grad * total, axis=0, keepdims=True)
    sums[1:2, :] += jnp.sum(grad * vec[7:8, :], axis=0, keepdims=True)


def out_call(sc, parts, cots, middle, vec):
    rows, width = middle.shape
    fw = width // 4
    tile = rows // 2

    def row(n):
        return pl.BlockSpec((tile, n), lambda i, sc: (i, 0))

    return pl.pallas_call(
        out_kernel,
        grid_spec=pltpu.PrefetchScalarGridSpec(
            num_scalar_prefetch=1,
            grid=(2,),
            in_specs=[row(width)] * 3 + [row(fw)] * 4 + [row(width), whole_spec(vec.shape)],
            out_specs=[row(fw)] * 4 + [whole_spec((8, width))],
            scratch_shapes=[pltpu.VMEM((tile, width), BF)],
        ),
        out_shape=[jax.ShapeDtypeStruct((rows, fw), BF)] * 4
        + [jax.ShapeDtypeStruct((8, width), F32)],
        compiler_params=params(),
        name="block_out",
    )(sc, *parts, *cots, middle, vec)


def placed(pieces, t, axis):
    return jnp.concatenate(unxor(pieces, t), axis=axis)


def reduce4(pieces):
    far = (pieces[2].astype(F32) + px(pieces[3], 1).astype(F32)).astype(BF)
    return pieces[0], px(pieces[1], 1), px(far, 2)


def spans_of(image_ids, row_count, first_row, margin, near):
    tokens = image_ids.shape[0]
    most = tokens // IMG_LEAST + 1
    place = jnp.arange(tokens, dtype=jnp.int32)
    names = jnp.arange(most, dtype=jnp.int32)[:, None]
    same = image_ids[None, :] == names
    low = jnp.min(jnp.where(same, place[None, :], tokens), axis=1)
    high = jnp.max(jnp.where(same, place[None, :] + 1, 0), axis=1)
    own = lax.dynamic_slice_in_dim(image_ids, first_row, row_count, 0)
    mine = own[None, :] == names
    start = jnp.sum(jnp.where(mine, low[:, None], 0), axis=0)
    end = jnp.sum(jnp.where(mine, high[:, None], 0), axis=0)
    valid = own >= 0
    shift = margin - first_row
    start = jnp.where(valid, start + shift, 0)
    end = jnp.where(valid, end + shift, 0)
    lo = jnp.min(jnp.where(valid, start, near).reshape(-1, TILE), axis=1)
    hi = jnp.max(end.reshape(-1, TILE), axis=1)
    lo = jnp.clip(lo // TILE, 0, near // TILE)
    hi = jnp.clip(-(-hi // TILE), 0, near // TILE)
    spans = jnp.concatenate(
        [start[None, :], end[None, :], jnp.zeros((6, row_count), jnp.int32)], axis=0
    )
    return spans, jnp.stack([lo, hi], axis=1).reshape(-1)


def per_device(
    block_input,
    cotangent,
    image_ids,
    qkv_weight,
    proj_weight,
    fc1_weight,
    fc2_weight,
    norm1_gain,
    norm1_shift,
    q_bias,
    v_bias,
    proj_bias,
    scale_attn,
    norm2_gain,
    norm2_shift,
    fc1_bias,
    fc2_bias,
    scale_mlp,
):
    row_count, fw = block_input.shape
    n_seq = lax.axis_size("seq")
    width = 4 * fw
    features = qkv_weight.shape[0]
    sub = row_count // 4
    t = lax.axis_index("tensor").astype(jnp.int32)
    s = lax.axis_index("seq").astype(jnp.int32)
    reach = (IMG - 1 + row_count - 1) // row_count
    tile_rows = min(128, row_count)

    xs = gather4(block_input)
    if n_seq == 8:
        z2, z4, z6 = ps(qkv_weight, 2), ps(qkv_weight, 4), ps(qkv_weight, 6)
        found = [None] * 8
        for bits, piece in ((0, qkv_weight), (2, z2), (4, z4), (6, z6)):
            found[bits] = piece
            found[bits ^ 1] = ps(piece, 1)
        w_qkv = jnp.zeros((8,) + qkv_weight.shape, BF)
        for bits in range(8):
            w_qkv = lax.dynamic_update_slice(w_qkv, found[bits][None], (s ^ bits, 0, 0))
    else:
        w_qkv = lax.all_gather(qkv_weight, "seq", axis=1, tiled=True)[None]
    vec_own = jnp.stack(
        [
            norm1_gain,
            norm1_shift,
            norm2_gain,
            norm2_shift,
            proj_bias,
            scale_attn,
            fc2_bias,
            scale_mlp,
        ]
    )
    vec = placed([vec_own] + [px(vec_own, r) for r in range(1, 4)], t, 1)
    others = lax.all_gather(
        jnp.concatenate([fc1_weight, fc2_weight, proj_weight], axis=0), "seq", axis=1, tiled=True
    )
    units = fc1_weight.shape[0]
    ws = gather4(others[2 * units :])

    offsets_of = []
    counts = []
    for place in range(2 * reach + 1):
        offset = reach - place
        if offset == 0:
            count = row_count
        else:
            need = IMG - 1 - (abs(offset) - 1) * row_count
            count = min(row_count, -(-need // tile_rows) * tile_rows)
        offsets_of.append(offset)
        counts.append(count)
    offsets = [sum(counts[:k]) for k in range(len(counts))]
    near = sum(counts)
    margin = offsets[reach]
    spans, edges = spans_of(image_ids, row_count, s * row_count, margin, near)
    sc = jnp.concatenate([t[None], edges])
    sc_t = t[None]

    normed1, query, kv0, kv1, w_full = qkv_call(
        sc_t, xs, w_qkv, vec, q_bias[None, :], v_bias[None, :]
    )
    nears = []
    for kv in (kv0, kv1):
        pieces = []
        for offset, count in zip(offsets_of, counts):
            if offset == 0:
                pieces.append(kv)
            elif offset > 0:
                pieces.append(passed_along(kv[row_count - count :], offset))
            else:
                pieces.append(passed_along(kv[:count], offset))
        nears.append(pieces)
    cots = swap4([rows_at(cotangent, t ^ r, sub) for r in range(4)])
    grad_second = (
        jnp.concatenate(unxor(cots, t), axis=1).astype(F32) * vec[7:8, :]
    ).astype(BF)
    grads = gather4(grad_second)
    contexts = []
    stats = []
    for pair in range(2):
        ctx, st = fwd_call(pair, sc, query, spans, nears[pair], offsets, counts)
        contexts.append(ctx)
        stats.append(st)
    context = jnp.concatenate(contexts, axis=1)
    ctx_rows = swap4([rows_at(context, t ^ r, sub) for r in range(4)])
    branch, middle, normed2 = proj_call(sc_t, ctx_rows, ws, xs, vec)
    n_near = px(normed2, 1)
    n_across = px(normed2, 2)
    n_far = px(n_across, 1)
    bias1 = fc1_bias[None, :]
    hid_b, gb_b, s2, s3, d2, d3, fb_b = mlp_call((n_across, n_far), grads[2:], others, bias1)
    hid_a, gb_a, s0, s1, d0, d1, fb_a = mlp_call((normed2, n_near), grads[:2], others, bias1)
    parts = reduce4([d0, d1, d2, d3])
    grad_middle, grad_branch, grad_ctx, sums_mid = mid_call(
        sc_t, parts, cots, middle, branch, ws, vec
    )
    swapped = swap4([grad_ctx[r] for r in range(4)])
    grad_rows = jnp.stack(swapped)

    rows_a = jnp.concatenate([normed2, n_near], axis=0)
    rows_b = jnp.concatenate([n_across, n_far], axis=0)
    gs_a = jnp.concatenate(grads[:2], axis=0)
    gs_b = jnp.concatenate(grads[2:], axis=0)
    fc1_part = (tn(gb_a, rows_a) + tn(gb_b, rows_b)).astype(BF)
    fc2_part = (tn(hid_a, gs_a) + tn(hid_b, gs_b)).astype(BF)
    fc_out = lax.psum_scatter(
        jnp.concatenate([fc1_part, fc2_part], axis=0), "seq", scatter_dimension=1, tiled=True
    ).astype(F32)
    o0, o1, o2, o3, sums_out = out_call(sc_t, reduce4([s0, s1, s2, s3]), cots, middle, vec)
    block_output = placed(swap4([o0, o1, o2, o3]), t, 0)
    branch_rows = placed(gather4(grad_branch), t, 0)
    proj_part = tn(context, branch_rows).astype(BF)
    proj_out = lax.psum_scatter(proj_part, "seq", scatter_dimension=1, tiled=True).astype(F32)

    grad_q = []
    grad_k = []
    grad_v = []
    for pair in range(2):
        got = bwd_call(
            pair, sc, query, spans, stats[pair], grad_rows, nears[pair], offsets, counts, reach
        )
        grad_q.append(got[0])
        total = got[1 + reach]
        for k, (offset, count) in enumerate(zip(offsets_of, counts)):
            if offset == 0:
                continue
            back = passed_along(got[1 + k], -offset).astype(F32)
            if count < row_count:
                gap = row_count - count
                ends = ((gap, 0), (0, 0)) if offset > 0 else ((0, gap), (0, 0))
                back = jnp.pad(back, ends)
            total = total + back
        total = total.astype(BF)
        grad_k.append(total[:, :PAIR])
        grad_v.append(total[:, PAIR:])
    gk = jnp.concatenate(grad_k, axis=1)
    gv = jnp.concatenate(grad_v, axis=1)
    gq = jnp.concatenate(grad_q, axis=1)
    pieces = gn1_call(sc_t, grad_q[0], grad_q[1], gk, gv, w_full)
    i0, i1, i2, i3, sums_last = last_call(sc_t, reduce4(pieces), xs, grad_middle, vec)
    input_grad = placed(swap4([i0, i1, i2, i3]), t, 0)
    qkv_parts = [tn(g, normed1) for g in (gq, gk, gv)]
    if n_seq == 8:
        unit = 128
        blocks = jnp.concatenate(
            [
                g.astype(BF).reshape(features, width // unit, unit).transpose(1, 0, 2)
                for g in qkv_parts
            ],
            axis=0,
        ).reshape(2, 2, 2, 3, features, unit)
        for axis, bits in ((1, 2), (1, 1), (0, 4)):
            if bits == 2:
                mine = (s >> 1) & 1
            elif bits == 1:
                mine = s & 1
            else:
                mine = (s >> 2) & 1
            keep = lax.dynamic_index_in_dim(blocks, mine, axis, keepdims=False)
            send = lax.dynamic_index_in_dim(blocks, 1 - mine, axis, keepdims=False)
            blocks = (keep.astype(F32) + ps(send.astype(BF), bits).astype(F32))
        qkv_out = blocks.transpose(1, 0, 2).reshape(features, 3 * unit)
    else:
        qkv_out = lax.psum_scatter(
            jnp.stack(qkv_parts, axis=1).reshape(features, 3 * width).astype(BF),
            "seq",
            scatter_dimension=1,
            tiled=True,
        ).astype(F32)

    rows8 = jnp.concatenate([sums_last[0:2], sums_mid[0:4], sums_out[0:2]], axis=0)
    cut = [lax.dynamic_slice_in_dim(rows8, (t ^ r) * fw, fw, 1) for r in range(4)]
    got = swap4(cut)
    own8 = got[0] + got[1] + got[2] + got[3]
    flat = jnp.concatenate(
        [
            own8.reshape(-1),
            jnp.sum(gq.astype(F32), axis=0),
            jnp.sum(gv.astype(F32), axis=0),
            fb_a[0] + fb_b[0],
        ]
    ).reshape(-1, 128)
    if n_seq == 8:
        for bits in (2, 1, 4):
            flat = flat + ps(flat, bits)
    else:
        flat = lax.psum(flat, "seq")
    flat = flat.reshape(-1)
    own8 = flat[: 8 * fw].reshape(8, fw)
    q_bias_grad = flat[8 * fw : 8 * fw + features]
    v_bias_grad = flat[8 * fw + features : 8 * fw + 2 * features]
    fc1_bias_grad = flat[8 * fw + 2 * features :]
    return (
        block_output,
        input_grad,
        qkv_out,
        proj_out,
        fc_out[:units],
        fc_out[units:],
        own8[0],
        own8[1],
        q_bias_grad,
        v_bias_grad,
        own8[5],
        own8[4],
        own8[2],
        own8[3],
        fc1_bias_grad,
        own8[7],
        own8[6],
    )


def solution(mesh):
    cut = P("tensor", "seq")
    by_tensor = P("tensor")
    in_specs = (P("seq", "tensor"), P("seq", "tensor"), P()) + (cut,) * 4 + (by_tensor,) * 11
    out_specs = (P("seq", "tensor"), P("seq", "tensor")) + (cut,) * 4 + (by_tensor,) * 11
    return jax.shard_map(
        per_device, mesh=mesh, in_specs=in_specs, out_specs=out_specs, check_vma=False
    )
```

time: 1280 us -> 561 us (0.44)
  waiting for transfers between devices: 710 us -> 203 us
  matrix products: 218 us -> 14.6 us
  Pallas kernels: 0 us -> 161 us
  other arithmetic: 166 us -> 16 us
  blocking collectives: 115 us -> 0 us
  starting transfers between devices: 26.2 us -> 105 us
  local copies, waits for them, and re-layouts: 22.7 us -> 35.6 us
    reduce_scatter x8 -> x0, waiting for transfers between devices: 410 us -> none  [the longest x4 156 us: narrow(): return lax.psum_scatter(term, 'tensor', scatter_dimension=1, tiled=True)]
    dot_general x42 -> x8, matrix products: 218 us -> 14.6 us  [tn(): lax.dot_general(left, right, (((0,), (0,)), ((), ())), preferred_element_...]
    all_gather x7 -> x1, waiting for transfers between devices: 216 us -> 52.1 us  [per_device(): lax.all_gather(jnp.concatenate([fc1_weight, fc2_weight, proj_weight], axi...]
    pallas_call x0 -> x12, Pallas kernels: none -> 161 us  [the longest x2 58.9 us: bwd_call(): pl.pallas_call(functools.partial(bwd_kernel, offsets, counts, own), grid_...]
    ppermute x8 -> x74, starting transfers between devices: 25.4 us -> 105 us  [the longest x16 61.2 us: passed_along(): return lax.ppermute(block, 'seq', route)]
    ppermute x8 -> x74, waiting for transfers between devices: 83.2 us -> 151 us  [the longest x45 79.1 us: px(): return lax.ppermute(value, 'tensor', pairs)]
    psum x5 -> x0, blocking collectives: 66.1 us -> none  [the longest x1 39.2 us: per_device(): lax.psum((norm1_gain_grad, norm1_shift_grad, q_bias_grad, v_bias_grad, pr...]
    convert_element_type x8 -> x7, other arithmetic: 63.4 us -> 1.86 us  [the longest x1 0.67 us: per_device(): lax.psum_scatter(proj_part, 'seq', scatter_dimension=1, tiled=True)]
  transfers between devices with their start and end apart: 23 -> 77, of which waited for: 20 -> 27; matrix products, arithmetic and copies ran while one was open for 6% -> 9% of each run, Pallas kernels for 0% -> 28%
where the time goes in v1:
time: 561 us; the launch traced here: 551 us
  waiting for transfers between devices  203 us (36%)
  Pallas kernels  161 us (29%)
  starting transfers between devices  105 us (19%)
  local copies, waits for them, and re-layouts  35.6 us (6%)
  other arithmetic  16 us (3%)
  between operations  15.6 us (3%)
  matrix products  14.6 us (3%)
    ppermute x45, waiting for transfers between devices, px(): return lax.ppermute(value, 'tensor', pairs)  79.1 us
    ppermute x16, starting transfers between devices, passed_along(): return lax.ppermute(block, 'seq', route)  61.2 us
    pallas_call x2, Pallas kernels, bwd_call(): pl.pallas_call(functools.partial(bwd_kernel, offsets, counts, own), grid_...  58.9 us
    ppermute x13, waiting for transfers between devices, ps(): return lax.ppermute(value, 'seq', pairs)  54.9 us
    all_gather x1, waiting for transfers between devices, per_device(): lax.all_gather(jnp.concatenate([fc1_weight, fc2_weight, proj_weight], axi...  52.1 us
    pallas_call x2, Pallas kernels, fwd_call(): pl.pallas_call(functools.partial(fwd_kernel, offsets, counts), grid_spec=...  51.7 us
    ppermute x45, starting transfers between devices, px(): return lax.ppermute(value, 'tensor', pairs)  27.7 us
    unnamed x168, local copies, waits for them, and re-layouts  23 us
  transfers between devices with their start and end apart: 77, of which 27 were waited for; matrix products, arithmetic and copies ran while one was open for 9% of the time, Pallas kernels for 28%

profile of v1, /device:TPU:0, one launch (start us, length us, event | category | flops | bytes accessed | tf_op | source)
XLA Modules:
  0.0 551.3 jit_solution(15710567867344962527)
XLA Ops:
  27.1 21.6 %collective-permute-done.6 = bf16[256,384]{1,0:T(8,128)(2,1)S(1)} collective-permute-done((bf16[256,384]{1,0:T(8,128)(2,1)S(1)}, bf16[256,384]{1,0:T(8,128)(2,1)S(1)}, u32[]{:S(2)}, u32[]{:S(2)}) %collective-permute-start.6) | collective-permute-done | bytes 196640 | tf_op jit(solution)/shard_map/ppermute | solution.py:31
  51.3 5.7 %collective-permute-done.7 = bf16[256,384]{1,0:T(8,128)(2,1)S(1)} collective-permute-done((bf16[256,384]{1,0:T(8,128)(2,1)S(1)}, bf16[256,384]{1,0:T(8,128)(2,1)S(1)}, u32[]{:S(2)}, u32[]{:S(2)}) %collective-permute-start.7) | collective-permute-done | bytes 196640 | tf_op jit(solution)/shard_map/ppermute | solution.py:31
  57.7 5.6 %collective-permute-done.9 = bf16[256,384]{1,0:T(8,128)(2,1)S(1)} collective-permute-done((bf16[256,384]{1,0:T(8,128)(2,1)S(1)}, bf16[256,384]{1,0:T(8,128)(2,1)S(1)}, u32[]{:S(2)}, u32[]{:S(2)}) %collective-permute-start.9) | collective-permute-done | bytes 196640 | tf_op jit(solution)/shard_map/ppermute | solution.py:31
  64.9 7.2 %qkv.1 = (bf16[1024,1024]{1,0:T(8,128)(2,1)}, bf16[1024,256]{1,0:T(8,128)(2,1)}, bf16[1024,256]{1,0:T(8,128)(2,1)}, bf16[1024,256]{1,0:T(8,128)(2,1)}, bf16[256,3072]{1,0:T(8,128)(2,1)}) custom-call(s32[1]{0:T(128)} %bitcast.sc, bf16[1024,256]{1,0:T(8,128)(2,1)} %x0.5, bf16[1024,256]{1,0:T(8,128)(2,1)} %copy-done.5, bf16[1024,256]{1,0:T(8,128)(2,1)} %copy-done.4, ...), custom_call_target="tpu_custom_call" | custom-call | tf_op jit(solution)/shard_map/qkv/pallas_call | solution.py:130
  77.3 52.1 %all-gather.2.cloned.1.call-done.fc1.fc2 = bf16[2304,1024]{1,0:T(8,128)(2,1)} async-done(((bf16[2304,128]{1,0:T(8,128)(2,1)}), bf16[2304,1024]{1,0:T(8,128)(2,1)}) %all-gather.2.cloned.1.call-update) | async-done | bytes 4718608 | tf_op jit(solution)/shard_map/all_gather | solution.py:776
  135.9 4.2 collective-permute-start.18
  143.5 5.2 collective-permute-start.17
  150.7 25.9 %attn_fwd.2 = (bf16[1024,128]{1,0:T(8,128)(2,1)}, f32[8,1024]{1,0:T(8,128)}) custom-call(s32[9]{0:T(128)} %pad_add_fusion.1.sc, bf16[1024,256]{1,0:T(8,128)(2,1)} %get-tuple-element.73.q_ref, s32[8,1024]{1,0:T(8,128)} %add_add_fusion.se_ref, bf16[384,256]{1,0:T(8,128)(2,1)} %copy-done.45, bf16[1024,256]{1,0:T(8,128)(2,1)} %copy-done.16, ...), custom_call_target="tpu_custom_call" | custom-call | tf_op jit(solution)/shard_map/attn_fwd/pallas_call | solution.py:237
  179.9 25.9 %attn_fwd.3 = (bf16[1024,128]{1,0:T(8,128)(2,1)}, f32[8,1024]{1,0:T(8,128)}) custom-call(s32[9]{0:T(128)} %pad_add_fusion.1.sc, bf16[1024,256]{1,0:T(8,128)(2,1)} %get-tuple-element.73.q_ref, s32[8,1024]{1,0:T(8,128)} %add_add_fusion.se_ref, bf16[384,256]{1,0:T(8,128)(2,1)} %copy-done.43, bf16[1024,256]{1,0:T(8,128)(2,1)} %copy-done.14, ...), custom_call_target="tpu_custom_call" | custom-call | tf_op jit(solution)/shard_map/attn_fwd/pallas_call | solution.py:237
  216.7 4.3 proj.1
  222.1 5.9 %collective-permute-done.35.g0 = bf16[256,1024]{1,0:T(8,128)(2,1)S(1)} collective-permute-done((bf16[256,1024]{1,0:T(8,128)(2,1)S(1)}, bf16[256,1024]{1,0:T(8,128)(2,1)S(1)}, u32[]{:S(2)}, u32[]{:S(2)}) %collective-permute-start.35) | collective-permute-done | bytes 524320 | tf_op jit(solution)/shard_map/ppermute | solution.py:26
  228.1 10.6 %collective-permute-done.33.n0 = bf16[256,1024]{1,0:T(8,128)(2,1)S(1)} collective-permute-done((bf16[256,1024]{1,0:T(8,128)(2,1)}, bf16[256,1024]{1,0:T(8,128)(2,1)S(1)}, u32[]{:S(2)}, u32[]{:S(2)}) %collective-permute-start.33) | collective-permute-done | bytes 524320 | tf_op jit(solution)/shard_map/ppermute | solution.py:26
  241.4 10.1 %mlp.3 = (bf16[512,1024]{1,0:T(8,128)(2,1)}, bf16[512,1024]{1,0:T(8,128)(2,1)}, bf16[256,1024]{1,0:T(8,128)(2,1)}, bf16[256,1024]{1,0:T(8,128)(2,1)}, bf16[256,1...) custom-call(bf16[256,1024]{1,0:T(8,128)(2,1)} %copy-done.24, bf16[256,1024]{1,0:T(8,128)(2,1)} %copy-done.28, ...), custom_call_target="tpu_custom_call" | custom-call | tf_op jit(solution)/shard_map/mlp/pallas_call | solution.py:462
  253.3 10.3 %mlp.2 = (bf16[512,1024]{1,0:T(8,128)(2,1)}, bf16[512,1024]{1,0:T(8,128)(2,1)}, bf16[256,1024]{1,0:T(8,128)(2,1)}, bf16[256,1024]{1,0:T(8,128)(2,1)}, bf16[256,1...) custom-call(bf16[256,1024]{1,0:T(8,128)(2,1)} %get-tuple-element.78.n0, ...), custom_call_target="tpu_custom_call" | custom-call | tf_op jit(solution)/shard_map/mlp/pallas_call | solution.py:462
  265.8 12.5 %collective-permute-done.44.a2 = bf16[256,1024]{1,0:T(8,128)(2,1)S(1)} collective-permute-done((bf16[256,1024]{1,0:T(8,128)(2,1)S(1)}, bf16[256,1024]{1,0:T(8,128)(2,1)S(1)}, u32[]{:S(2)}, u32[]{:S(2)}) %collective-permute-start.44) | collective-permute-done | bytes 524320 | tf_op jit(solution)/shard_map/ppermute | solution.py:26
  279.1 5.9 %mid.1 = (f32[256,1024]{1,0:T(8,128)}, bf16[256,1024]{1,0:T(8,128)(2,1)}, bf16[4,256,256]{2,1,0:T(8,128)(2,1)}, f32[8,1024]{1,0:T(8,128)}) custom-call(s32[1]{0:T(128)} %bitcast.sc, bf16[256,1024]{1,0:T(8,128)(2,1)} %get-tuple-element.89.a0, bf16[256,1024]{1,0:T(8,128)(2,1)} %copy-done.53, bf16[256,1024]{1,0:T(8,128)(2,1)} %copy-done.54, ...), custom_call_target="tpu_custom_call" | custom-call | tf_op jit(solution)/shard_map/mid/pallas_call | solution.py:529
  286.3 12.0 %collective-permute-done.65 = bf16[256,1024]{1,0:T(8,128)(2,1)S(1)} collective-permute-done((bf16[256,1024]{1,0:T(8,128)(2,1)}, bf16[256,1024]{1,0:T(8,128)(2,1)S(1)}, u32[]{:S(2)}, u32[]{:S(2)}) %collective-permute-start.65) | collective-permute-done | bytes 524320 | tf_op jit(solution)/shard_map/ppermute | solution.py:26
  315.4 6.5 %copy.58 = bf16[2048,1024]{0,1:T(8,128)(2,1)} copy(bf16[2048,1024]{1,0:T(8,128)(2,1)} %pad_maximum_fusion) | data formatting | bytes 8388608
  328.4 14.4 %collective-permute-done.46 = bf16[256,256]{1,0:T(8,128)(2,1)S(1)} collective-permute-done((bf16[256,256]{1,0:T(8,128)(2,1)S(1)}, bf16[256,256]{1,0:T(8,128)(2,1)S(1)}, u32[]{:S(2)}, u32[]{:S(2)}) %collective-permute-start.46) | collective-permute-done | bytes 131104 | tf_op jit(solution)/shard_map/ppermute | solution.py:26
  345.3 29.4 %attn_bwd.2 = (bf16[1024,128]{1,0:T(8,128)(2,1)}, bf16[384,256]{1,0:T(8,128)(2,1)}, bf16[1024,256]{1,0:T(8,128)(2,1)}, f32[1024,256]{1,0:T(8,128)}, bf16[1024,256]{1,0:T(8,128)(2,1)}, /*index=5*/bf16[384,256]{1,0:T(8,128)(2,1)}) custom-call(s32[9]{0:T(128)} %pad_add_fusion.1.sc, bf16[1024,256]{1,0:T(8,128)(2,1)} %get-tuple-element.73.q_ref, ...), custom_call_target="tpu_custom_call" | custom-call | tf_op jit(solution)/shard_map/attn_bwd/pallas_call | solution.py:335
  376.1 17.6 %collective-permute-start.50 = (bf16[1024,256]{1,0:T(8,128)(2,1)}, bf16[1024,256]{1,0:T(8,128)(2,1)S(1)}, u32[]{:S(2)}, u32[]{:S(2)}) collective-permute-start(bf16[1024,256]{1,0:T(8,128)(2,1)} %get-tuple-element.101), channel_id=1, source_target_pairs={{0,4},{4,8},{8,12},{12,16},{16,20},{20,24},{24,28},{1,5},{5,9},{9,... | collective-permute-start | bytes 1572872 | tf_op jit(solution)/shard_map/ppermute | solution.py:37
  402.3 4.6 collective-permute-start.51
  406.9 29.5 %attn_bwd.3 = (bf16[1024,128]{1,0:T(8,128)(2,1)}, bf16[384,256]{1,0:T(8,128)(2,1)}, bf16[1024,256]{1,0:T(8,128)(2,1)}, f32[1024,256]{1,0:T(8,128)}, bf16[1024,256]{1,0:T(8,128)(2,1)}, /*index=5*/bf16[384,256]{1,0:T(8,128)(2,1)}) custom-call(s32[9]{0:T(128)} %pad_add_fusion.1.sc, bf16[1024,256]{1,0:T(8,128)(2,1)} %get-tuple-element.73.q_ref, ...), custom_call_target="tpu_custom_call" | custom-call | tf_op jit(solution)/shard_map/attn_bwd/pallas_call | solution.py:335
  440.2 9.8 %collective-permute-start.54 = (bf16[1024,256]{1,0:T(8,128)(2,1)S(1)}, bf16[1024,256]{1,0:T(8,128)(2,1)S(1)}, u32[]{:S(2)}, u32[]{:S(2)}) collective-permute-start(bf16[1024,256]{1,0:T(8,128)(2,1)S(1)} %copy-done.68), channel_id=1, source_target_pairs={{0,4},{4,8},{8,12},{12,16},{16,20},{20,24},{24,28},{1,5},{5,9},{9,... | collective-permute-start | bytes 1572872 | tf_op jit(solution)/shard_map/ppermute | solution.py:37
  451.4 4.8 collective-permute-start.55
  456.5 9.1 %collective-permute-done.52 = bf16[384,256]{1,0:T(8,128)(2,1)S(1)} collective-permute-done((bf16[384,256]{1,0:T(8,128)(2,1)S(1)}, bf16[384,256]{1,0:T(8,128)(2,1)S(1)}, u32[]{:S(2)}, u32[]{:S(2)}) %collective-permute-start.52) | collective-permute-done | bytes 196640 | tf_op jit(solution)/shard_map/ppermute | solution.py:37
  466.1 5.5 collective-permute-done.54
  473.6 6.1 %gn1.1 = (bf16[256,1024]{1,0:T(8,128)(2,1)}, bf16[256,1024]{1,0:T(8,128)(2,1)}, bf16[256,1024]{1,0:T(8,128)(2,1)}, bf16[256,1024]{1,0:T(8,128)(2,1)}) custom-call(s32[1]{0:T(128)} %bitcast.sc, bf16[1024,128]{1,0:T(8,128)(2,1)} %get-tuple-element.95.gq0, bf16[1024,128]{1,0:T(8,128)(2,1)} %get-tuple-element.97.gq1, bf16[1024,256]{1,0:T(8,128)(2,1)} %pad_maximum_fusion.5.gk, ...), custom_call_target="tpu_custom_call" | custom-call | tf_op jit(solution)/shard_map/gn1/pallas_call | solution.py:580
  484.6 11.6 %collective-permute-done.58.a2 = bf16[256,1024]{1,0:T(8,128)(2,1)S(1)} collective-permute-done((bf16[256,1024]{1,0:T(8,128)(2,1)S(1)}, bf16[256,1024]{1,0:T(8,128)(2,1)S(1)}, u32[]{:S(2)}, u32[]{:S(2)}) %collective-permute-start.58) | collective-permute-done | bytes 524320 | tf_op jit(solution)/shard_map/ppermute | solution.py:26
  506.6 7.2 %collective-permute-done.71 = f32[28,128]{1,0:T(8,128)S(1)} collective-permute-done((f32[28,128]{1,0:T(8,128)S(1)}, f32[28,128]{1,0:T(8,128)S(1)}, u32[]{:S(2)}, u32[]{:S(2)}) %collective-permute-start.71) | collective-permute-done | bytes 14368 | tf_op jit(solution)/shard_map/ppermute | solution.py:31
  524.8 4.9 collective-permute-done.63
  531.6 7.8 %collective-permute-done.64 = bf16[3,256,128]{2,1,0:T(8,128)(2,1)S(1)} collective-permute-done((bf16[3,256,128]{2,1,0:T(8,128)(2,1)S(1)}, bf16[3,256,128]{2,1,0:T(8,128)(2,1)S(1)}, u32[]{:S(2)}, u32[]{:S(2)}) %collective-permute-start.64) | collective-permute-done | bytes 196640 | tf_op jit(solution)/shard_map/ppermute | solution.py:31
  (400 shorter events, 142.1 us)
Async XLA Ops:
  7.2 122.1 %all-gather.2.cloned.1.call-start = ((), (), s32[]{:S(2)}) async-start(), calls=%async_computation.2 | async-start | bytes 5308416 | tf_op jit(solution)/shard_map/all_gather | solution.py:776
  9.3 531.2 %reduce-scatter.7.cloned.1.call-start = ((), (), s32[]{:S(2)}) async-start(), calls=%async_computation.3 | async-start | bytes 589824
  22.0 26.7 %collective-permute-start.6 = (bf16[256,384]{1,0:T(8,128)(2,1)S(1)}, bf16[256,384]{1,0:T(8,128)(2,1)S(1)}, u32[]{:S(2)}, u32[]{:S(2)}) collective-permute-start(bf16[256,384]{1,0:T(8,128)(2,1)S(1)} %copy-done.59), channel_id=1, source_target_pairs={{0,16},{4,20},{8,24},{12,28},{16,0},{20,4},{24,8},{28,12},{1,17},{... | collective-permute-start | bytes 589832 | tf_op jit(solution)/shard_map/ppermute | solution.py:31
  24.6 25.8 %collective-permute-start.8 = (bf16[256,384]{1,0:T(8,128)(2,1)S(1)}, bf16[256,384]{1,0:T(8,128)(2,1)S(1)}, u32[]{:S(2)}, u32[]{:S(2)}) collective-permute-start(bf16[256,384]{1,0:T(8,128)(2,1)S(1)} %copy-done.59), channel_id=1, source_target_pairs={{0,24},{4,28},{8,16},{12,20},{16,8},{20,12},{24,0},{28,4},{1,25},{... | collective-permute-start | bytes 589832 | tf_op jit(solution)/shard_map/ppermute | solution.py:31
  24.8 32.8 %collective-permute-start.1 = (bf16[1024,256]{1,0:T(8,128)(2,1)S(1)}, bf16[1024,256]{1,0:T(8,128)(2,1)S(1)}, u32[]{:S(2)}, u32[]{:S(2)}) collective-permute-start(bf16[1024,256]{1,0:T(8,128)(2,1)S(1)} %copy-done.3), channel_id=1, source_target_pairs={{0,2},{1,3},{2,0},{3,1},{4,6},{5,7},{6,4},{7,5},{8,10},{9,11},{10,... | collective-permute-start | bytes 1572872 | tf_op jit(solution)/shard_map/ppermute | solution.py:26
  26.4 37.1 %collective-permute-start = (bf16[1024,256]{1,0:T(8,128)(2,1)S(1)}, bf16[1024,256]{1,0:T(8,128)(2,1)S(1)}, u32[]{:S(2)}, u32[]{:S(2)}) collective-permute-start(bf16[1024,256]{1,0:T(8,128)(2,1)S(1)} %copy-done.3), channel_id=1, source_target_pairs={{0,1},{1,0},{2,3},{3,2},{4,5},{5,4},{6,7},{7,6},{8,9},{9,8},{10,11... | collective-permute-start | bytes 1572872 | tf_op jit(solution)/shard_map/ppermute | solution.py:26
  26.5 23.4 %collective-permute-start.5 = (bf16[256,384]{1,0:T(8,128)(2,1)S(1)}, bf16[256,384]{1,0:T(8,128)(2,1)S(1)}, u32[]{:S(2)}, u32[]{:S(2)}) collective-permute-start(bf16[256,384]{1,0:T(8,128)(2,1)S(1)} %collective-permute-done.4), channel_id=1, source_target_pairs={{0,4},{4,0},{8,12},{12,8},{16,20},{20,16},{24,28},{28,24},{1,5},{5... | collective-permute-start | bytes 589832 | tf_op jit(solution)/shard_map/ppermute | solution.py:31
  48.8 81.7 %collective-permute-start.28 = (bf16[256,256]{1,0:T(8,128)(2,1)}, bf16[256,256]{1,0:T(8,128)(2,1)S(1)}, u32[]{:S(2)}, u32[]{:S(2)}) collective-permute-start(bf16[256,256]{1,0:T(8,128)(2,1)} %get-tuple-element.216), channel_id=1, source_target_pairs={{0,3},{1,2},{2,1},{3,0},{4,7},{5,6},{6,5},{7,4},{8,11},{9,10},{10,... | collective-permute-start | bytes 393224 | tf_op jit(solution)/shard_map/ppermute | solution.py:26
  50.4 81.3 %collective-permute-start.29 = (bf16[256,256]{1,0:T(8,128)(2,1)}, bf16[256,256]{1,0:T(8,128)(2,1)S(1)}, u32[]{:S(2)}, u32[]{:S(2)}) collective-permute-start(bf16[256,256]{1,0:T(8,128)(2,1)} %get-tuple-element.215), channel_id=1, source_target_pairs={{0,2},{1,3},{2,0},{3,1},{4,6},{5,7},{6,4},{7,5},{8,10},{9,11},{10,... | collective-permute-start | bytes 393224 | tf_op jit(solution)/shard_map/ppermute | solution.py:26
  63.4 69.7 %collective-permute-start.30 = (bf16[256,256]{1,0:T(8,128)(2,1)S(1)}, bf16[256,256]{1,0:T(8,128)(2,1)S(1)}, u32[]{:S(2)}, u32[]{:S(2)}) collective-permute-start(bf16[256,256]{1,0:T(8,128)(2,1)S(1)} %get-tuple-element.214), channel_id=1, source_target_pairs={{0,1},{1,0},{2,3},{3,2},{4,5},{5,4},{6,7},{7,6},{8,9},{9,8},{10,11... | collective-permute-start | bytes 393224 | tf_op jit(solution)/shard_map/ppermute | solution.py:26
  72.1 71.4 %collective-permute-start.14 = (bf16[1024,256]{1,0:T(8,128)(2,1)}, bf16[1024,256]{1,0:T(8,128)(2,1)S(1)}, u32[]{:S(2)}, u32[]{:S(2)}) collective-permute-start(bf16[1024,256]{1,0:T(8,128)(2,1)} %get-tuple-element.74.refs_2_), channel_id=1, source_target_pairs={{0,4},{4,8},{8,12},{12,16},{16,20},{20,24},{24,28},{1,5},{5,9},{9,... | collective-permute-start | bytes 1572872 | tf_op jit(solution)/shard_map/ppermute | solution.py:37
  74.9 73.8 %collective-permute-start.15 = (bf16[1024,256]{1,0:T(8,128)(2,1)}, bf16[1024,256]{1,0:T(8,128)(2,1)S(1)}, u32[]{:S(2)}, u32[]{:S(2)}) collective-permute-start(bf16[1024,256]{1,0:T(8,128)(2,1)} %get-tuple-element.74.refs_2_), channel_id=1, source_target_pairs={{4,0},{8,4},{12,8},{16,12},{20,16},{24,20},{28,24},{5,1},{9,5},{13... | collective-permute-start | bytes 1572872 | tf_op jit(solution)/shard_map/ppermute | solution.py:37
  133.1 43.6 %collective-permute-start.25 = (bf16[256,1024]{1,0:T(8,128)(2,1)S(1)}, bf16[256,1024]{1,0:T(8,128)(2,1)S(1)}, u32[]{:S(2)}, u32[]{:S(2)}) collective-permute-start(bf16[256,1024]{1,0:T(8,128)(2,1)S(1)} %slice.158.w0), channel_id=1, source_target_pairs={{0,2},{1,3},{2,0},{3,1},{4,6},{5,7},{6,4},{7,5},{8,10},{9,11},{10,... | collective-permute-start | bytes 1572872 | tf_op jit(solution)/shard_map/ppermute | solution.py:26
  135.9 42.4 %collective-permute-start.18 = (bf16[1024,256]{1,0:T(8,128)(2,1)S(1)}, bf16[1024,256]{1,0:T(8,128)(2,1)S(1)}, u32[]{:S(2)}, u32[]{:S(2)}) collective-permute-start(bf16[1024,256]{1,0:T(8,128)(2,1)S(1)} %copy-done.10), channel_id=1, source_target_pairs={{0,4},{4,8},{8,12},{12,16},{16,20},{20,24},{24,28},{1,5},{5,9},{9,... | collective-permute-start | bytes 1572872 | tf_op jit(solution)/shard_map/ppermute | solution.py:37
  142.2 36.1 %collective-permute-start.19 = (bf16[1024,256]{1,0:T(8,128)(2,1)S(1)}, bf16[1024,256]{1,0:T(8,128)(2,1)S(1)}, u32[]{:S(2)}, u32[]{:S(2)}) collective-permute-start(bf16[1024,256]{1,0:T(8,128)(2,1)S(1)} %copy-done.10), channel_id=1, source_target_pairs={{4,0},{8,4},{12,8},{16,12},{20,16},{24,20},{28,24},{5,1},{9,5},{13... | collective-permute-start | bytes 1572872 | tf_op jit(solution)/shard_map/ppermute | solution.py:37
  143.5 33.1 %collective-permute-start.17 = (bf16[384,256]{1,0:T(8,128)(2,1)S(1)}, bf16[384,256]{1,0:T(8,128)(2,1)S(1)}, u32[]{:S(2)}, u32[]{:S(2)}) collective-permute-start(bf16[384,256]{1,0:T(8,128)(2,1)S(1)} %get-tuple-element.222), channel_id=1, source_target_pairs={{0,8},{4,12},{8,16},{12,20},{16,24},{20,28},{1,9},{5,13},{9,17},{1... | collective-permute-start | bytes 589832 | tf_op jit(solution)/shard_map/ppermute | solution.py:37
  148.7 29.4 %collective-permute-start.20 = (bf16[384,256]{1,0:T(8,128)(2,1)S(1)}, bf16[384,256]{1,0:T(8,128)(2,1)S(1)}, u32[]{:S(2)}, u32[]{:S(2)}) collective-permute-start(bf16[384,256]{1,0:T(8,128)(2,1)S(1)} %get-tuple-element.221), channel_id=1, source_target_pairs={{8,0},{12,4},{16,8},{20,12},{24,16},{28,20},{9,1},{13,5},{17,9},{2... | collective-permute-start | bytes 589832 | tf_op jit(solution)/shard_map/ppermute | solution.py:37
  176.6 39.0 %collective-permute-start.24 = (bf16[256,1024]{1,0:T(8,128)(2,1)S(1)}, bf16[256,1024]{1,0:T(8,128)(2,1)S(1)}, u32[]{:S(2)}, u32[]{:S(2)}) collective-permute-start(bf16[256,1024]{1,0:T(8,128)(2,1)S(1)} %slice.158.w0), channel_id=1, source_target_pairs={{0,1},{1,0},{2,3},{3,2},{4,5},{5,4},{6,7},{7,6},{8,9},{9,8},{10,11... | collective-permute-start | bytes 1572872 | tf_op jit(solution)/shard_map/ppermute | solution.py:26
  176.7 38.9 %collective-permute-start.26 = (bf16[256,1024]{1,0:T(8,128)(2,1)S(1)}, bf16[256,1024]{1,0:T(8,128)(2,1)S(1)}, u32[]{:S(2)}, u32[]{:S(2)}) collective-permute-start(bf16[256,1024]{1,0:T(8,128)(2,1)S(1)} %collective-permute-done.25.w2), channel_id=1, source_target_pairs={{0,1},{1,0},{2,3},{3,2},{4,5},{5,4},{6,7},{7,6},{8,9},{9,8},{10,11... | collective-permute-start | bytes 1572872 | tf_op jit(solution)/shard_map/ppermute | solution.py:26
  209.5 18.6 %collective-permute-start.35 = (bf16[256,1024]{1,0:T(8,128)(2,1)S(1)}, bf16[256,1024]{1,0:T(8,128)(2,1)S(1)}, u32[]{:S(2)}, u32[]{:S(2)}) collective-permute-start(bf16[256,1024]{1,0:T(8,128)(2,1)S(1)} %multiply_convert_fusion.g0), channel_id=1, source_target_pairs={{0,2},{1,3},{2,0},{3,1},{4,6},{5,7},{6,4},{7,5},{8,10},{9,11},{10,... | collective-permute-start | bytes 1572872 | tf_op jit(solution)/shard_map/ppermute | solution.py:26
  286.3 18.8 %collective-permute-start.67 = (bf16[256,1024]{1,0:T(8,128)(2,1)}, bf16[256,1024]{1,0:T(8,128)(2,1)S(1)}, u32[]{:S(2)}, u32[]{:S(2)}) collective-permute-start(bf16[256,1024]{1,0:T(8,128)(2,1)} %get-tuple-element.119), channel_id=1, source_target_pairs={{0,1},{1,0},{2,3},{3,2},{4,5},{5,4},{6,7},{7,6},{8,9},{9,8},{10,11... | collective-permute-start | bytes 1572872 | tf_op jit(solution)/shard_map/ppermute | solution.py:26
  307.1 235.0 %reduce-scatter.9.cloned.1.call-start = ((), (), s32[]{:S(2)}) async-start(), calls=%async_computation.4 | async-start | bytes 4718592
  323.4 71.1 %collective-permute-start.32 = (bf16[256,1024]{1,0:T(8,128)(2,1)S(1)}, bf16[256,1024]{1,0:T(8,128)(2,1)S(1)}, u32[]{:S(2)}, u32[]{:S(2)}) collective-permute-start(bf16[256,1024]{1,0:T(8,128)(2,1)S(1)} %copy-done.66), channel_id=1, source_target_pairs={{0,1},{1,0},{2,3},{3,2},{4,5},{5,4},{6,7},{7,6},{8,9},{9,8},{10,11... | collective-permute-start | bytes 1572872 | tf_op jit(solution)/shard_map/ppermute | solution.py:26
  325.1 69.4 %collective-permute-start.38 = (bf16[256,1024]{1,0:T(8,128)(2,1)S(1)}, bf16[256,1024]{1,0:T(8,128)(2,1)S(1)}, u32[]{:S(2)}, u32[]{:S(2)}) collective-permute-start(bf16[256,1024]{1,0:T(8,128)(2,1)S(1)} %add_convert_fusion.6), channel_id=1, source_target_pairs={{0,2},{1,3},{2,0},{3,1},{4,6},{5,7},{6,4},{7,5},{8,10},{9,11},{10,... | collective-permute-start | bytes 1572872 | tf_op jit(solution)/shard_map/ppermute | solution.py:26
  374.7 75.3 %collective-permute-start.49 = (bf16[1024,256]{1,0:T(8,128)(2,1)}, bf16[1024,256]{1,0:T(8,128)(2,1)S(1)}, u32[]{:S(2)}, u32[]{:S(2)}) collective-permute-start(bf16[1024,256]{1,0:T(8,128)(2,1)} %get-tuple-element.100), channel_id=1, source_target_pairs={{4,0},{8,4},{12,8},{16,12},{20,16},{24,20},{28,24},{5,1},{9,5},{13... | collective-permute-start | bytes 1572872 | tf_op jit(solution)/shard_map/ppermute | solution.py:37
  376.1 75.2 %collective-permute-start.50 = (bf16[1024,256]{1,0:T(8,128)(2,1)}, bf16[1024,256]{1,0:T(8,128)(2,1)S(1)}, u32[]{:S(2)}, u32[]{:S(2)}) collective-permute-start(bf16[1024,256]{1,0:T(8,128)(2,1)} %get-tuple-element.101), channel_id=1, source_target_pairs={{0,4},{4,8},{8,12},{12,16},{16,20},{20,24},{24,28},{1,5},{5,9},{9,... | collective-permute-start | bytes 1572872 | tf_op jit(solution)/shard_map/ppermute | solution.py:37
  399.7 80.2 %collective-permute-start.39 = (bf16[256,256]{1,0:T(8,128)(2,1)}, bf16[256,256]{1,0:T(8,128)(2,1)S(1)}, u32[]{:S(2)}, u32[]{:S(2)}) collective-permute-start(bf16[256,256]{1,0:T(8,128)(2,1)} %get-tuple-element.84), channel_id=1, source_target_pairs={{0,3},{1,2},{2,1},{3,0},{4,7},{5,6},{6,5},{7,4},{8,11},{9,10},{10,... | collective-permute-start | bytes 393224 | tf_op jit(solution)/shard_map/ppermute | solution.py:26
  401.0 37.9 %collective-permute-start.48 = (bf16[384,256]{1,0:T(8,128)(2,1)S(1)}, bf16[384,256]{1,0:T(8,128)(2,1)S(1)}, u32[]{:S(2)}, u32[]{:S(2)}) collective-permute-start(bf16[384,256]{1,0:T(8,128)(2,1)S(1)} %copy-done.72), channel_id=1, source_target_pairs={{8,0},{12,4},{16,8},{20,12},{24,16},{28,20},{9,1},{13,5},{17,9},{2... | collective-permute-start | bytes 589832 | tf_op jit(solution)/shard_map/ppermute | solution.py:37
  402.3 37.9 %collective-permute-start.51 = (bf16[384,256]{1,0:T(8,128)(2,1)S(1)}, bf16[384,256]{1,0:T(8,128)(2,1)S(1)}, u32[]{:S(2)}, u32[]{:S(2)}) collective-permute-start(bf16[384,256]{1,0:T(8,128)(2,1)S(1)} %copy-done.71), channel_id=1, source_target_pairs={{0,8},{4,12},{8,16},{12,20},{16,24},{20,28},{1,9},{5,13},{9,17},{1... | collective-permute-start | bytes 589832 | tf_op jit(solution)/shard_map/ppermute | solution.py:37
  438.9 27.2 %collective-permute-start.53 = (bf16[1024,256]{1,0:T(8,128)(2,1)S(1)}, bf16[1024,256]{1,0:T(8,128)(2,1)S(1)}, u32[]{:S(2)}, u32[]{:S(2)}) collective-permute-start(bf16[1024,256]{1,0:T(8,128)(2,1)S(1)} %copy-done.69), channel_id=1, source_target_pairs={{4,0},{8,4},{12,8},{16,12},{20,16},{24,20},{28,24},{5,1},{9,5},{13... | collective-permute-start | bytes 1572872 | tf_op jit(solution)/shard_map/ppermute | solution.py:37
  440.2 31.3 %collective-permute-start.54 = (bf16[1024,256]{1,0:T(8,128)(2,1)S(1)}, bf16[1024,256]{1,0:T(8,128)(2,1)S(1)}, u32[]{:S(2)}, u32[]{:S(2)}) collective-permute-start(bf16[1024,256]{1,0:T(8,128)(2,1)S(1)} %copy-done.68), channel_id=1, source_target_pairs={{0,4},{4,8},{8,12},{12,16},{16,20},{20,24},{24,28},{1,5},{5,9},{9,... | collective-permute-start | bytes 1572872 | tf_op jit(solution)/shard_map/ppermute | solution.py:37
  484.5 30.9 %collective-permute-start.62 = (bf16[2,2,3,256,128]{4,3,2,1,0:T(8,128)(2,1)S(1)}, bf16[2,2,3,256,128]{4,3,2,1,0:T(8,128)(2,1)S(1)}, u32[]{:S(2)}, u32[]{:S(2)}) collective-permute-start(bf16[2,2,3,256,128]{4,3,2,1,0:T(8,128)(2,1)S(1)} %dynamic-slice_bitcast_fusion), channel_id=1, source_target_pairs={{0,8},{4,12},{8,0},{12,4},{16,24},{20,28},{24,16},{28,20},{1,9},{5... | collective-permute-start | bytes 2359304 | tf_op jit(solution)/shard_map/ppermute | solution.py:31
  (125 other events, 1449.7 us)
Sparse Core Ops, SparseCore 0:
  10.1 119.2 all-gather.1
  307.2 69.6 reduce-scatter.6
  380.6 125.0 reduce-scatter.8

commit v2 on v1

--- a/solution.py
+++ b/solution.py
@@ -6,6 +6,7 @@
 from jax.experimental import pallas as pl
 from jax.experimental.pallas import tpu as pltpu
 from jax.sharding import PartitionSpec as P
+
 
 HEAD_DIM = 64
 IMG = 1370
@@ -75,6 +76,10 @@
     )
 
 
+def costs(micros):
+    return pl.CostEstimate(flops=int(micros * 1e9), transcendentals=0, bytes_accessed=1 << 20)
+
+
 def stats_of(chunks, width):
     total = sum(jnp.sum(c, axis=1, keepdims=True) for c in chunks)
     square = sum(jnp.sum(c * c, axis=1, keepdims=True) for c in chunks)
@@ -83,15 +88,16 @@
     return mean, rstd
 
 
-def qkv_kernel(sc, x0, x1, x2, x3, w_ref, vec, qb, vb, n1_ref, q_ref, kv0_ref, kv1_ref, wout, wscr):
+def qkv_kernel(sc, x0, x1, x2, x3, w_ref, vec, qb, vb, n1_ref, q_ref, kv0_ref, kv1_ref, wout, wproj, wscr):
     groups = w_ref.shape[0]
-    part = w_ref.shape[2]
-    features = w_ref.shape[1]
+    part = w_ref.shape[2] * 3 // 4
+    small = w_ref.shape[2] - part
 
     @pl.when(pl.program_id(0) == 0)
     def _():
         for g in range(groups):
-            wscr[:, g * part : (g + 1) * part] = w_ref[g]
+            wscr[:, g * part : (g + 1) * part] = w_ref[g, :, :part]
+            wproj[:, g * small : (g + 1) * small] = w_ref[g, :, part:]
         wout[...] = wscr[...]
 
     t = sc[0]
@@ -118,6 +124,7 @@
 def qkv_call(sc, xs, w, vec, qb, vb):
     rows, fw = xs[0].shape
     groups, features, part = w.shape
+    part = part * 3 // 4
     width = 4 * fw
     tile = TILE
 
@@ -140,6 +147,7 @@
                 row(2 * PAIR),
                 row(2 * PAIR),
                 full((features, groups * part)),
+                full((features, width)),
             ],
             scratch_shapes=[pltpu.VMEM((features, groups * part), BF)],
         ),
@@ -149,9 +157,11 @@
             jax.ShapeDtypeStruct((rows, 2 * PAIR), BF),
             jax.ShapeDtypeStruct((rows, 2 * PAIR), BF),
             jax.ShapeDtypeStruct((features, groups * part), BF),
+            jax.ShapeDtypeStruct((features, width), BF),
         ],
         compiler_params=params(),
         name="qkv",
+        cost_estimate=costs(7),
     )(sc, *xs, w, vec, qb, vb)
 
 
@@ -166,9 +176,15 @@
         copy.wait()
 
 
-def head_lanes(shape, head):
-    lane = lax.broadcasted_iota(jnp.int32, shape, 1)
-    return (lane >= head * HEAD_DIM) & (lane < (head + 1) * HEAD_DIM)
+def by_head(values):
+    lane = lax.broadcasted_iota(jnp.int32, values.shape, 1)
+    first = jnp.where(lane < HEAD_DIM, values, 0.0)
+    second = jnp.where(lane < HEAD_DIM, 0.0, values)
+    return jnp.concatenate([first, second], axis=0).astype(BF)
+
+
+def joined(values):
+    return jnp.concatenate([values[0:HEAD_DIM, :TILE], values[HEAD_DIM:PAIR, TILE:]], axis=0)
 
 
 def scores_of(kv, head_query, j, start, end):
@@ -179,6 +195,10 @@
 
 def fold8(values, how):
     return how(values.reshape(values.shape[0] // 8, 8, values.shape[1]), axis=0)
+
+
+def twice(row):
+    return jnp.concatenate([row, row], axis=1)
 
 
 def fwd_kernel(offsets, counts, sc, q_ref, se_ref, *refs):
@@ -193,42 +213,41 @@
 
     lo = sc[1 + 2 * i]
     hi = sc[2 + 2 * i]
-    start = se_ref[0:1, :]
-    end = se_ref[1:2, :]
-    query = q_ref[...].astype(F32) * SCALE
+    start = twice(se_ref[0:1, :])
+    end = twice(se_ref[1:2, :])
+    head_query = by_head(q_ref[...].astype(F32) * SCALE)
+
+    def first(j, peak):
+        score = scores_of(kv, head_query, j, start, end)
+        s_scr[j - lo] = score
+        return jnp.maximum(peak, fold8(score, jnp.max))
+
+    peak8 = lax.fori_loop(lo, hi, first, jnp.full((8, 2 * TILE), NEG, F32))
+    peak = jnp.max(peak8, axis=0, keepdims=True)
+    peak = jnp.maximum(peak, 0.1 * NEG)
+
+    def second(j, total):
+        expon = jnp.exp(s_scr[j - lo] - peak)
+        s_scr[j - lo] = expon
+        return total + fold8(expon, jnp.sum)
+
+    total8 = lax.fori_loop(lo, hi, second, jnp.zeros((8, 2 * TILE), F32))
+    total = jnp.sum(total8, axis=0, keepdims=True)
+    inverse = 1.0 / jnp.where(end > start, total, 1.0)
+    acc[...] = jnp.zeros(acc.shape, F32)
+
+    def third(j, carry):
+        prob = (s_scr[j - lo] * inverse).astype(BF)
+        vals = kv[pl.ds(pl.multiple_of(j * TILE, TILE), TILE), PAIR : 2 * PAIR]
+        acc[...] += tn(vals, prob)
+        return carry
+
+    lax.fori_loop(lo, hi, third, 0)
     for head in range(2):
-        head_query = jnp.where(head_lanes(query.shape, head), query, 0.0).astype(BF)
-
-        def first(j, peak):
-            score = scores_of(kv, head_query, j, start, end)
-            s_scr[j - lo] = score
-            return jnp.maximum(peak, fold8(score, jnp.max))
-
-        peak8 = lax.fori_loop(lo, hi, first, jnp.full((8, TILE), NEG, F32))
-        peak = jnp.max(peak8, axis=0, keepdims=True)
-        peak = jnp.maximum(peak, 0.1 * NEG)
-
-        def second(j, total):
-            expon = jnp.exp(s_scr[j - lo] - peak)
-            s_scr[j - lo] = expon
-            return total + fold8(expon, jnp.sum)
-
-        total8 = lax.fori_loop(lo, hi, second, jnp.zeros((8, TILE), F32))
-        total = jnp.sum(total8, axis=0, keepdims=True)
-        inverse = 1.0 / jnp.where(end > start, total, 1.0)
-        acc[head] = jnp.zeros(acc.shape[1:], F32)
-
-        def third(j, carry):
-            prob = (s_scr[j - lo] * inverse).astype(BF)
-            vals = kv[pl.ds(pl.multiple_of(j * TILE, TILE), TILE), PAIR : 2 * PAIR]
-            acc[head] += tn(vals, prob)
-            return carry
-
-        lax.fori_loop(lo, hi, third, 0)
-        st_ref[head : head + 1, :] = peak
-        st_ref[2 + head : 3 + head, :] = inverse
-    both = jnp.concatenate([acc[0, 0:HEAD_DIM, :], acc[1, HEAD_DIM:PAIR, :]], axis=0)
-    ctx_ref[...] = both.T.astype(BF)
+        at = slice(head * TILE, (head + 1) * TILE)
+        st_ref[head : head + 1, :] = peak[:, at]
+        st_ref[2 + head : 3 + head, :] = inverse[:, at]
+    ctx_ref[...] = joined(acc[...]).T.astype(BF)
 
 
 def fwd_call(pair, sc, query, spans, pieces, offsets, counts):
@@ -250,8 +269,8 @@
             ],
             scratch_shapes=[
                 pltpu.VMEM((near, 2 * PAIR), BF),
-                pltpu.VMEM((near // TILE, TILE, TILE), F32),
-                pltpu.VMEM((2, PAIR, TILE), F32),
+                pltpu.VMEM((near // TILE, TILE, 2 * TILE), F32),
+                pltpu.VMEM((PAIR, 2 * TILE), F32),
                 pltpu.SemaphoreType.DMA((len(pieces),)),
             ],
         ),
@@ -261,10 +280,11 @@
         ],
         compiler_params=params(),
         name="attn_fwd",
+        cost_estimate=costs(17),
     )(sc, query, spans, *pieces)
 
 
-def bwd_kernel(offsets, counts, own, sc, q_ref, se_ref, st_ref, g_ref, *refs):
+def bwd_kernel(offsets, counts, sc, q_ref, se_ref, st_ref, g_ref, *refs):
     n = len(counts)
     pieces = refs[:n]
     dq_ref = refs[n]
@@ -282,41 +302,38 @@
     hi = sc[2 + 2 * i]
     start = se_ref[0:1, :]
     end = se_ref[1:2, :]
-    query = q_ref[...].astype(F32) * SCALE
-    grad = g_ref[0].astype(F32)
-    for head in range(2):
-        lanes = head_lanes(query.shape, head)
-        head_query = jnp.where(lanes, query, 0.0).astype(BF)
-        head_grad = jnp.where(lanes, grad, 0.0).astype(BF)
-        peak = st_ref[head : head + 1, :]
-        inverse = st_ref[2 + head : 3 + head, :]
-
-        def first(j, dot8):
-            score = scores_of(kv, head_query, j, start, end)
-            weight = jnp.exp(score - peak) * inverse
-            vals = kv[pl.ds(pl.multiple_of(j * TILE, TILE), TILE), PAIR : 2 * PAIR]
-            grad_prob = nt(vals, head_grad)
-            w_scr[j - lo] = weight
-            g_scr[j - lo] = grad_prob
-            return dot8 + fold8(weight * grad_prob, jnp.sum)
-
-        dot8 = lax.fori_loop(lo, hi, first, jnp.zeros((8, TILE), F32))
-        rowdot = jnp.sum(dot8, axis=0, keepdims=True)
-        dq_scr[head] = jnp.zeros(dq_scr.shape[1:], F32)
-
-        def second(j, carry):
-            weight = w_scr[j - lo]
-            grad_score = (weight * (g_scr[j - lo] - rowdot)).astype(BF)
-            prob = weight.astype(BF)
-            at = pl.ds(pl.multiple_of(j * TILE, TILE), TILE)
-            acc[at, 0:PAIR] += nn(grad_score, head_query)
-            acc[at, PAIR : 2 * PAIR] += nn(prob, head_grad)
-            dq_scr[head] += tn(kv[at, 0:PAIR], grad_score)
-            return carry
-
-        lax.fori_loop(lo, hi, second, 0)
-    both = jnp.concatenate([dq_scr[0, 0:HEAD_DIM, :], dq_scr[1, HEAD_DIM:PAIR, :]], axis=0)
-    dq_ref[...] = (both.T * SCALE).astype(BF)
+    start = twice(start)
+    end = twice(end)
+    head_query = by_head(q_ref[...].astype(F32) * SCALE)
+    head_grad = by_head(g_ref[0].astype(F32))
+    peak = jnp.concatenate([st_ref[0:1, :], st_ref[1:2, :]], axis=1)
+    inverse = jnp.concatenate([st_ref[2:3, :], st_ref[3:4, :]], axis=1)
+
+    def first(j, dot8):
+        score = scores_of(kv, head_query, j, start, end)
+        weight = jnp.exp(score - peak) * inverse
+        vals = kv[pl.ds(pl.multiple_of(j * TILE, TILE), TILE), PAIR : 2 * PAIR]
+        grad_prob = nt(vals, head_grad)
+        w_scr[j - lo] = weight
+        g_scr[j - lo] = grad_prob
+        return dot8 + fold8(weight * grad_prob, jnp.sum)
+
+    dot8 = lax.fori_loop(lo, hi, first, jnp.zeros((8, 2 * TILE), F32))
+    rowdot = jnp.sum(dot8, axis=0, keepdims=True)
+    dq_scr[...] = jnp.zeros(dq_scr.shape, F32)
+
+    def second(j, carry):
+        weight = w_scr[j - lo]
+        grad_score = (weight * (g_scr[j - lo] - rowdot)).astype(BF)
+        prob = weight.astype(BF)
+        at = pl.ds(pl.multiple_of(j * TILE, TILE), TILE)
+        acc[at, 0:PAIR] += nn(grad_score, head_query)
+        acc[at, PAIR : 2 * PAIR] += nn(prob, head_grad)
+        dq_scr[...] += tn(kv[at, 0:PAIR], grad_score)
+        return carry
+
+    lax.fori_loop(lo, hi, second, 0)
+    dq_ref[...] = (joined(dq_scr[...]).T * SCALE).astype(BF)
 
     @pl.when(r == pl.num_programs(0) - 1)
     def _():
@@ -333,7 +350,7 @@
         return pl.BlockSpec((count, 2 * PAIR), lambda r, sc: (0, 0))
 
     return pl.pallas_call(
-        functools.partial(bwd_kernel, offsets, counts, own),
+        functools.partial(bwd_kernel, offsets, counts),
         grid_spec=pltpu.PrefetchScalarGridSpec(
             num_scalar_prefetch=1,
             grid=(rows // TILE,),
@@ -348,10 +365,10 @@
             + [whole(c) for c in counts],
             scratch_shapes=[
                 pltpu.VMEM((near, 2 * PAIR), BF),
-                pltpu.VMEM((near // TILE, TILE, TILE), F32),
-                pltpu.VMEM((near // TILE, TILE, TILE), F32),
+                pltpu.VMEM((near // TILE, TILE, 2 * TILE), F32),
+                pltpu.VMEM((near // TILE, TILE, 2 * TILE), F32),
                 pltpu.VMEM((near, 2 * PAIR), F32),
-                pltpu.VMEM((2, PAIR, TILE), F32),
+                pltpu.VMEM((PAIR, 2 * TILE), F32),
                 pltpu.SemaphoreType.DMA((len(pieces),)),
             ],
         ),
@@ -362,6 +379,7 @@
         ],
         compiler_params=params(),
         name="attn_bwd",
+        cost_estimate=costs(22),
     )(sc, query, spans, stats, grads, *pieces)
 
 
@@ -414,6 +432,7 @@
         ],
         compiler_params=params(),
         name="proj",
+        cost_estimate=costs(4),
     )(sc, *contexts, *ws, *xs, vec)
 
 
@@ -476,7 +495,41 @@
         + [jax.ShapeDtypeStruct((8, hidden_units), F32)],
         compiler_params=params(),
         name="mlp",
+        cost_estimate=costs(10),
     )(*normed, *grads, weights, weights, bias)
+
+
+def wgrad_kernel(n0, n1, n2, n3, g0, g1, g2, g3, ba, bb, ha, hb, out):
+    hidden_units = ba.shape[1]
+    for k, (lefts, rights) in enumerate((((n0, n1, n2, n3), (ba, bb)), ((g0, g1, g2, g3), (ha, hb)))):
+        total = 0.0
+        for half in range(2):
+            left = jnp.concatenate([lefts[2 * half][...], lefts[2 * half + 1][...]], axis=0)
+            total = total + tn(left, rights[half][...])
+        out[:, k * hidden_units : (k + 1) * hidden_units] = total.astype(BF)
+
+
+def wgrad_call(normed, grads, befores, hiddens):
+    sub, width = normed[0].shape
+    rows, hidden_units = befores[0].shape
+    tile = TILE
+
+    def left():
+        return pl.BlockSpec((sub, tile), lambda i: (0, i))
+
+    def right():
+        return pl.BlockSpec((rows, hidden_units), lambda i: (0, 0))
+
+    return pl.pallas_call(
+        wgrad_kernel,
+        grid=(width // tile,),
+        in_specs=[left()] * 8 + [right()] * 4,
+        out_specs=pl.BlockSpec((tile, 2 * hidden_units), lambda i: (i, 0)),
+        out_shape=jax.ShapeDtypeStruct((width, 2 * hidden_units), BF),
+        compiler_params=params(),
+        name="wgrads",
+        cost_estimate=costs(9),
+    )(*normed, *grads, *befores, *hiddens)
 
 
 def mid_kernel(
@@ -551,6 +604,7 @@
         ],
         compiler_params=params(),
         name="mid",
+        cost_estimate=costs(6),
     )(sc, *parts, *cots, middle, branch, *ws, vec)
 
 
@@ -588,17 +642,75 @@
         out_shape=[jax.ShapeDtypeStruct((sub, wide // 3), BF)] * 4,
         compiler_params=params(),
         name="gn1",
+        cost_estimate=costs(6),
     )(sc, gq0, gq1, gk, gv, w)
 
 
-def last_kernel(sc, a0, a1, a2, x0, x1, x2, x3, gm, vec, o0, o1, o2, o3, sums, scr):
+def qkvg_kernel(gq, gk, gv, n1, out):
+    unit = out.shape[2]
+    per = n1.shape[1] // unit
+    for c, ref in enumerate((gq, gk, gv)):
+        both = tn(ref[...], n1[...]).astype(BF)
+        for k in range(per):
+            out[c * per + k] = both[:, k * unit : (k + 1) * unit]
+
+
+def qkvg_call(gq, gk, gv, n1):
+    features = gq.shape[1]
+    unit = n1.shape[1] // 8
+    return pl.pallas_call(
+        qkvg_kernel,
+        out_shape=jax.ShapeDtypeStruct((24, features, unit), BF),
+        compiler_params=params(0),
+        name="qkv_grad",
+        cost_estimate=costs(5),
+    )(gq, gk, gv, n1)
+
+
+def nsum_kernel(sc, a0, a1, a2, a3, x0, x1, x2, x3, sums):
+    t = sc[0]
+    r = pl.program_id(0)
+    width = 4 * x0.shape[1]
+
+    @pl.when(r == 0)
+    def _():
+        sums[...] = jnp.zeros(sums.shape, F32)
+
+    value = jnp.concatenate(unxor([x[...].astype(F32) for x in (x0, x1, x2, x3)], t), axis=1)
+    mean, rstd = stats_of([value], width)
+    scaled = (value - mean) * rstd
+    for k, ref in enumerate((a0, a1, a2, a3)):
+
+        @pl.when(r == k)
+        def _():
+            part = ref[...].astype(F32)
+            sums[0:1, :] += jnp.sum(part * scaled, axis=0, keepdims=True)
+            sums[1:2, :] += jnp.sum(part, axis=0, keepdims=True)
+
+
+def nsum_call(sc, pieces, xs):
+    sub, width = pieces[0].shape
+    fw = width // 4
+    return pl.pallas_call(
+        nsum_kernel,
+        grid_spec=pltpu.PrefetchScalarGridSpec(
+            num_scalar_prefetch=1,
+            grid=(4,),
+            in_specs=[whole_spec((sub, width))] * 4
+            + [pl.BlockSpec((sub, fw), lambda r, sc: (sc[0] ^ r, 0))] * 4,
+            out_specs=whole_spec((8, width)),
+        ),
+        out_shape=jax.ShapeDtypeStruct((8, width), F32),
+        compiler_params=params(),
+        name="norm_sums",
+        cost_estimate=costs(5),
+    )(sc, *pieces, *xs)
+
+
+def last_kernel(sc, a0, a1, a2, x0, x1, x2, x3, gm, vec, o0, o1, o2, o3, scr):
     t = sc[0]
     fw = x0.shape[1]
     width = 4 * fw
-
-    @pl.when(pl.program_id(0) == 0)
-    def _():
-        sums[...] = jnp.zeros(sums.shape, F32)
 
     grad_normed = a0[...].astype(F32) + a1[...].astype(F32) + a2[...].astype(F32)
     chunks = unxor([x[...].astype(F32) for x in (x0, x1, x2, x3)], t)
@@ -611,8 +723,6 @@
     scr[...] = (gm[...] + rstd * (inner - mean_a - scaled * mean_b)).astype(BF)
     for r, ref in enumerate((o0, o1, o2, o3)):
         ref[...] = scr[:, pl.ds(pl.multiple_of((t ^ r) * fw, fw), fw)]
-    sums[0:1, :] += jnp.sum(grad_normed * scaled, axis=0, keepdims=True)
-    sums[1:2, :] += jnp.sum(grad_normed, axis=0, keepdims=True)
 
 
 def last_call(sc, parts, xs, grad_middle, vec):
@@ -632,13 +742,13 @@
             num_scalar_prefetch=1,
             grid=(2,),
             in_specs=[row(width)] * 3 + [mine(fw)] * 4 + [row(width), whole_spec(vec.shape)],
-            out_specs=[row(fw)] * 4 + [whole_spec((8, width))],
+            out_specs=[row(fw)] * 4,
             scratch_shapes=[pltpu.VMEM((tile, width), BF)],
         ),
-        out_shape=[jax.ShapeDtypeStruct((rows, fw), BF)] * 4
-        + [jax.ShapeDtypeStruct((8, width), F32)],
+        out_shape=[jax.ShapeDtypeStruct((rows, fw), BF)] * 4,
         compiler_params=params(),
         name="last",
+        cost_estimate=costs(3),
     )(sc, *parts, *xs, grad_middle, vec)
 
 
@@ -680,7 +790,12 @@
         + [jax.ShapeDtypeStruct((8, width), F32)],
         compiler_params=params(),
         name="block_out",
+        cost_estimate=costs(3),
     )(sc, *parts, *cots, middle, vec)
+
+
+def after(*values):
+    return lax.optimization_barrier(values)
 
 
 def placed(pieces, t, axis):
@@ -690,6 +805,16 @@
 def reduce4(pieces):
     far = (pieces[2].astype(F32) + px(pieces[3], 1).astype(F32)).astype(BF)
     return pieces[0], px(pieces[1], 1), px(far, 2)
+
+
+def halved(blocks, s):
+    for axis, bits, place in ((1, 2, 1), (1, 1, 0), (0, 4, 2)):
+        mine = (s >> place) & 1
+        keep = lax.dynamic_index_in_dim(blocks, mine, axis, keepdims=False)
+        send = lax.dynamic_index_in_dim(blocks, 1 - mine, axis, keepdims=False)
+        got = ps(send.astype(BF), bits)
+        blocks = keep.astype(F32) + got.astype(F32)
+    return blocks
 
 
 def spans_of(image_ids, row_count, first_row, margin, near):
@@ -750,16 +875,23 @@
 
     xs = gather4(block_input)
     if n_seq == 8:
-        z2, z4, z6 = ps(qkv_weight, 2), ps(qkv_weight, 4), ps(qkv_weight, 6)
+        own = jnp.concatenate([qkv_weight, proj_weight], axis=1)
+        z2, z4, z6 = ps(own, 2), ps(own, 4), ps(own, 6)
         found = [None] * 8
-        for bits, piece in ((0, qkv_weight), (2, z2), (4, z4), (6, z6)):
+        for bits, piece in ((0, own), (2, z2), (4, z4), (6, z6)):
             found[bits] = piece
             found[bits ^ 1] = ps(piece, 1)
-        w_qkv = jnp.zeros((8,) + qkv_weight.shape, BF)
+        w_qkv = jnp.zeros((8,) + own.shape, BF)
         for bits in range(8):
             w_qkv = lax.dynamic_update_slice(w_qkv, found[bits][None], (s ^ bits, 0, 0))
     else:
-        w_qkv = lax.all_gather(qkv_weight, "seq", axis=1, tiled=True)[None]
+        w_qkv = jnp.concatenate(
+            [
+                lax.all_gather(w, "seq", axis=1, tiled=True)[None]
+                for w in (qkv_weight, proj_weight)
+            ],
+            axis=2,
+        )
     vec_own = jnp.stack(
         [
             norm1_gain,
@@ -773,11 +905,7 @@
         ]
     )
     vec = placed([vec_own] + [px(vec_own, r) for r in range(1, 4)], t, 1)
-    others = lax.all_gather(
-        jnp.concatenate([fc1_weight, fc2_weight, proj_weight], axis=0), "seq", axis=1, tiled=True
-    )
     units = fc1_weight.shape[0]
-    ws = gather4(others[2 * units :])
 
     offsets_of = []
     counts = []
@@ -797,7 +925,7 @@
     sc = jnp.concatenate([t[None], edges])
     sc_t = t[None]
 
-    normed1, query, kv0, kv1, w_full = qkv_call(
+    normed1, query, kv0, kv1, w_full, proj_full = qkv_call(
         sc_t, xs, w_qkv, vec, q_bias[None, :], v_bias[None, :]
     )
     nears = []
@@ -818,8 +946,15 @@
     grads = gather4(grad_second)
     contexts = []
     stats = []
+    stacked = jnp.concatenate([fc1_weight, fc2_weight], axis=0)
+    stacked, *nears[0] = after(stacked, *nears[0])
+    others = lax.all_gather(stacked, "seq", axis=1, tiled=True)
+    ws = gather4(proj_full)
     for pair in range(2):
         ctx, st = fwd_call(pair, sc, query, spans, nears[pair], offsets, counts)
+        if pair == 0:
+            ctx, *rest = after(ctx, *ws, *grads)
+            ws, grads = rest[:4], rest[4:]
         contexts.append(ctx)
         stats.append(st)
     context = jnp.concatenate(contexts, axis=1)
@@ -830,28 +965,22 @@
     n_far = px(n_across, 1)
     bias1 = fc1_bias[None, :]
     hid_b, gb_b, s2, s3, d2, d3, fb_b = mlp_call((n_across, n_far), grads[2:], others, bias1)
+    far = (d2.astype(F32) + px(d3, 1).astype(F32)).astype(BF)
+    far, n_near = after(far, n_near)
+    far = px(far, 2)
     hid_a, gb_a, s0, s1, d0, d1, fb_a = mlp_call((normed2, n_near), grads[:2], others, bias1)
-    parts = reduce4([d0, d1, d2, d3])
+    from_near = px(d1, 1)
+
+    fc_part = wgrad_call((normed2, n_near, n_across, n_far), grads, (gb_a, gb_b), (hid_a, hid_b))
+    far, fc_part = after(far, fc_part)
+    fc_out = lax.psum_scatter(fc_part, "seq", scatter_dimension=0, tiled=True)
     grad_middle, grad_branch, grad_ctx, sums_mid = mid_call(
-        sc_t, parts, cots, middle, branch, ws, vec
+        sc_t, (d0, from_near, far), cots, middle, branch, ws, vec
     )
-    swapped = swap4([grad_ctx[r] for r in range(4)])
-    grad_rows = jnp.stack(swapped)
-
-    rows_a = jnp.concatenate([normed2, n_near], axis=0)
-    rows_b = jnp.concatenate([n_across, n_far], axis=0)
-    gs_a = jnp.concatenate(grads[:2], axis=0)
-    gs_b = jnp.concatenate(grads[2:], axis=0)
-    fc1_part = (tn(gb_a, rows_a) + tn(gb_b, rows_b)).astype(BF)
-    fc2_part = (tn(hid_a, gs_a) + tn(hid_b, gs_b)).astype(BF)
-    fc_out = lax.psum_scatter(
-        jnp.concatenate([fc1_part, fc2_part], axis=0), "seq", scatter_dimension=1, tiled=True
-    ).astype(F32)
-    o0, o1, o2, o3, sums_out = out_call(sc_t, reduce4([s0, s1, s2, s3]), cots, middle, vec)
-    block_output = placed(swap4([o0, o1, o2, o3]), t, 0)
-    branch_rows = placed(gather4(grad_branch), t, 0)
-    proj_part = tn(context, branch_rows).astype(BF)
-    proj_out = lax.psum_scatter(proj_part, "seq", scatter_dimension=1, tiled=True).astype(F32)
+    grad_rows = jnp.stack(swap4([grad_ctx[r] for r in range(4)]))
+    grad_rows, grad_branch, s0, s1, s2, s3 = after(grad_rows, grad_branch, s0, s1, s2, s3)
+    seconds = reduce4([s0, s1, s2, s3])
+    branch_all = gather4(grad_branch)
 
     grad_q = []
     grad_k = []
@@ -860,6 +989,21 @@
         got = bwd_call(
             pair, sc, query, spans, stats[pair], grad_rows, nears[pair], offsets, counts, reach
         )
+        got = list(got)
+        if pair == 0:
+            got[1], grad_rows = after(got[1], grad_rows)
+        if pair == 0:
+            got[0], *branch_all = after(got[0], *branch_all)
+            branch_rows = placed(branch_all, t, 0)
+            proj_part = tn(branch_rows, context).astype(BF)
+            if n_seq == 8:
+                proj_out = halved(proj_part.reshape(2, 2, 2, width // 8, features), s)
+            else:
+                proj_out = lax.psum_scatter(proj_part, "seq", scatter_dimension=0, tiled=True)
+        else:
+            got[0], *seconds = after(got[0], *seconds)
+            o0, o1, o2, o3, sums_out = out_call(sc_t, seconds, cots, middle, vec)
+            block_output = placed(swap4([o0, o1, o2, o3]), t, 0)
         grad_q.append(got[0])
         total = got[1 + reach]
         for k, (offset, count) in enumerate(zip(offsets_of, counts)):
@@ -877,37 +1021,24 @@
     gk = jnp.concatenate(grad_k, axis=1)
     gv = jnp.concatenate(grad_v, axis=1)
     gq = jnp.concatenate(grad_q, axis=1)
-    pieces = gn1_call(sc_t, grad_q[0], grad_q[1], gk, gv, w_full)
-    i0, i1, i2, i3, sums_last = last_call(sc_t, reduce4(pieces), xs, grad_middle, vec)
-    input_grad = placed(swap4([i0, i1, i2, i3]), t, 0)
-    qkv_parts = [tn(g, normed1) for g in (gq, gk, gv)]
     if n_seq == 8:
-        unit = 128
-        blocks = jnp.concatenate(
-            [
-                g.astype(BF).reshape(features, width // unit, unit).transpose(1, 0, 2)
-                for g in qkv_parts
-            ],
-            axis=0,
-        ).reshape(2, 2, 2, 3, features, unit)
-        for axis, bits in ((1, 2), (1, 1), (0, 4)):
-            if bits == 2:
-                mine = (s >> 1) & 1
-            elif bits == 1:
-                mine = s & 1
-            else:
-                mine = (s >> 2) & 1
-            keep = lax.dynamic_index_in_dim(blocks, mine, axis, keepdims=False)
-            send = lax.dynamic_index_in_dim(blocks, 1 - mine, axis, keepdims=False)
-            blocks = (keep.astype(F32) + ps(send.astype(BF), bits).astype(F32))
-        qkv_out = blocks.transpose(1, 0, 2).reshape(features, 3 * unit)
+        unit = width // 8
+        blocks = qkvg_call(gq, gk, gv, normed1).reshape(2, 2, 2, 3, features, unit)
+        blocks, gk = after(blocks, gk)
+        blocks = halved(blocks, s)
+        qkv_out = jnp.concatenate([blocks[k] for k in range(3)], axis=1)
     else:
+        qkv_parts = [tn(g, normed1) for g in (gq, gk, gv)]
         qkv_out = lax.psum_scatter(
             jnp.stack(qkv_parts, axis=1).reshape(features, 3 * width).astype(BF),
             "seq",
             scatter_dimension=1,
             tiled=True,
         ).astype(F32)
+    pieces = gn1_call(sc_t, grad_q[0], grad_q[1], gk, gv, w_full)
+    sums_last = nsum_call(sc_t, pieces, xs)
+    i0, i1, i2, i3 = last_call(sc_t, reduce4(pieces), xs, grad_middle, vec)
+    input_grad = placed(swap4([i0, i1, i2, i3]), t, 0)
 
     rows8 = jnp.concatenate([sums_last[0:2], sums_mid[0:4], sums_out[0:2]], axis=0)
     cut = [lax.dynamic_slice_in_dim(rows8, (t ^ r) * fw, fw, 1) for r in range(4)]
@@ -935,9 +1066,9 @@
         block_output,
         input_grad,
         qkv_out,
-        proj_out,
-        fc_out[:units],
-        fc_out[units:],
+        proj_out.T.astype(F32),
+        fc_out[:, :units].T.astype(F32),
+        fc_out[:, units:].T.astype(F32),
         own8[0],
         own8[1],
         q_bias_grad,
@@ -957,6 +1088,7 @@
     by_tensor = P("tensor")
     in_specs = (P("seq", "tensor"), P("seq", "tensor"), P()) + (cut,) * 4 + (by_tensor,) * 11
     out_specs = (P("seq", "tensor"), P("seq", "tensor")) + (cut,) * 4 + (by_tensor,) * 11
+
     return jax.shard_map(
         per_device, mesh=mesh, in_specs=in_specs, out_specs=out_specs, check_vma=False
     )

time: 561 us -> 487 us (0.87); the launches traced: 551 us -> 485 us
  waiting for transfers between devices: 203 us -> 177 us
  matrix products: 14.6 us -> 0.76 us
  Pallas kernels: 161 us -> 148 us
  local copies, waits for them, and re-layouts: 35.6 us -> 22.6 us
    all_gather x1, waiting for transfers between devices: 52.1 us -> 7.24 us  [per_device(): others = lax.all_gather(stacked, 'seq', axis=1, tiled=True)]
    ppermute x16, waiting for transfers between devices: 17.2 us -> 56.3 us  [passed_along(): return lax.ppermute(block, 'seq', route)]
    ppermute x45, waiting for transfers between devices: 79.1 us -> 53.8 us  [px(): return lax.ppermute(value, 'tensor', pairs)]
    pallas_call x2, Pallas kernels: 51.7 us -> 34 us  [fwd_call(): pl.pallas_call(functools.partial(fwd_kernel, offsets, counts), grid_spec=...]
    dot_general x8 -> x1, matrix products: 14.6 us -> 0.76 us  [tn(): lax.dot_general(left, right, (((0,), (0,)), ((), ())), preferred_element_...]
    unnamed x168 -> x117, local copies, waits for them, and re-layouts: 23 us -> 11.4 us
    ppermute x16, starting transfers between devices: 61.2 us -> 54 us  [passed_along(): return lax.ppermute(block, 'seq', route)]
    ppermute x13 -> x16, starting transfers between devices: 15.7 us -> 21.4 us  [ps(): return lax.ppermute(value, 'seq', pairs)]
  transfers between devices with their start and end apart: 77 -> 79, of which waited for: 27 -> 33; matrix products, arithmetic and copies ran while one was open for 9% -> 6% of each run, Pallas kernels for 28% -> 16%
where the time goes in v2:
time: 487 us; the launch traced here: 485 us
  waiting for transfers between devices  177 us (36%)
  Pallas kernels  148 us (30%)
  starting transfers between devices  104 us (21%)
  local copies, waits for them, and re-layouts  22.6 us (5%)
  other arithmetic  17.4 us (4%)
  between operations  15.5 us (3%)
    ppermute x16, waiting for transfers between devices, ps(): return lax.ppermute(value, 'seq', pairs)  59.2 us
    ppermute x16, waiting for transfers between devices, passed_along(): return lax.ppermute(block, 'seq', route)  56.3 us
    ppermute x16, starting transfers between devices, passed_along(): return lax.ppermute(block, 'seq', route)  54 us
    ppermute x45, waiting for transfers between devices, px(): return lax.ppermute(value, 'tensor', pairs)  53.8 us
    pallas_call x2, Pallas kernels, bwd_call(): pl.pallas_call(functools.partial(bwd_kernel, offsets, counts), grid_spec=...  43.2 us
    pallas_call x2, Pallas kernels, fwd_call(): pl.pallas_call(functools.partial(fwd_kernel, offsets, counts), grid_spec=...  34 us
    ppermute x45, starting transfers between devices, px(): return lax.ppermute(value, 'tensor', pairs)  28.7 us
    ppermute x16, starting transfers between devices, ps(): return lax.ppermute(value, 'seq', pairs)  21.4 us
  transfers between devices with their start and end apart: 79, of which 33 were waited for; matrix products, arithmetic and copies ran while one was open for 6% of the time, Pallas kernels for 16%

profile of v2, /device:TPU:0, one launch (start us, length us, event | category | flops | bytes accessed | tf_op | source)
XLA Modules:
  0.0 484.7 jit_solution(4509096305445158532)
XLA Ops:
  15.2 7.7 %collective-permute-done.10 = f32[8,256]{1,0:T(8,128)S(1)} collective-permute-done((f32[8,256]{1,0:T(8,128)S(1)}, f32[8,256]{1,0:T(8,128)S(1)}, u32[]{:S(2)}, u32[]{:S(2)}) %collective-permute-start.10) | collective-permute-done | bytes 8224 | tf_op jit(solution)/shard_map/ppermute | solution.py:27
  39.1 7.9 %collective-permute-done.6 = bf16[256,512]{1,0:T(8,128)(2,1)S(1)} collective-permute-done((bf16[256,512]{1,0:T(8,128)(2,1)S(1)}, bf16[256,512]{1,0:T(8,128)(2,1)S(1)}, u32[]{:S(2)}, u32[]{:S(2)}) %collective-permute-start.6) | collective-permute-done | bytes 262176 | tf_op jit(solution)/shard_map/ppermute | solution.py:32
  50.6 6.6 %collective-permute-done.7 = bf16[256,512]{1,0:T(8,128)(2,1)S(1)} collective-permute-done((bf16[256,512]{1,0:T(8,128)(2,1)S(1)}, bf16[256,512]{1,0:T(8,128)(2,1)S(1)}, u32[]{:S(2)}, u32[]{:S(2)}) %collective-permute-start.7) | collective-permute-done | bytes 262176 | tf_op jit(solution)/shard_map/ppermute | solution.py:32
  61.5 7.6 %qkv.1 = (bf16[1024,1024]{1,0:T(8,128)(2,1)}, bf16[1024,256]{1,0:T(8,128)(2,1)}, bf16[1024,256]{1,0:T(8,128)(2,1)}, bf16[1024,256]{1,0:T(8,128)(2,1)}, bf16[256,...) custom-call(s32[1]{0:T(128)} %bitcast.sc, bf16[1024,256]{1,0:T(8,128)(2,1)} %x0.7, ...), custom_call_target="tpu_custom_call" | custom-call | flops 7000000000 | bytes 1048576 | tf_op jit(solution)/shard_map/qkv/pallas_call | solution.py:137
  73.7 11.6 %collective-permute-start.17 = (bf16[384,256]{1,0:T(8,128)(2,1)S(1)}, bf16[384,256]{1,0:T(8,128)(2,1)S(1)}, u32[]{:S(2)}, u32[]{:S(2)}) collective-permute-start(bf16[384,256]{1,0:T(8,128)(2,1)S(1)} %get-tuple-element.300), channel_id=1, source_target_pairs={{0,8},{4,12},{8,16},{12,20},{16,24},{20,28},{1,9},{5,13},{9,17},{1... | collective-permute-start | bytes 589832 | tf_op jit(solution)/shard_map/ppermute | solution.py:38
  88.5 8.8 %collective-permute-done.20.refs_4_ = bf16[384,256]{1,0:T(8,128)(2,1)} collective-permute-done((bf16[384,256]{1,0:T(8,128)(2,1)S(1)}, bf16[384,256]{1,0:T(8,128)(2,1)}, u32[]{:S(2)}, u32[]{:S(2)}) %collective-permute-start.20) | collective-permute-done | bytes 196640 | tf_op jit(solution)/shard_map/ppermute | solution.py:38
  105.0 11.3 %collective-permute-start.13 = (bf16[384,256]{1,0:T(8,128)(2,1)S(1)}, bf16[384,256]{1,0:T(8,128)(2,1)S(1)}, u32[]{:S(2)}, u32[]{:S(2)}) collective-permute-start(bf16[384,256]{1,0:T(8,128)(2,1)S(1)} %get-tuple-element.302), channel_id=1, source_target_pairs={{0,8},{4,12},{8,16},{12,20},{16,24},{20,28},{1,9},{5,13},{9,17},{1... | collective-permute-start | bytes 589832 | tf_op jit(solution)/shard_map/ppermute | solution.py:38
  118.4 17.1 %attn_fwd.3 = (bf16[1024,128]{1,0:T(8,128)(2,1)}, f32[8,1024]{1,0:T(8,128)}) custom-call(s32[9]{0:T(128)} %pad_add_fusion.1.sc, bf16[1024,256]{1,0:T(8,128)(2,1)} %get-tuple-element.111.q_ref, s32[8,1024]{1,0:T(8,128)} %add_add_fusion.se_ref, bf16[384,256]{1,0:T(8,128)(2,1)} %copy-done.47, bf16[1024,256]{1,0:T(8,128)(2,1)} %copy-done.26, ...), custom_call_target="tpu_custom_call" | custom-call | flops 16999999488 | bytes 1048576 | tf_op jit(solution)/shard_map/attn_fwd/pallas_call | solution.py:256
  137.9 16.9 %attn_fwd.2 = (bf16[1024,128]{1,0:T(8,128)(2,1)}, f32[8,1024]{1,0:T(8,128)}) custom-call(s32[9]{0:T(128)} %pad_add_fusion.1.sc, bf16[1024,256]{1,0:T(8,128)(2,1)} %get-tuple-element.111.q_ref, s32[8,1024]{1,0:T(8,128)} %add_add_fusion.se_ref, bf16[384,256]{1,0:T(8,128)(2,1)} %copy-done.48, bf16[1024,256]{1,0:T(8,128)(2,1)} %copy-done.30, ...), custom_call_target="tpu_custom_call" | custom-call | flops 16999999488 | bytes 1048576 | tf_op jit(solution)/shard_map/attn_fwd/pallas_call | solution.py:256
  158.7 4.5 collective-permute-done.31.c2
  165.7 4.2 proj.1
  171.5 13.2 %collective-permute-done.33.n0.n2 = bf16[256,1024]{1,0:T(8,128)(2,1)S(1)} collective-permute-done((bf16[256,1024]{1,0:T(8,128)(2,1)}, bf16[256,1024]{1,0:T(8,128)(2,1)S(1)}, u32[]{:S(2)}, u32[]{:S(2)}) %collective-permute-start.33) | collective-permute-done | bytes 524320 | tf_op jit(solution)/shard_map/ppermute | solution.py:27
  186.7 7.2 %all-gather.2.cloned.1.call-done.fc1.fc2 = bf16[2048,1024]{1,0:T(8,128)(2,1)} async-done(((bf16[2048,128]{1,0:T(8,128)(2,1)}), bf16[2048,1024]{1,0:T(8,128)(2,1)}) %all-gather.2.cloned.1.call-update) | async-done | bytes 4194320 | tf_op jit(solution)/shard_map/all_gather | solution.py:951
  193.9 10.2 %mlp.2 = (bf16[512,1024]{1,0:T(8,128)(2,1)}, bf16[512,1024]{1,0:T(8,128)(2,1)}, bf16[256,1024]{1,0:T(8,128)(2,1)}, bf16[256,1024]{1,0:T(8,128)(2,1)}, bf16[256,1...) custom-call(bf16[256,1024]{1,0:T(8,128)(2,1)} %copy-done.41, bf16[256,1024]{1,0:T(8,128)(2,1)} %copy-done.42, ...), custom_call_target="tpu_custom_call" | custom-call | flops 10000000000 | bytes 1048576 | tf_op jit(solution)/shard_map/mlp/pallas_call | solution.py:481
  208.4 10.1 %mlp.3 = (bf16[512,1024]{1,0:T(8,128)(2,1)}, bf16[512,1024]{1,0:T(8,128)(2,1)}, bf16[256,1024]{1,0:T(8,128)(2,1)}, bf16[256,1024]{1,0:T(8,128)(2,1)}, bf16[256,1...) custom-call(bf16[256,1024]{1,0:T(8,128)(2,1)} %get-tuple-element.129.n0, ...), custom_call_target="tpu_custom_call" | custom-call | flops 10000000000 | bytes 1048576 | tf_op jit(solution)/shard_map/mlp/pallas_call | solution.py:481
  220.2 9.3 %wgrads.1 = bf16[1024,2048]{1,0:T(8,128)(2,1)} custom-call(bf16[256,1024]{1,0:T(8,128)(2,1)} %get-tuple-element.129.n0, bf16[256,1024]{1,0:T(8,128)(2,1)} %copy-done.45, bf16[256,1024]{1,0:T(8,128)(2,1)} %copy-done.41, bf16[256,1024]{1,0:T(8,128)(2,1)} %copy-done.42, bf16[256,1024]{1,0:T(8,128)(2,1)} %copy-done.9, bf16[256,1024]{1,0:T(8,128)(2,1)} %copy-done.36, ...), custom_call_target="tpu_custom_call" | custom-call | flops 8999999488 | bytes 1048576 | tf_op jit(solution)/shard_map/wgrads/pallas_call | solution.py:523
  233.9 5.8 %mid.1 = (f32[256,1024]{1,0:T(8,128)}, bf16[256,1024]{1,0:T(8,128)(2,1)}, bf16[4,256,256]{2,1,0:T(8,128)(2,1)}, f32[8,1024]{1,0:T(8,128)}) custom-call(s32[1]{0:T(128)} %bitcast.sc, bf16[256,1024]{1,0:T(8,128)(2,1)} %get-tuple-element.138.a0, bf16[256,1024]{1,0:T(8,128)(2,1)} %copy-done.44, bf16[256,1024]{1,0:T(8,128)(2,1)} %copy-done.46, ...), custom_call_target="tpu_custom_call" | custom-call | flops 6000000000 | bytes 1048576 | tf_op jit(solution)/shard_map/mid/pallas_call | solution.py:582
  242.8 3.9 collective-permute-done.41
  250.4 21.6 %attn_bwd.2 = (bf16[1024,128]{1,0:T(8,128)(2,1)}, bf16[384,256]{1,0:T(8,128)(2,1)}, bf16[1024,256]{1,0:T(8,128)(2,1)}, f32[1024,256]{1,0:T(8,128)}, bf16[1024,256]{1,0:T(8,128)(2,1)}, /*index=5*/bf16[384,256]{1,0:T(8,128)(2,1)}) custom-call(s32[9]{0:T(128)} %pad_add_fusion.1.sc, bf16[1024,256]{1,0:T(8,128)(2,1)} %get-tuple-element.111.q_ref, ...), custom_call_target="tpu_custom_call" | custom-call | flops 22000001024 | bytes 1048576 | tf_op jit(solution)/shard_map/attn_bwd/pallas_call | solution.py:352
  272.0 21.6 %attn_bwd.3 = (bf16[1024,128]{1,0:T(8,128)(2,1)}, bf16[384,256]{1,0:T(8,128)(2,1)}, bf16[1024,256]{1,0:T(8,128)(2,1)}, f32[1024,256]{1,0:T(8,128)}, bf16[1024,256]{1,0:T(8,128)(2,1)}, /*index=5*/bf16[384,256]{1,0:T(8,128)(2,1)}) custom-call(s32[9]{0:T(128)} %pad_add_fusion.1.sc, bf16[1024,256]{1,0:T(8,128)(2,1)} %get-tuple-element.111.q_ref, ...), custom_call_target="tpu_custom_call" | custom-call | flops 22000001024 | bytes 1048576 | tf_op jit(solution)/shard_map/attn_bwd/pallas_call | solution.py:352
  293.6 6.8 %collective-permute-start.57 = (bf16[1024,256]{1,0:T(8,128)(2,1)}, bf16[1024,256]{1,0:T(8,128)(2,1)}, u32[]{:S(2)}, u32[]{:S(2)}) collective-permute-start(bf16[1024,256]{1,0:T(8,128)(2,1)} %get-tuple-element.181), channel_id=1, source_target_pairs={{0,4},{4,8},{8,12},{12,16},{16,20},{20,24},{24,28},{1,5},{5,9},{9,... | collective-permute-start | bytes 1572872 | tf_op jit(solution)/shard_map/ppermute | solution.py:38
  310.9 19.9 %collective-permute-done.55 = bf16[384,256]{1,0:T(8,128)(2,1)S(1)} collective-permute-done((bf16[384,256]{1,0:T(8,128)(2,1)}, bf16[384,256]{1,0:T(8,128)(2,1)S(1)}, u32[]{:S(2)}, u32[]{:S(2)}) %collective-permute-start.55) | collective-permute-done | bytes 196640 | tf_op jit(solution)/shard_map/ppermute | solution.py:38
  333.5 5.4 %collective-permute-start.54 = (bf16[384,256]{1,0:T(8,128)(2,1)S(1)}, bf16[384,256]{1,0:T(8,128)(2,1)S(1)}, u32[]{:S(2)}, u32[]{:S(2)}) collective-permute-start(bf16[384,256]{1,0:T(8,128)(2,1)S(1)} %copy-done.51), channel_id=1, source_target_pairs={{0,8},{4,12},{8,16},{12,20},{16,24},{20,28},{1,9},{5,13},{9,17},{1... | collective-permute-start | bytes 589832 | tf_op jit(solution)/shard_map/ppermute | solution.py:38
  344.4 22.3 %collective-permute-done.51 = bf16[384,256]{1,0:T(8,128)(2,1)S(1)} collective-permute-done((bf16[384,256]{1,0:T(8,128)(2,1)S(1)}, bf16[384,256]{1,0:T(8,128)(2,1)S(1)}, u32[]{:S(2)}, u32[]{:S(2)}) %collective-permute-start.51) | collective-permute-done | bytes 196640 | tf_op jit(solution)/shard_map/ppermute | solution.py:38
  371.0 10.1 %collective-permute-done.44.a2 = bf16[256,1024]{1,0:T(8,128)(2,1)S(1)} collective-permute-done((bf16[256,1024]{1,0:T(8,128)(2,1)S(1)}, bf16[256,1024]{1,0:T(8,128)(2,1)S(1)}, u32[]{:S(2)}, u32[]{:S(2)}) %collective-permute-start.44) | collective-permute-done | bytes 524320 | tf_op jit(solution)/shard_map/ppermute | solution.py:27
  382.1 5.1 %qkv_grad.1 = bf16[24,256,128]{2,1,0:T(8,128)(2,1)} custom-call(bf16[1024,256]{1,0:T(8,128)(2,1)} %copy-done.2, bf16[1024,256]{1,0:T(8,128)(2,1)} %pad_maximum_fusion.3.gk, bf16[1024,256]{1,0:T(8,128)(2,1)} %pad_maximum_fusion.4.gv, bf16[1024,1024]{1,0:T(8,128)(2,1)} %get-tuple-element.183.n1), custom_call_target="tpu_custom_call" | custom-call | flops 5000000000 | bytes 1048576 | tf_op jit(solution)/shard_map/qkv_grad/pallas_call | solution.py:661
  387.2 6.1 %gn1.1 = (bf16[256,1024]{1,0:T(8,128)(2,1)}, bf16[256,1024]{1,0:T(8,128)(2,1)}, bf16[256,1024]{1,0:T(8,128)(2,1)}, bf16[256,1024]{1,0:T(8,128)(2,1)}) custom-call(s32[1]{0:T(128)} %bitcast.sc, bf16[1024,128]{1,0:T(8,128)(2,1)} %get-tuple-element.171.gq0, bf16[1024,128]{1,0:T(8,128)(2,1)} %get-tuple-element.172.gq1, bf16[1024,256]{1,0:T(8,128)(2,1)} %pad_maximum_fusion.3.gk, ...), custom_call_target="tpu_custom_call" | custom-call | flops 6000000000 | bytes 1048576 | tf_op jit(solution)/shard_map/gn1/pallas_call | solution.py:634
  397.9 5.6 %norm_sums.1 = f32[8,1024]{1,0:T(8,128)} custom-call(s32[1]{0:T(128)} %bitcast.sc, bf16[256,1024]{1,0:T(8,128)(2,1)} %get-tuple-element.186.a0, bf16[256,1024]{1,0:T(8,128)(2,1)} %get-tuple-element.187.a1, bf16[256,1024]{1,0:T(8,128)(2,1)} %get-tuple-element.188.a2, bf16[256,1024]{1,0:T(8,128)(2,1)} %get-tuple-element.189.a3, bf16[1024,256]{1,0:T(8,128)(2,1)} %x0.7, ...), custom_call_target="tpu_custom_call" | custom-call | flops 5000000000 | bytes 1048576 | tf_op jit(solution)/shard_map/norm_sums/pallas_call | solution.py:694
  409.8 3.9 collective-permute-start.74
  440.6 12.0 %collective-permute-done.65 = bf16[2,2,3,256,128]{4,3,2,0,1:T(8,128)(2,1)S(1)} collective-permute-done((bf16[2,2,3,256,128]{4,3,2,0,1:T(8,128)(2,1)S(1)}, bf16[2,2,3,256,128]{4,3,2,0,1:T(8,128)(2,1)S(1)}, u32[]{:S(2)}, u32[]{:S(2)}) %collective-permute-start.65) | collective-permute-done | bytes 786464 | tf_op jit(solution)/shard_map/ppermute | solution.py:32
  459.6 4.3 collective-permute-done.66
  467.4 6.4 %collective-permute-done.67 = bf16[3,256,128]{2,1,0:T(8,128)(2,1)S(1)} collective-permute-done((bf16[3,256,128]{2,1,0:T(8,128)(2,1)S(1)}, bf16[3,256,128]{2,1,0:T(8,128)(2,1)S(1)}, u32[]{:S(2)}, u32[]{:S(2)}) %collective-permute-start.67) | collective-permute-done | bytes 196640 | tf_op jit(solution)/shard_map/ppermute | solution.py:32
  (350 shorter events, 154.1 us)
Async XLA Ops:
  7.2 186.7 %all-gather.2.cloned.1.call-start = ((), (), s32[]{:S(2)}) async-start(), calls=%async_computation.1 | async-start | bytes 4718592 | tf_op jit(solution)/shard_map/all_gather | solution.py:951
  7.2 52.7 %collective-permute-start = (bf16[1024,256]{1,0:T(8,128)(2,1)}, bf16[1024,256]{1,0:T(8,128)(2,1)}, u32[]{:S(2)}, u32[]{:S(2)}) collective-permute-start(bf16[1024,256]{1,0:T(8,128)(2,1)} %x0.7), channel_id=1, source_target_pairs={{0,1},{1,0},{2,3},{3,2},{4,5},{5,4},{6,7},{7,6},{8,9},{9,8},{10,11... | collective-permute-start | bytes 1572872 | tf_op jit(solution)/shard_map/ppermute | solution.py:27
  7.8 41.0 %collective-permute-start.1 = (bf16[1024,256]{1,0:T(8,128)(2,1)}, bf16[1024,256]{1,0:T(8,128)(2,1)}, u32[]{:S(2)}, u32[]{:S(2)}) collective-permute-start(bf16[1024,256]{1,0:T(8,128)(2,1)} %x0.7), channel_id=1, source_target_pairs={{0,2},{1,3},{2,0},{3,1},{4,6},{5,7},{6,4},{7,5},{8,10},{9,11},{10,... | collective-permute-start | bytes 1572872 | tf_op jit(solution)/shard_map/ppermute | solution.py:27
  26.1 20.9 %collective-permute-start.6 = (bf16[256,512]{1,0:T(8,128)(2,1)S(1)}, bf16[256,512]{1,0:T(8,128)(2,1)S(1)}, u32[]{:S(2)}, u32[]{:S(2)}) collective-permute-start(bf16[256,512]{1,0:T(8,128)(2,1)S(1)} %constant_dynamic-update-slice_fusion), channel_id=1, source_target_pairs={{0,16},{4,20},{8,24},{12,28},{16,0},{20,4},{24,8},{28,12},{1,17},{... | collective-permute-start | bytes 786440 | tf_op jit(solution)/shard_map/ppermute | solution.py:32
  47.0 52.2 %collective-permute-start.25 = (bf16[256,256]{1,0:T(8,128)(2,1)S(1)}, bf16[256,256]{1,0:T(8,128)(2,1)S(1)}, u32[]{:S(2)}, u32[]{:S(2)}) collective-permute-start(bf16[256,256]{1,0:T(8,128)(2,1)S(1)} %get-tuple-element.297), channel_id=1, source_target_pairs={{0,2},{1,3},{2,0},{3,1},{4,6},{5,7},{6,4},{7,5},{8,10},{9,11},{10,... | collective-permute-start | bytes 393224 | tf_op jit(solution)/shard_map/ppermute | solution.py:27
  69.1 28.2 %collective-permute-start.18 = (bf16[1024,256]{1,0:T(8,128)(2,1)}, bf16[1024,256]{1,0:T(8,128)(2,1)S(1)}, u32[]{:S(2)}, u32[]{:S(2)}) collective-permute-start(bf16[1024,256]{1,0:T(8,128)(2,1)} %get-tuple-element.117.refs_2_), channel_id=1, source_target_pairs={{0,4},{4,8},{8,12},{12,16},{16,20},{20,24},{24,28},{1,5},{5,9},{9,... | collective-permute-start | bytes 1572872 | tf_op jit(solution)/shard_map/ppermute | solution.py:38
  71.3 26.0 %collective-permute-start.19 = (bf16[1024,256]{1,0:T(8,128)(2,1)}, bf16[1024,256]{1,0:T(8,128)(2,1)S(1)}, u32[]{:S(2)}, u32[]{:S(2)}) collective-permute-start(bf16[1024,256]{1,0:T(8,128)(2,1)} %get-tuple-element.117.refs_2_), channel_id=1, source_target_pairs={{4,0},{8,4},{12,8},{16,12},{20,16},{24,20},{28,24},{5,1},{9,5},{13... | collective-permute-start | bytes 1572872 | tf_op jit(solution)/shard_map/ppermute | solution.py:38
  97.3 377.3 %reduce-scatter.2.cloned.1.call-start = ((), (), s32[]{:S(2)}) async-start(), calls=%async_computation.2 | async-start | bytes 4718592 | tf_op jit(solution)/shard_map/reduce_scatter | solution.py:976
  99.5 18.3 %collective-permute-start.28 = (bf16[256,1024]{1,0:T(8,128)(2,1)S(1)}, bf16[256,1024]{1,0:T(8,128)(2,1)S(1)}, u32[]{:S(2)}, u32[]{:S(2)}) collective-permute-start(bf16[256,1024]{1,0:T(8,128)(2,1)S(1)} %multiply_convert_fusion.g0), channel_id=1, source_target_pairs={{0,2},{1,3},{2,0},{3,1},{4,6},{5,7},{6,4},{7,5},{8,10},{9,11},{10,... | collective-permute-start | bytes 1572872 | tf_op jit(solution)/shard_map/ppermute | solution.py:27
  102.4 33.9 %collective-permute-start.14 = (bf16[1024,256]{1,0:T(8,128)(2,1)S(1)}, bf16[1024,256]{1,0:T(8,128)(2,1)S(1)}, u32[]{:S(2)}, u32[]{:S(2)}) collective-permute-start(bf16[1024,256]{1,0:T(8,128)(2,1)S(1)} %copy-done.15), channel_id=1, source_target_pairs={{0,4},{4,8},{8,12},{12,16},{16,20},{20,24},{24,28},{1,5},{5,9},{9,... | collective-permute-start | bytes 1572872 | tf_op jit(solution)/shard_map/ppermute | solution.py:38
  103.7 33.1 %collective-permute-start.15 = (bf16[1024,256]{1,0:T(8,128)(2,1)S(1)}, bf16[1024,256]{1,0:T(8,128)(2,1)S(1)}, u32[]{:S(2)}, u32[]{:S(2)}) collective-permute-start(bf16[1024,256]{1,0:T(8,128)(2,1)S(1)} %copy-done.15), channel_id=1, source_target_pairs={{4,0},{8,4},{12,8},{16,12},{20,16},{24,20},{28,24},{5,1},{9,5},{13... | collective-permute-start | bytes 1572872 | tf_op jit(solution)/shard_map/ppermute | solution.py:38
  105.0 30.5 %collective-permute-start.13 = (bf16[384,256]{1,0:T(8,128)(2,1)S(1)}, bf16[384,256]{1,0:T(8,128)(2,1)S(1)}, u32[]{:S(2)}, u32[]{:S(2)}) collective-permute-start(bf16[384,256]{1,0:T(8,128)(2,1)S(1)} %get-tuple-element.302), channel_id=1, source_target_pairs={{0,8},{4,12},{8,16},{12,20},{16,24},{20,28},{1,9},{5,13},{9,17},{1... | collective-permute-start | bytes 589832 | tf_op jit(solution)/shard_map/ppermute | solution.py:38
  116.3 19.3 %collective-permute-start.16 = (bf16[384,256]{1,0:T(8,128)(2,1)S(1)}, bf16[384,256]{1,0:T(8,128)(2,1)S(1)}, u32[]{:S(2)}, u32[]{:S(2)}) collective-permute-start(bf16[384,256]{1,0:T(8,128)(2,1)S(1)} %get-tuple-element.301), channel_id=1, source_target_pairs={{8,0},{12,4},{16,8},{20,12},{24,16},{28,20},{9,1},{13,5},{17,9},{2... | collective-permute-start | bytes 589832 | tf_op jit(solution)/shard_map/ppermute | solution.py:38
  117.8 18.5 %collective-permute-start.22 = (bf16[256,1024]{1,0:T(8,128)(2,1)}, bf16[256,1024]{1,0:T(8,128)(2,1)S(1)}, u32[]{:S(2)}, u32[]{:S(2)}) collective-permute-start(bf16[256,1024]{1,0:T(8,128)(2,1)} %get-tuple-element.125.w0), channel_id=1, source_target_pairs={{0,2},{1,3},{2,0},{3,1},{4,6},{5,7},{6,4},{7,5},{8,10},{9,11},{10,... | collective-permute-start | bytes 1572872 | tf_op jit(solution)/shard_map/ppermute | solution.py:27
  135.6 19.2 %collective-permute-start.27 = (bf16[256,1024]{1,0:T(8,128)(2,1)S(1)}, bf16[256,1024]{1,0:T(8,128)(2,1)S(1)}, u32[]{:S(2)}, u32[]{:S(2)}) collective-permute-start(bf16[256,1024]{1,0:T(8,128)(2,1)S(1)} %multiply_convert_fusion.g0), channel_id=1, source_target_pairs={{0,1},{1,0},{2,3},{3,2},{4,5},{5,4},{6,7},{7,6},{8,9},{9,8},{10,11... | collective-permute-start | bytes 1572872 | tf_op jit(solution)/shard_map/ppermute | solution.py:27
  135.7 19.1 %collective-permute-start.29 = (bf16[256,1024]{1,0:T(8,128)(2,1)S(1)}, bf16[256,1024]{1,0:T(8,128)(2,1)S(1)}, u32[]{:S(2)}, u32[]{:S(2)}) collective-permute-start(bf16[256,1024]{1,0:T(8,128)(2,1)S(1)} %collective-permute-done.28.g0.g2), channel_id=1, source_target_pairs={{0,1},{1,0},{2,3},{3,2},{4,5},{5,4},{6,7},{7,6},{8,9},{9,8},{10,11... | collective-permute-start | bytes 1572872 | tf_op jit(solution)/shard_map/ppermute | solution.py:27
  136.2 18.6 %collective-permute-start.21 = (bf16[256,1024]{1,0:T(8,128)(2,1)S(1)}, bf16[256,1024]{1,0:T(8,128)(2,1)S(1)}, u32[]{:S(2)}, u32[]{:S(2)}) collective-permute-start(bf16[256,1024]{1,0:T(8,128)(2,1)S(1)} %copy-done.28), channel_id=1, source_target_pairs={{0,1},{1,0},{2,3},{3,2},{4,5},{5,4},{6,7},{7,6},{8,9},{9,8},{10,11... | collective-permute-start | bytes 1572872 | tf_op jit(solution)/shard_map/ppermute | solution.py:27
  136.3 18.5 %collective-permute-start.23 = (bf16[256,1024]{1,0:T(8,128)(2,1)S(1)}, bf16[256,1024]{1,0:T(8,128)(2,1)S(1)}, u32[]{:S(2)}, u32[]{:S(2)}) collective-permute-start(bf16[256,1024]{1,0:T(8,128)(2,1)S(1)} %collective-permute-done.22.w2), channel_id=1, source_target_pairs={{0,1},{1,0},{2,3},{3,2},{4,5},{5,4},{6,7},{7,6},{8,9},{9,8},{10,11... | collective-permute-start | bytes 1572872 | tf_op jit(solution)/shard_map/ppermute | solution.py:27
  293.6 38.5 %collective-permute-start.57 = (bf16[1024,256]{1,0:T(8,128)(2,1)}, bf16[1024,256]{1,0:T(8,128)(2,1)}, u32[]{:S(2)}, u32[]{:S(2)}) collective-permute-start(bf16[1024,256]{1,0:T(8,128)(2,1)} %get-tuple-element.181), channel_id=1, source_target_pairs={{0,4},{4,8},{8,12},{12,16},{16,20},{20,24},{24,28},{1,5},{5,9},{9,... | collective-permute-start | bytes 1572872 | tf_op jit(solution)/shard_map/ppermute | solution.py:38
  300.4 33.1 %collective-permute-start.56 = (bf16[1024,256]{1,0:T(8,128)(2,1)}, bf16[1024,256]{1,0:T(8,128)(2,1)}, u32[]{:S(2)}, u32[]{:S(2)}) collective-permute-start(bf16[1024,256]{1,0:T(8,128)(2,1)} %get-tuple-element.180), channel_id=1, source_target_pairs={{4,0},{8,4},{12,8},{16,12},{20,16},{24,20},{28,24},{5,1},{9,5},{13... | collective-permute-start | bytes 1572872 | tf_op jit(solution)/shard_map/ppermute | solution.py:38
  301.7 38.7 %collective-permute-start.43 = (bf16[256,1024]{1,0:T(8,128)(2,1)}, bf16[256,1024]{1,0:T(8,128)(2,1)S(1)}, u32[]{:S(2)}, u32[]{:S(2)}) collective-permute-start(bf16[256,1024]{1,0:T(8,128)(2,1)} %get-tuple-element.161), channel_id=1, source_target_pairs={{0,1},{1,0},{2,3},{3,2},{4,5},{5,4},{6,7},{7,6},{8,9},{9,8},{10,11... | collective-permute-start | bytes 1572872 | tf_op jit(solution)/shard_map/ppermute | solution.py:27
  305.0 25.8 %collective-permute-start.55 = (bf16[384,256]{1,0:T(8,128)(2,1)}, bf16[384,256]{1,0:T(8,128)(2,1)S(1)}, u32[]{:S(2)}, u32[]{:S(2)}) collective-permute-start(bf16[384,256]{1,0:T(8,128)(2,1)} %get-tuple-element.179), channel_id=1, source_target_pairs={{8,0},{12,4},{16,8},{20,12},{24,16},{28,20},{9,1},{13,5},{17,9},{2... | collective-permute-start | bytes 589832 | tf_op jit(solution)/shard_map/ppermute | solution.py:38
  310.1 56.7 %collective-permute-start.49 = (bf16[256,1024]{1,0:T(8,128)(2,1)S(1)}, bf16[256,1024]{1,0:T(8,128)(2,1)S(1)}, u32[]{:S(2)}, u32[]{:S(2)}) collective-permute-start(bf16[256,1024]{1,0:T(8,128)(2,1)S(1)} %copy-done.6), channel_id=1, source_target_pairs={{0,2},{1,3},{2,0},{3,1},{4,6},{5,7},{6,4},{7,5},{8,10},{9,11},{10,... | collective-permute-start | bytes 1572872 | tf_op jit(solution)/shard_map/ppermute | solution.py:27
  330.8 37.8 %collective-permute-start.53 = (bf16[1024,256]{1,0:T(8,128)(2,1)}, bf16[1024,256]{1,0:T(8,128)(2,1)S(1)}, u32[]{:S(2)}, u32[]{:S(2)}) collective-permute-start(bf16[1024,256]{1,0:T(8,128)(2,1)} %get-tuple-element.176), channel_id=1, source_target_pairs={{0,4},{4,8},{8,12},{12,16},{16,20},{20,24},{24,28},{1,5},{5,9},{9,... | collective-permute-start | bytes 1572872 | tf_op jit(solution)/shard_map/ppermute | solution.py:38
  332.1 36.6 %collective-permute-start.52 = (bf16[1024,256]{1,0:T(8,128)(2,1)}, bf16[1024,256]{1,0:T(8,128)(2,1)S(1)}, u32[]{:S(2)}, u32[]{:S(2)}) collective-permute-start(bf16[1024,256]{1,0:T(8,128)(2,1)} %get-tuple-element.175), channel_id=1, source_target_pairs={{4,0},{8,4},{12,8},{16,12},{20,16},{24,20},{28,24},{5,1},{9,5},{13... | collective-permute-start | bytes 1572872 | tf_op jit(solution)/shard_map/ppermute | solution.py:38
  340.4 26.3 %collective-permute-start.51 = (bf16[384,256]{1,0:T(8,128)(2,1)S(1)}, bf16[384,256]{1,0:T(8,128)(2,1)S(1)}, u32[]{:S(2)}, u32[]{:S(2)}) collective-permute-start(bf16[384,256]{1,0:T(8,128)(2,1)S(1)} %copy-done.50), channel_id=1, source_target_pairs={{8,0},{12,4},{16,8},{20,12},{24,16},{28,20},{9,1},{13,5},{17,9},{2... | collective-permute-start | bytes 589832 | tf_op jit(solution)/shard_map/ppermute | solution.py:38
  344.4 36.7 %collective-permute-start.48 = (bf16[256,1024]{1,0:T(8,128)(2,1)S(1)}, bf16[256,1024]{1,0:T(8,128)(2,1)S(1)}, u32[]{:S(2)}, u32[]{:S(2)}) collective-permute-start(bf16[256,1024]{1,0:T(8,128)(2,1)S(1)} %copy-done.6), channel_id=1, source_target_pairs={{0,1},{1,0},{2,3},{3,2},{4,5},{5,4},{6,7},{7,6},{8,9},{9,8},{10,11... | collective-permute-start | bytes 1572872 | tf_op jit(solution)/shard_map/ppermute | solution.py:27
  393.3 60.4 %collective-permute-start.59 = (bf16[256,1024]{1,0:T(8,128)(2,1)}, bf16[256,1024]{1,0:T(8,128)(2,1)}, u32[]{:S(2)}, u32[]{:S(2)}) collective-permute-start(bf16[256,1024]{1,0:T(8,128)(2,1)} %get-tuple-element.187.a1), channel_id=1, source_target_pairs={{0,1},{1,0},{2,3},{3,2},{4,5},{5,4},{6,7},{7,6},{8,9},{9,8},{10,11... | collective-permute-start | bytes 1572872 | tf_op jit(solution)/shard_map/ppermute | solution.py:27
  393.3 45.5 %collective-permute-start.60 = (bf16[256,1024]{1,0:T(8,128)(2,1)}, bf16[256,1024]{1,0:T(8,128)(2,1)S(1)}, u32[]{:S(2)}, u32[]{:S(2)}) collective-permute-start(bf16[256,1024]{1,0:T(8,128)(2,1)} %get-tuple-element.189.a3), channel_id=1, source_target_pairs={{0,1},{1,0},{2,3},{3,2},{4,5},{5,4},{6,7},{7,6},{8,9},{9,8},{10,11... | collective-permute-start | bytes 1572872 | tf_op jit(solution)/shard_map/ppermute | solution.py:27
  407.4 23.5 %collective-permute-start.45 = (bf16[256,256]{1,0:T(8,128)(2,1)}, bf16[256,256]{1,0:T(8,128)(2,1)}, u32[]{:S(2)}, u32[]{:S(2)}) collective-permute-start(bf16[256,256]{1,0:T(8,128)(2,1)} %get-tuple-element.165), channel_id=1, source_target_pairs={{0,3},{1,2},{2,1},{3,0},{4,7},{5,6},{6,5},{7,4},{8,11},{9,10},{10,... | collective-permute-start | bytes 393224 | tf_op jit(solution)/shard_map/ppermute | solution.py:27
  409.4 23.7 %collective-permute-start.46 = (bf16[256,256]{1,0:T(8,128)(2,1)}, bf16[256,256]{1,0:T(8,128)(2,1)}, u32[]{:S(2)}, u32[]{:S(2)}) collective-permute-start(bf16[256,256]{1,0:T(8,128)(2,1)} %get-tuple-element.166), channel_id=1, source_target_pairs={{0,2},{1,3},{2,0},{3,1},{4,6},{5,7},{6,4},{7,5},{8,10},{9,11},{10,... | collective-permute-start | bytes 393224 | tf_op jit(solution)/shard_map/ppermute | solution.py:27
  430.9 21.7 %collective-permute-start.65 = (bf16[2,2,3,256,128]{4,3,2,0,1:T(8,128)(2,1)S(1)}, bf16[2,2,3,256,128]{4,3,2,0,1:T(8,128)(2,1)S(1)}, u32[]{:S(2)}, u32[]{:S(2)}) collective-permute-start(bf16[2,2,3,256,128]{4,3,2,0,1:T(8,128)(2,1)S(1)} %copy_bitcast_fusion), channel_id=1, source_target_pairs={{0,8},{4,12},{8,0},{12,4},{16,24},{20,28},{24,16},{28,20},{1,9},{5... | collective-permute-start | bytes 2359304 | tf_op jit(solution)/shard_map/ppermute | solution.py:32
  (102 other events, 1162.3 us)
Sparse Core Ops, SparseCore 0:
  97.5 96.4 all-gather.1
  307.2 105.1 reduce-scatter.1

commit v3 on v2

--- a/solution.py
+++ b/solution.py
@@ -1005,11 +1005,17 @@
             o0, o1, o2, o3, sums_out = out_call(sc_t, seconds, cots, middle, vec)
             block_output = placed(swap4([o0, o1, o2, o3]), t, 0)
         grad_q.append(got[0])
+        backs = [
+            passed_along(got[1 + k], -offset)
+            for k, offset in enumerate(offsets_of)
+            if offset != 0
+        ]
+        if pair == 1:
+            *backs, block_output = after(*backs, block_output)
         total = got[1 + reach]
-        for k, (offset, count) in enumerate(zip(offsets_of, counts)):
-            if offset == 0:
-                continue
-            back = passed_along(got[1 + k], -offset).astype(F32)
+        others_of = [(o, c) for o, c in zip(offsets_of, counts) if o != 0]
+        for back, (offset, count) in zip(backs, others_of):
+            back = back.astype(F32)
             if count < row_count:
                 gap = row_count - count
                 ends = ((gap, 0), (0, 0)) if offset > 0 else ((0, gap), (0, 0))
@@ -1038,8 +1044,6 @@
     pieces = gn1_call(sc_t, grad_q[0], grad_q[1], gk, gv, w_full)
     sums_last = nsum_call(sc_t, pieces, xs)
     i0, i1, i2, i3 = last_call(sc_t, reduce4(pieces), xs, grad_middle, vec)
-    input_grad = placed(swap4([i0, i1, i2, i3]), t, 0)
-
     rows8 = jnp.concatenate([sums_last[0:2], sums_mid[0:4], sums_out[0:2]], axis=0)
     cut = [lax.dynamic_slice_in_dim(rows8, (t ^ r) * fw, fw, 1) for r in range(4)]
     got = swap4(cut)
@@ -1052,6 +1056,8 @@
             fb_a[0] + fb_b[0],
         ]
     ).reshape(-1, 128)
+    flat, i0, i1, i2, i3 = after(flat, i0, i1, i2, i3)
+    input_grad = placed(swap4([i0, i1, i2, i3]), t, 0)
     if n_seq == 8:
         for bits in (2, 1, 4):
             flat = flat + ps(flat, bits)

time: 487 us -> 443 us (0.910)
  waiting for transfers between devices: 177 us -> 129 us
    ppermute x16, waiting for transfers between devices: 56.3 us -> 25.1 us  [passed_along(): return lax.ppermute(block, 'seq', route)]
    ppermute x16, waiting for transfers between devices: 59.2 us -> 39.2 us  [ps(): return lax.ppermute(value, 'seq', pairs)]
    unnamed x117 -> x127, local copies, waits for them, and re-layouts: 11.4 us -> 10.7 us
  transfers between devices with their start and end apart: 79 -> 79, of which waited for: 33 -> 32; matrix products, arithmetic and copies ran while one was open for 6% -> 7% of each run, Pallas kernels for 16% -> 28%
where the time goes in v3:
time: 443 us; the launch traced here: 441 us
  Pallas kernels  148 us (33%)
  waiting for transfers between devices  129 us (29%)
  starting transfers between devices  107 us (24%)
  local copies, waits for them, and re-layouts  22.9 us (5%)
  other arithmetic  17 us (4%)
  between operations  15.4 us (3%)
    ppermute x45, waiting for transfers between devices, px(): return lax.ppermute(value, 'tensor', pairs)  57.7 us
    ppermute x16, starting transfers between devices, passed_along(): return lax.ppermute(block, 'seq', route)  56.1 us
    pallas_call x2, Pallas kernels, bwd_call(): pl.pallas_call(functools.partial(bwd_kernel, offsets, counts), grid_spec=...  43.5 us
    ppermute x16, waiting for transfers between devices, ps(): return lax.ppermute(value, 'seq', pairs)  39.2 us
    pallas_call x2, Pallas kernels, fwd_call(): pl.pallas_call(functools.partial(fwd_kernel, offsets, counts), grid_spec=...  33.8 us
    ppermute x45, starting transfers between devices, px(): return lax.ppermute(value, 'tensor', pairs)  27.2 us
    ppermute x16, waiting for transfers between devices, passed_along(): return lax.ppermute(block, 'seq', route)  25.1 us
    ppermute x16, starting transfers between devices, ps(): return lax.ppermute(value, 'seq', pairs)  24 us
  transfers between devices with their start and end apart: 79, of which 32 were waited for; matrix products, arithmetic and copies ran while one was open for 7% of the time, Pallas kernels for 28%

profile of v3, /device:TPU:0, one launch (start us, length us, event | category | flops | bytes accessed | tf_op | source)
XLA Modules:
  0.0 440.6 jit_solution(4471211410354650050)
XLA Ops:
  15.2 7.7 %collective-permute-done.10 = f32[8,256]{1,0:T(8,128)S(1)} collective-permute-done((f32[8,256]{1,0:T(8,128)S(1)}, f32[8,256]{1,0:T(8,128)S(1)}, u32[]{:S(2)}, u32[]{:S(2)}) %collective-permute-start.10) | collective-permute-done | bytes 8224 | tf_op jit(solution)/shard_map/ppermute | solution.py:27
  31.7 3.8 collective-permute-start.8
  39.1 7.9 %collective-permute-done.6 = bf16[256,512]{1,0:T(8,128)(2,1)S(1)} collective-permute-done((bf16[256,512]{1,0:T(8,128)(2,1)S(1)}, bf16[256,512]{1,0:T(8,128)(2,1)S(1)}, u32[]{:S(2)}, u32[]{:S(2)}) %collective-permute-start.6) | collective-permute-done | bytes 262176 | tf_op jit(solution)/shard_map/ppermute | solution.py:32
  50.6 6.6 %collective-permute-done.7 = bf16[256,512]{1,0:T(8,128)(2,1)S(1)} collective-permute-done((bf16[256,512]{1,0:T(8,128)(2,1)S(1)}, bf16[256,512]{1,0:T(8,128)(2,1)S(1)}, u32[]{:S(2)}, u32[]{:S(2)}) %collective-permute-start.7) | collective-permute-done | bytes 262176 | tf_op jit(solution)/shard_map/ppermute | solution.py:32
  61.5 7.6 %qkv.1 = (bf16[1024,1024]{1,0:T(8,128)(2,1)}, bf16[1024,256]{1,0:T(8,128)(2,1)}, bf16[1024,256]{1,0:T(8,128)(2,1)}, bf16[1024,256]{1,0:T(8,128)(2,1)}, bf16[256,...) custom-call(s32[1]{0:T(128)} %bitcast.sc, bf16[1024,256]{1,0:T(8,128)(2,1)} %x0.7, ...), custom_call_target="tpu_custom_call" | custom-call | flops 7000000000 | bytes 1048576 | tf_op jit(solution)/shard_map/qkv/pallas_call | solution.py:137
  73.7 11.6 %collective-permute-start.17 = (bf16[384,256]{1,0:T(8,128)(2,1)S(1)}, bf16[384,256]{1,0:T(8,128)(2,1)S(1)}, u32[]{:S(2)}, u32[]{:S(2)}) collective-permute-start(bf16[384,256]{1,0:T(8,128)(2,1)S(1)} %get-tuple-element.320), channel_id=1, source_target_pairs={{0,8},{4,12},{8,16},{12,20},{16,24},{20,28},{1,9},{5,13},{9,17},{1... | collective-permute-start | bytes 589832 | tf_op jit(solution)/shard_map/ppermute | solution.py:38
  88.5 8.7 %collective-permute-done.20.refs_4_ = bf16[384,256]{1,0:T(8,128)(2,1)S(1)} collective-permute-done((bf16[384,256]{1,0:T(8,128)(2,1)S(1)}, bf16[384,256]{1,0:T(8,128)(2,1)S(1)}, u32[]{:S(2)}, u32[]{:S(2)}) %collective-permute-start.20) | collective-permute-done | bytes 196640 | tf_op jit(solution)/shard_map/ppermute | solution.py:38
  105.6 10.7 %collective-permute-start.13 = (bf16[384,256]{1,0:T(8,128)(2,1)S(1)}, bf16[384,256]{1,0:T(8,128)(2,1)S(1)}, u32[]{:S(2)}, u32[]{:S(2)}) collective-permute-start(bf16[384,256]{1,0:T(8,128)(2,1)S(1)} %get-tuple-element.322), channel_id=1, source_target_pairs={{0,8},{4,12},{8,16},{12,20},{16,24},{20,28},{1,9},{5,13},{9,17},{1... | collective-permute-start | bytes 589832 | tf_op jit(solution)/shard_map/ppermute | solution.py:38
  118.4 16.9 %attn_fwd.3 = (bf16[1024,128]{1,0:T(8,128)(2,1)}, f32[8,1024]{1,0:T(8,128)}) custom-call(s32[9]{0:T(128)} %pad_add_fusion.1.sc, bf16[1024,256]{1,0:T(8,128)(2,1)} %get-tuple-element.121.q_ref, s32[8,1024]{1,0:T(8,128)} %add_add_fusion.se_ref, bf16[384,256]{1,0:T(8,128)(2,1)} %copy-done.49, bf16[1024,256]{1,0:T(8,128)(2,1)} %copy-done.26, ...), custom_call_target="tpu_custom_call" | custom-call | flops 16999999488 | bytes 1048576 | tf_op jit(solution)/shard_map/attn_fwd/pallas_call | solution.py:256
  137.7 16.9 %attn_fwd.2 = (bf16[1024,128]{1,0:T(8,128)(2,1)}, f32[8,1024]{1,0:T(8,128)}) custom-call(s32[9]{0:T(128)} %pad_add_fusion.1.sc, bf16[1024,256]{1,0:T(8,128)(2,1)} %get-tuple-element.121.q_ref, s32[8,1024]{1,0:T(8,128)} %add_add_fusion.se_ref, bf16[384,256]{1,0:T(8,128)(2,1)} %copy-done.51, bf16[1024,256]{1,0:T(8,128)(2,1)} %copy-done.29, ...), custom_call_target="tpu_custom_call" | custom-call | flops 16999999488 | bytes 1048576 | tf_op jit(solution)/shard_map/attn_fwd/pallas_call | solution.py:256
  158.6 4.5 %collective-permute-done.31.c2 = bf16[256,256]{1,0:T(8,128)(2,1)S(1)} collective-permute-done((bf16[256,256]{1,0:T(8,128)(2,1)S(1)}, bf16[256,256]{1,0:T(8,128)(2,1)S(1)}, u32[]{:S(2)}, u32[]{:S(2)}) %collective-permute-start.31) | collective-permute-done | bytes 131104 | tf_op jit(solution)/shard_map/ppermute | solution.py:27
  165.6 4.2 proj.1
  171.4 13.2 %collective-permute-done.33.n0.n2 = bf16[256,1024]{1,0:T(8,128)(2,1)S(1)} collective-permute-done((bf16[256,1024]{1,0:T(8,128)(2,1)}, bf16[256,1024]{1,0:T(8,128)(2,1)S(1)}, u32[]{:S(2)}, u32[]{:S(2)}) %collective-permute-start.33) | collective-permute-done | bytes 524320 | tf_op jit(solution)/shard_map/ppermute | solution.py:27
  186.5 7.3 %all-gather.2.cloned.1.call-done.fc1.fc2 = bf16[2048,1024]{1,0:T(8,128)(2,1)} async-done(((bf16[2048,128]{1,0:T(8,128)(2,1)}), bf16[2048,1024]{1,0:T(8,128)(2,1)}) %all-gather.2.cloned.1.call-update) | async-done | bytes 4194320 | tf_op jit(solution)/shard_map/all_gather | solution.py:951
  193.8 10.2 %mlp.2 = (bf16[512,1024]{1,0:T(8,128)(2,1)}, bf16[512,1024]{1,0:T(8,128)(2,1)}, bf16[256,1024]{1,0:T(8,128)(2,1)}, bf16[256,1024]{1,0:T(8,128)(2,1)}, bf16[256,1...) custom-call(bf16[256,1024]{1,0:T(8,128)(2,1)} %copy-done.41, bf16[256,1024]{1,0:T(8,128)(2,1)} %copy-done.42, ...), custom_call_target="tpu_custom_call" | custom-call | flops 10000000000 | bytes 1048576 | tf_op jit(solution)/shard_map/mlp/pallas_call | solution.py:481
  208.2 10.1 %mlp.3 = (bf16[512,1024]{1,0:T(8,128)(2,1)}, bf16[512,1024]{1,0:T(8,128)(2,1)}, bf16[256,1024]{1,0:T(8,128)(2,1)}, bf16[256,1024]{1,0:T(8,128)(2,1)}, bf16[256,1...) custom-call(bf16[256,1024]{1,0:T(8,128)(2,1)} %get-tuple-element.139.n0, ...), custom_call_target="tpu_custom_call" | custom-call | flops 10000000000 | bytes 1048576 | tf_op jit(solution)/shard_map/mlp/pallas_call | solution.py:481
  220.0 9.3 %wgrads.1 = bf16[1024,2048]{1,0:T(8,128)(2,1)} custom-call(bf16[256,1024]{1,0:T(8,128)(2,1)} %get-tuple-element.139.n0, bf16[256,1024]{1,0:T(8,128)(2,1)} %copy-done.43, bf16[256,1024]{1,0:T(8,128)(2,1)} %copy-done.41, bf16[256,1024]{1,0:T(8,128)(2,1)} %copy-done.42, bf16[256,1024]{1,0:T(8,128)(2,1)} %copy-done.8, bf16[256,1024]{1,0:T(8,128)(2,1)} %copy-done.37, ...), custom_call_target="tpu_custom_call" | custom-call | flops 8999999488 | bytes 1048576 | tf_op jit(solution)/shard_map/wgrads/pallas_call | solution.py:523
  233.6 5.8 %mid.1 = (f32[256,1024]{1,0:T(8,128)}, bf16[256,1024]{1,0:T(8,128)(2,1)}, bf16[4,256,256]{2,1,0:T(8,128)(2,1)}, f32[8,1024]{1,0:T(8,128)}) custom-call(s32[1]{0:T(128)} %bitcast.sc, bf16[256,1024]{1,0:T(8,128)(2,1)} %get-tuple-element.148.a0, bf16[256,1024]{1,0:T(8,128)(2,1)} %copy-done.47, bf16[256,1024]{1,0:T(8,128)(2,1)} %copy-done.48, ...), custom_call_target="tpu_custom_call" | custom-call | flops 6000000000 | bytes 1048576 | tf_op jit(solution)/shard_map/mid/pallas_call | solution.py:582
  250.2 21.7 %attn_bwd.2 = (bf16[1024,128]{1,0:T(8,128)(2,1)}, bf16[384,256]{1,0:T(8,128)(2,1)}, bf16[1024,256]{1,0:T(8,128)(2,1)}, f32[1024,256]{1,0:T(8,128)}, bf16[1024,256]{1,0:T(8,128)(2,1)}, /*index=5*/bf16[384,256]{1,0:T(8,128)(2,1)}) custom-call(s32[9]{0:T(128)} %pad_add_fusion.1.sc, bf16[1024,256]{1,0:T(8,128)(2,1)} %get-tuple-element.121.q_ref, ...), custom_call_target="tpu_custom_call" | custom-call | flops 22000001024 | bytes 1048576 | tf_op jit(solution)/shard_map/attn_bwd/pallas_call | solution.py:352
  272.0 4.7 %collective-permute-start.57 = (bf16[1024,256]{1,0:T(8,128)(2,1)}, bf16[1024,256]{1,0:T(8,128)(2,1)S(1)}, u32[]{:S(2)}, u32[]{:S(2)}) collective-permute-start(bf16[1024,256]{1,0:T(8,128)(2,1)} %get-tuple-element.191), channel_id=1, source_target_pairs={{0,4},{4,8},{8,12},{12,16},{16,20},{20,24},{24,28},{1,5},{5,9},{9,... | collective-permute-start | bytes 1572872 | tf_op jit(solution)/shard_map/ppermute | solution.py:38
  278.0 4.0 collective-permute-start.58
  283.0 21.8 %attn_bwd.3 = (bf16[1024,128]{1,0:T(8,128)(2,1)}, bf16[384,256]{1,0:T(8,128)(2,1)}, bf16[1024,256]{1,0:T(8,128)(2,1)}, f32[1024,256]{1,0:T(8,128)}, bf16[1024,256]{1,0:T(8,128)(2,1)}, /*index=5*/bf16[384,256]{1,0:T(8,128)(2,1)}) custom-call(s32[9]{0:T(128)} %pad_add_fusion.1.sc, bf16[1024,256]{1,0:T(8,128)(2,1)} %get-tuple-element.121.q_ref, ...), custom_call_target="tpu_custom_call" | custom-call | flops 22000001024 | bytes 1048576 | tf_op jit(solution)/shard_map/attn_bwd/pallas_call | solution.py:352
  306.6 6.6 %collective-permute-done.55 = bf16[384,256]{1,0:T(8,128)(2,1)S(1)} collective-permute-done((bf16[384,256]{1,0:T(8,128)(2,1)S(1)}, bf16[384,256]{1,0:T(8,128)(2,1)S(1)}, u32[]{:S(2)}, u32[]{:S(2)}) %collective-permute-start.55) | collective-permute-done | bytes 196640 | tf_op jit(solution)/shard_map/ppermute | solution.py:38
  316.5 5.3 %collective-permute-start.44 = (bf16[1024,256]{1,0:T(8,128)(2,1)}, bf16[1024,256]{1,0:T(8,128)(2,1)}, u32[]{:S(2)}, u32[]{:S(2)}) collective-permute-start(bf16[1024,256]{1,0:T(8,128)(2,1)} %get-tuple-element.169), channel_id=1, source_target_pairs={{0,4},{4,8},{8,12},{12,16},{16,20},{20,24},{24,28},{1,5},{5,9},{9,... | collective-permute-start | bytes 1572872 | tf_op jit(solution)/shard_map/ppermute | solution.py:38
  321.8 7.1 %collective-permute-done.48.a2 = bf16[256,1024]{1,0:T(8,128)(2,1)S(1)} collective-permute-done((bf16[256,1024]{1,0:T(8,128)(2,1)S(1)}, bf16[256,1024]{1,0:T(8,128)(2,1)S(1)}, u32[]{:S(2)}, u32[]{:S(2)}) %collective-permute-start.48) | collective-permute-done | bytes 524320 | tf_op jit(solution)/shard_map/ppermute | solution.py:27
  341.7 5.5 %collective-permute-start.45 = (bf16[384,256]{1,0:T(8,128)(2,1)}, bf16[384,256]{1,0:T(8,128)(2,1)S(1)}, u32[]{:S(2)}, u32[]{:S(2)}) collective-permute-start(bf16[384,256]{1,0:T(8,128)(2,1)} %get-tuple-element.170), channel_id=1, source_target_pairs={{0,8},{4,12},{8,16},{12,20},{16,24},{20,28},{1,9},{5,13},{9,17},{1... | collective-permute-start | bytes 589832 | tf_op jit(solution)/shard_map/ppermute | solution.py:38
  350.6 8.9 %collective-permute-done.42 = bf16[384,256]{1,0:T(8,128)(2,1)S(1)} collective-permute-done((bf16[384,256]{1,0:T(8,128)(2,1)}, bf16[384,256]{1,0:T(8,128)(2,1)S(1)}, u32[]{:S(2)}, u32[]{:S(2)}) %collective-permute-start.42) | collective-permute-done | bytes 196640 | tf_op jit(solution)/shard_map/ppermute | solution.py:38
  362.6 5.0 %qkv_grad.1 = bf16[24,256,128]{2,1,0:T(8,128)(2,1)} custom-call(bf16[1024,256]{1,0:T(8,128)(2,1)} %copy-done.2, bf16[1024,256]{1,0:T(8,128)(2,1)} %pad_maximum_fusion.3.gk, bf16[1024,256]{1,0:T(8,128)(2,1)} %pad_maximum_fusion.4.gv, bf16[1024,1024]{1,0:T(8,128)(2,1)} %get-tuple-element.198.n1), custom_call_target="tpu_custom_call" | custom-call | flops 5000000000 | bytes 1048576 | tf_op jit(solution)/shard_map/qkv_grad/pallas_call | solution.py:661
  367.6 6.0 %gn1.1 = (bf16[256,1024]{1,0:T(8,128)(2,1)}, bf16[256,1024]{1,0:T(8,128)(2,1)}, bf16[256,1024]{1,0:T(8,128)(2,1)}, bf16[256,1024]{1,0:T(8,128)(2,1)}) custom-call(s32[1]{0:T(128)} %bitcast.sc, bf16[1024,128]{1,0:T(8,128)(2,1)} %get-tuple-element.186.gq0, bf16[1024,128]{1,0:T(8,128)(2,1)} %get-tuple-element.187.gq1, bf16[1024,256]{1,0:T(8,128)(2,1)} %pad_maximum_fusion.3.gk, ...), custom_call_target="tpu_custom_call" | custom-call | flops 6000000000 | bytes 1048576 | tf_op jit(solution)/shard_map/gn1/pallas_call | solution.py:634
  374.2 5.7 %norm_sums.1 = f32[8,1024]{1,0:T(8,128)} custom-call(s32[1]{0:T(128)} %bitcast.sc, bf16[256,1024]{1,0:T(8,128)(2,1)} %get-tuple-element.201.a0, bf16[256,1024]{1,0:T(8,128)(2,1)} %get-tuple-element.202.a1, bf16[256,1024]{1,0:T(8,128)(2,1)} %get-tuple-element.203.a2, bf16[256,1024]{1,0:T(8,128)(2,1)} %get-tuple-element.204.a3, bf16[1024,256]{1,0:T(8,128)(2,1)} %x0.7, ...), custom_call_target="tpu_custom_call" | custom-call | flops 5000000000 | bytes 1048576 | tf_op jit(solution)/shard_map/norm_sums/pallas_call | solution.py:694
  392.8 5.6 %collective-permute-done.64.a2 = bf16[256,1024]{1,0:T(8,128)(2,1)S(1)} collective-permute-done((bf16[256,1024]{1,0:T(8,128)(2,1)S(1)}, bf16[256,1024]{1,0:T(8,128)(2,1)S(1)}, u32[]{:S(2)}, u32[]{:S(2)}) %collective-permute-start.64) | collective-permute-done | bytes 524320 | tf_op jit(solution)/shard_map/ppermute | solution.py:27
  424.2 5.6 %collective-permute-done.70 = bf16[3,256,128]{2,1,0:T(8,128)(2,1)S(1)} collective-permute-done((bf16[3,256,128]{2,1,0:T(8,128)(2,1)S(1)}, bf16[3,256,128]{2,1,0:T(8,128)(2,1)S(1)}, u32[]{:S(2)}, u32[]{:S(2)}) %collective-permute-start.70) | collective-permute-done | bytes 196640 | tf_op jit(solution)/shard_map/ppermute | solution.py:32
  (360 shorter events, 148.5 us)
Async XLA Ops:
  7.2 186.6 %all-gather.2.cloned.1.call-start = ((), (), s32[]{:S(2)}) async-start(), calls=%async_computation.1 | async-start | bytes 4718592 | tf_op jit(solution)/shard_map/all_gather | solution.py:951
  7.2 52.7 %collective-permute-start = (bf16[1024,256]{1,0:T(8,128)(2,1)}, bf16[1024,256]{1,0:T(8,128)(2,1)}, u32[]{:S(2)}, u32[]{:S(2)}) collective-permute-start(bf16[1024,256]{1,0:T(8,128)(2,1)} %x0.7), channel_id=1, source_target_pairs={{0,1},{1,0},{2,3},{3,2},{4,5},{5,4},{6,7},{7,6},{8,9},{9,8},{10,11... | collective-permute-start | bytes 1572872 | tf_op jit(solution)/shard_map/ppermute | solution.py:27
  7.8 41.0 %collective-permute-start.1 = (bf16[1024,256]{1,0:T(8,128)(2,1)}, bf16[1024,256]{1,0:T(8,128)(2,1)}, u32[]{:S(2)}, u32[]{:S(2)}) collective-permute-start(bf16[1024,256]{1,0:T(8,128)(2,1)} %x0.7), channel_id=1, source_target_pairs={{0,2},{1,3},{2,0},{3,1},{4,6},{5,7},{6,4},{7,5},{8,10},{9,11},{10,... | collective-permute-start | bytes 1572872 | tf_op jit(solution)/shard_map/ppermute | solution.py:27
  26.1 20.9 %collective-permute-start.6 = (bf16[256,512]{1,0:T(8,128)(2,1)S(1)}, bf16[256,512]{1,0:T(8,128)(2,1)S(1)}, u32[]{:S(2)}, u32[]{:S(2)}) collective-permute-start(bf16[256,512]{1,0:T(8,128)(2,1)S(1)} %constant_dynamic-update-slice_fusion), channel_id=1, source_target_pairs={{0,16},{4,20},{8,24},{12,28},{16,0},{20,4},{24,8},{28,12},{1,17},{... | collective-permute-start | bytes 786440 | tf_op jit(solution)/shard_map/ppermute | solution.py:32
  47.0 52.8 %collective-permute-start.25 = (bf16[256,256]{1,0:T(8,128)(2,1)S(1)}, bf16[256,256]{1,0:T(8,128)(2,1)S(1)}, u32[]{:S(2)}, u32[]{:S(2)}) collective-permute-start(bf16[256,256]{1,0:T(8,128)(2,1)S(1)} %get-tuple-element.317), channel_id=1, source_target_pairs={{0,2},{1,3},{2,0},{3,1},{4,6},{5,7},{6,4},{7,5},{8,10},{9,11},{10,... | collective-permute-start | bytes 393224 | tf_op jit(solution)/shard_map/ppermute | solution.py:27
  69.1 28.8 %collective-permute-start.18 = (bf16[1024,256]{1,0:T(8,128)(2,1)}, bf16[1024,256]{1,0:T(8,128)(2,1)S(1)}, u32[]{:S(2)}, u32[]{:S(2)}) collective-permute-start(bf16[1024,256]{1,0:T(8,128)(2,1)} %get-tuple-element.127.refs_2_), channel_id=1, source_target_pairs={{0,4},{4,8},{8,12},{12,16},{16,20},{20,24},{24,28},{1,5},{5,9},{9,... | collective-permute-start | bytes 1572872 | tf_op jit(solution)/shard_map/ppermute | solution.py:38
  71.3 26.6 %collective-permute-start.19 = (bf16[1024,256]{1,0:T(8,128)(2,1)}, bf16[1024,256]{1,0:T(8,128)(2,1)S(1)}, u32[]{:S(2)}, u32[]{:S(2)}) collective-permute-start(bf16[1024,256]{1,0:T(8,128)(2,1)} %get-tuple-element.127.refs_2_), channel_id=1, source_target_pairs={{4,0},{8,4},{12,8},{16,12},{20,16},{24,20},{28,24},{5,1},{9,5},{13... | collective-permute-start | bytes 1572872 | tf_op jit(solution)/shard_map/ppermute | solution.py:38
  98.0 332.7 %reduce-scatter.2.cloned.1.call-start = ((), (), s32[]{:S(2)}) async-start(), calls=%async_computation.2 | async-start | bytes 4718592 | tf_op jit(solution)/shard_map/reduce_scatter | solution.py:976
  100.1 17.7 %collective-permute-start.28 = (bf16[256,1024]{1,0:T(8,128)(2,1)S(1)}, bf16[256,1024]{1,0:T(8,128)(2,1)S(1)}, u32[]{:S(2)}, u32[]{:S(2)}) collective-permute-start(bf16[256,1024]{1,0:T(8,128)(2,1)S(1)} %multiply_convert_fusion.g0), channel_id=1, source_target_pairs={{0,2},{1,3},{2,0},{3,1},{4,6},{5,7},{6,4},{7,5},{8,10},{9,11},{10,... | collective-permute-start | bytes 1572872 | tf_op jit(solution)/shard_map/ppermute | solution.py:27
  103.0 33.1 %collective-permute-start.14 = (bf16[1024,256]{1,0:T(8,128)(2,1)S(1)}, bf16[1024,256]{1,0:T(8,128)(2,1)S(1)}, u32[]{:S(2)}, u32[]{:S(2)}) collective-permute-start(bf16[1024,256]{1,0:T(8,128)(2,1)S(1)} %copy-done.14), channel_id=1, source_target_pairs={{0,4},{4,8},{8,12},{12,16},{16,20},{20,24},{24,28},{1,5},{5,9},{9,... | collective-permute-start | bytes 1572872 | tf_op jit(solution)/shard_map/ppermute | solution.py:38
  104.3 32.3 %collective-permute-start.15 = (bf16[1024,256]{1,0:T(8,128)(2,1)S(1)}, bf16[1024,256]{1,0:T(8,128)(2,1)S(1)}, u32[]{:S(2)}, u32[]{:S(2)}) collective-permute-start(bf16[1024,256]{1,0:T(8,128)(2,1)S(1)} %copy-done.14), channel_id=1, source_target_pairs={{4,0},{8,4},{12,8},{16,12},{20,16},{24,20},{28,24},{5,1},{9,5},{13... | collective-permute-start | bytes 1572872 | tf_op jit(solution)/shard_map/ppermute | solution.py:38
  105.6 29.8 %collective-permute-start.13 = (bf16[384,256]{1,0:T(8,128)(2,1)S(1)}, bf16[384,256]{1,0:T(8,128)(2,1)S(1)}, u32[]{:S(2)}, u32[]{:S(2)}) collective-permute-start(bf16[384,256]{1,0:T(8,128)(2,1)S(1)} %get-tuple-element.322), channel_id=1, source_target_pairs={{0,8},{4,12},{8,16},{12,20},{16,24},{20,28},{1,9},{5,13},{9,17},{1... | collective-permute-start | bytes 589832 | tf_op jit(solution)/shard_map/ppermute | solution.py:38
  116.3 19.2 %collective-permute-start.16 = (bf16[384,256]{1,0:T(8,128)(2,1)S(1)}, bf16[384,256]{1,0:T(8,128)(2,1)S(1)}, u32[]{:S(2)}, u32[]{:S(2)}) collective-permute-start(bf16[384,256]{1,0:T(8,128)(2,1)S(1)} %get-tuple-element.321), channel_id=1, source_target_pairs={{8,0},{12,4},{16,8},{20,12},{24,16},{28,20},{9,1},{13,5},{17,9},{2... | collective-permute-start | bytes 589832 | tf_op jit(solution)/shard_map/ppermute | solution.py:38
  117.8 18.4 %collective-permute-start.22 = (bf16[256,1024]{1,0:T(8,128)(2,1)S(1)}, bf16[256,1024]{1,0:T(8,128)(2,1)S(1)}, u32[]{:S(2)}, u32[]{:S(2)}) collective-permute-start(bf16[256,1024]{1,0:T(8,128)(2,1)S(1)} %copy-done.28), channel_id=1, source_target_pairs={{0,2},{1,3},{2,0},{3,1},{4,6},{5,7},{6,4},{7,5},{8,10},{9,11},{10,... | collective-permute-start | bytes 1572872 | tf_op jit(solution)/shard_map/ppermute | solution.py:27
  135.5 19.2 %collective-permute-start.27 = (bf16[256,1024]{1,0:T(8,128)(2,1)S(1)}, bf16[256,1024]{1,0:T(8,128)(2,1)S(1)}, u32[]{:S(2)}, u32[]{:S(2)}) collective-permute-start(bf16[256,1024]{1,0:T(8,128)(2,1)S(1)} %multiply_convert_fusion.g0), channel_id=1, source_target_pairs={{0,1},{1,0},{2,3},{3,2},{4,5},{5,4},{6,7},{7,6},{8,9},{9,8},{10,11... | collective-permute-start | bytes 1572872 | tf_op jit(solution)/shard_map/ppermute | solution.py:27
  135.6 19.1 %collective-permute-start.29 = (bf16[256,1024]{1,0:T(8,128)(2,1)S(1)}, bf16[256,1024]{1,0:T(8,128)(2,1)S(1)}, u32[]{:S(2)}, u32[]{:S(2)}) collective-permute-start(bf16[256,1024]{1,0:T(8,128)(2,1)S(1)} %collective-permute-done.28.g0.g2), channel_id=1, source_target_pairs={{0,1},{1,0},{2,3},{3,2},{4,5},{5,4},{6,7},{7,6},{8,9},{9,8},{10,11... | collective-permute-start | bytes 1572872 | tf_op jit(solution)/shard_map/ppermute | solution.py:27
  136.1 18.6 %collective-permute-start.21 = (bf16[256,1024]{1,0:T(8,128)(2,1)S(1)}, bf16[256,1024]{1,0:T(8,128)(2,1)S(1)}, u32[]{:S(2)}, u32[]{:S(2)}) collective-permute-start(bf16[256,1024]{1,0:T(8,128)(2,1)S(1)} %copy-done.28), channel_id=1, source_target_pairs={{0,1},{1,0},{2,3},{3,2},{4,5},{5,4},{6,7},{7,6},{8,9},{9,8},{10,11... | collective-permute-start | bytes 1572872 | tf_op jit(solution)/shard_map/ppermute | solution.py:27
  136.2 18.5 %collective-permute-start.23 = (bf16[256,1024]{1,0:T(8,128)(2,1)S(1)}, bf16[256,1024]{1,0:T(8,128)(2,1)S(1)}, u32[]{:S(2)}, u32[]{:S(2)}) collective-permute-start(bf16[256,1024]{1,0:T(8,128)(2,1)S(1)} %collective-permute-done.22.w2), channel_id=1, source_target_pairs={{0,1},{1,0},{2,3},{3,2},{4,5},{5,4},{6,7},{7,6},{8,9},{9,8},{10,11... | collective-permute-start | bytes 1572872 | tf_op jit(solution)/shard_map/ppermute | solution.py:27
  271.9 33.0 %collective-permute-start.47 = (bf16[256,1024]{1,0:T(8,128)(2,1)S(1)}, bf16[256,1024]{1,0:T(8,128)(2,1)S(1)}, u32[]{:S(2)}, u32[]{:S(2)}) collective-permute-start(bf16[256,1024]{1,0:T(8,128)(2,1)S(1)} %copy-done.33), channel_id=1, source_target_pairs={{0,1},{1,0},{2,3},{3,2},{4,5},{5,4},{6,7},{7,6},{8,9},{9,8},{10,11... | collective-permute-start | bytes 1572872 | tf_op jit(solution)/shard_map/ppermute | solution.py:27
  272.0 42.5 %collective-permute-start.57 = (bf16[1024,256]{1,0:T(8,128)(2,1)}, bf16[1024,256]{1,0:T(8,128)(2,1)S(1)}, u32[]{:S(2)}, u32[]{:S(2)}) collective-permute-start(bf16[1024,256]{1,0:T(8,128)(2,1)} %get-tuple-element.191), channel_id=1, source_target_pairs={{0,4},{4,8},{8,12},{12,16},{16,20},{20,24},{24,28},{1,5},{5,9},{9,... | collective-permute-start | bytes 1572872 | tf_op jit(solution)/shard_map/ppermute | solution.py:38
  276.7 37.9 %collective-permute-start.56 = (bf16[1024,256]{1,0:T(8,128)(2,1)}, bf16[1024,256]{1,0:T(8,128)(2,1)S(1)}, u32[]{:S(2)}, u32[]{:S(2)}) collective-permute-start(bf16[1024,256]{1,0:T(8,128)(2,1)} %get-tuple-element.190), channel_id=1, source_target_pairs={{4,0},{8,4},{12,8},{16,12},{20,16},{24,20},{28,24},{5,1},{9,5},{13... | collective-permute-start | bytes 1572872 | tf_op jit(solution)/shard_map/ppermute | solution.py:38
  278.0 28.5 %collective-permute-start.58 = (bf16[384,256]{1,0:T(8,128)(2,1)}, bf16[384,256]{1,0:T(8,128)(2,1)S(1)}, u32[]{:S(2)}, u32[]{:S(2)}) collective-permute-start(bf16[384,256]{1,0:T(8,128)(2,1)} %get-tuple-element.192), channel_id=1, source_target_pairs={{0,8},{4,12},{8,16},{12,20},{16,24},{20,28},{1,9},{5,13},{9,17},{1... | collective-permute-start | bytes 589832 | tf_op jit(solution)/shard_map/ppermute | solution.py:38
  282.0 33.8 %collective-permute-start.53 = (bf16[256,1024]{1,0:T(8,128)(2,1)S(1)}, bf16[256,1024]{1,0:T(8,128)(2,1)S(1)}, u32[]{:S(2)}, u32[]{:S(2)}) collective-permute-start(bf16[256,1024]{1,0:T(8,128)(2,1)S(1)} %copy-done.6), channel_id=1, source_target_pairs={{0,2},{1,3},{2,0},{3,1},{4,6},{5,7},{6,4},{7,5},{8,10},{9,11},{10,... | collective-permute-start | bytes 1572872 | tf_op jit(solution)/shard_map/ppermute | solution.py:27
  306.5 27.1 %collective-permute-start.52 = (bf16[256,1024]{1,0:T(8,128)(2,1)S(1)}, bf16[256,1024]{1,0:T(8,128)(2,1)S(1)}, u32[]{:S(2)}, u32[]{:S(2)}) collective-permute-start(bf16[256,1024]{1,0:T(8,128)(2,1)S(1)} %copy-done.6), channel_id=1, source_target_pairs={{0,1},{1,0},{2,3},{3,2},{4,5},{5,4},{6,7},{7,6},{8,9},{9,8},{10,11... | collective-permute-start | bytes 1572872 | tf_op jit(solution)/shard_map/ppermute | solution.py:27
  313.2 46.3 %collective-permute-start.43 = (bf16[1024,256]{1,0:T(8,128)(2,1)}, bf16[1024,256]{1,0:T(8,128)(2,1)S(1)}, u32[]{:S(2)}, u32[]{:S(2)}) collective-permute-start(bf16[1024,256]{1,0:T(8,128)(2,1)} %get-tuple-element.168), channel_id=1, source_target_pairs={{4,0},{8,4},{12,8},{16,12},{20,16},{24,20},{28,24},{5,1},{9,5},{13... | collective-permute-start | bytes 1572872 | tf_op jit(solution)/shard_map/ppermute | solution.py:38
  315.8 18.7 %collective-permute-start.54 = (bf16[256,1024]{1,0:T(8,128)(2,1)S(1)}, bf16[256,1024]{1,0:T(8,128)(2,1)S(1)}, u32[]{:S(2)}, u32[]{:S(2)}) collective-permute-start(bf16[256,1024]{1,0:T(8,128)(2,1)S(1)} %collective-permute-done.53), channel_id=1, source_target_pairs={{0,1},{1,0},{2,3},{3,2},{4,5},{5,4},{6,7},{7,6},{8,9},{9,8},{10,11... | collective-permute-start | bytes 1572872 | tf_op jit(solution)/shard_map/ppermute | solution.py:27
  316.5 43.0 %collective-permute-start.44 = (bf16[1024,256]{1,0:T(8,128)(2,1)}, bf16[1024,256]{1,0:T(8,128)(2,1)}, u32[]{:S(2)}, u32[]{:S(2)}) collective-permute-start(bf16[1024,256]{1,0:T(8,128)(2,1)} %get-tuple-element.169), channel_id=1, source_target_pairs={{0,4},{4,8},{8,12},{12,16},{16,20},{20,24},{24,28},{1,5},{5,9},{9,... | collective-permute-start | bytes 1572872 | tf_op jit(solution)/shard_map/ppermute | solution.py:38
  339.4 20.1 %collective-permute-start.42 = (bf16[384,256]{1,0:T(8,128)(2,1)}, bf16[384,256]{1,0:T(8,128)(2,1)S(1)}, u32[]{:S(2)}, u32[]{:S(2)}) collective-permute-start(bf16[384,256]{1,0:T(8,128)(2,1)} %get-tuple-element.167), channel_id=1, source_target_pairs={{8,0},{12,4},{16,8},{20,12},{24,16},{28,20},{9,1},{13,5},{17,9},{2... | collective-permute-start | bytes 589832 | tf_op jit(solution)/shard_map/ppermute | solution.py:38
  341.7 17.8 %collective-permute-start.45 = (bf16[384,256]{1,0:T(8,128)(2,1)}, bf16[384,256]{1,0:T(8,128)(2,1)S(1)}, u32[]{:S(2)}, u32[]{:S(2)}) collective-permute-start(bf16[384,256]{1,0:T(8,128)(2,1)} %get-tuple-element.170), channel_id=1, source_target_pairs={{0,8},{4,12},{8,16},{12,20},{16,24},{20,28},{1,9},{5,13},{9,17},{1... | collective-permute-start | bytes 589832 | tf_op jit(solution)/shard_map/ppermute | solution.py:38
  347.2 35.5 %collective-permute-start.71 = (bf16[2,2,128,256]{2,3,0,1:T(8,128)(2,1)S(1)}, bf16[2,2,128,256]{2,3,0,1:T(8,128)(2,1)S(1)}, u32[]{:S(2)}, u32[]{:S(2)}) collective-permute-start(bf16[2,2,128,256]{2,3,0,1:T(8,128)(2,1)S(1)} %bitcast.132), channel_id=1, source_target_pairs={{0,8},{4,12},{8,0},{12,4},{16,24},{20,28},{24,16},{28,20},{1,9},{5... | collective-permute-start | bytes 786440 | tf_op jit(solution)/shard_map/ppermute | solution.py:32
  373.7 19.2 %collective-permute-start.62 = (bf16[256,1024]{1,0:T(8,128)(2,1)}, bf16[256,1024]{1,0:T(8,128)(2,1)S(1)}, u32[]{:S(2)}, u32[]{:S(2)}) collective-permute-start(bf16[256,1024]{1,0:T(8,128)(2,1)} %get-tuple-element.202.a1), channel_id=1, source_target_pairs={{0,1},{1,0},{2,3},{3,2},{4,5},{5,4},{6,7},{7,6},{8,9},{9,8},{10,11... | collective-permute-start | bytes 1572872 | tf_op jit(solution)/shard_map/ppermute | solution.py:27
  383.0 24.3 %collective-permute-start.68 = (bf16[2,2,3,256,128]{4,3,2,0,1:T(8,128)(2,1)S(1)}, bf16[2,2,3,256,128]{4,3,2,0,1:T(8,128)(2,1)S(1)}, u32[]{:S(2)}, u32[]{:S(2)}) collective-permute-start(bf16[2,2,3,256,128]{4,3,2,0,1:T(8,128)(2,1)S(1)} %copy_bitcast_fusion), channel_id=1, source_target_pairs={{0,8},{4,12},{8,0},{12,4},{16,24},{20,28},{24,16},{28,20},{1,9},{5... | collective-permute-start | bytes 2359304 | tf_op jit(solution)/shard_map/ppermute | solution.py:32
  (107 other events, 1178.8 us)
Sparse Core Ops, SparseCore 0:
  98.1 95.6 all-gather.1
  244.8 117.6 reduce-scatter.1

commit v4 on v3

--- a/solution.py
+++ b/solution.py
@@ -16,6 +16,7 @@
 BF = jnp.bfloat16
 F32 = jnp.float32
 TILE = 256
+STEP = 2 * TILE
 PAIR = 2 * HEAD_DIM
 SCALE = HEAD_DIM ** (-0.5)
 INV_SQRT2 = 0.7071067811865476
@@ -172,6 +173,8 @@
     ]
     for copy in copies:
         copy.start()
+    last = offsets[-1] + counts[-1]
+    target[last:, :] = jnp.zeros((target.shape[0] - last, target.shape[1]), target.dtype)
     for copy in copies:
         copy.wait()
 
@@ -187,9 +190,13 @@
     return jnp.concatenate([values[0:HEAD_DIM, :TILE], values[HEAD_DIM:PAIR, TILE:]], axis=0)
 
 
-def scores_of(kv, head_query, j, start, end):
-    raw = nt(kv[pl.ds(pl.multiple_of(j * TILE, TILE), TILE), 0:PAIR], head_query)
-    place = lax.broadcasted_iota(jnp.int32, raw.shape, 0) + j * TILE
+def step_rows(lo, j):
+    return pl.ds(pl.multiple_of(lo * TILE + j * STEP, TILE), STEP)
+
+
+def scores_of(kv, head_query, lo, j, start, end):
+    raw = nt(kv[step_rows(lo, j), 0:PAIR], head_query)
+    place = lax.broadcasted_iota(jnp.int32, raw.shape, 0) + (lo * TILE + j * STEP)
     return jnp.where((place >= start) & (place < end), raw, NEG)
 
 
@@ -212,37 +219,37 @@
         load_pieces(pieces, kv, sem, offsets, counts)
 
     lo = sc[1 + 2 * i]
-    hi = sc[2 + 2 * i]
+    steps = (sc[2 + 2 * i] - lo + 1) // 2
     start = twice(se_ref[0:1, :])
     end = twice(se_ref[1:2, :])
     head_query = by_head(q_ref[...].astype(F32) * SCALE)
 
     def first(j, peak):
-        score = scores_of(kv, head_query, j, start, end)
-        s_scr[j - lo] = score
+        score = scores_of(kv, head_query, lo, j, start, end)
+        s_scr[j] = score
         return jnp.maximum(peak, fold8(score, jnp.max))
 
-    peak8 = lax.fori_loop(lo, hi, first, jnp.full((8, 2 * TILE), NEG, F32))
+    peak8 = lax.fori_loop(0, steps, first, jnp.full((8, 2 * TILE), NEG, F32))
     peak = jnp.max(peak8, axis=0, keepdims=True)
     peak = jnp.maximum(peak, 0.1 * NEG)
 
     def second(j, total):
-        expon = jnp.exp(s_scr[j - lo] - peak)
-        s_scr[j - lo] = expon
+        expon = jnp.exp(s_scr[j] - peak)
+        s_scr[j] = expon
         return total + fold8(expon, jnp.sum)
 
-    total8 = lax.fori_loop(lo, hi, second, jnp.zeros((8, 2 * TILE), F32))
+    total8 = lax.fori_loop(0, steps, second, jnp.zeros((8, 2 * TILE), F32))
     total = jnp.sum(total8, axis=0, keepdims=True)
     inverse = 1.0 / jnp.where(end > start, total, 1.0)
     acc[...] = jnp.zeros(acc.shape, F32)
 
     def third(j, carry):
-        prob = (s_scr[j - lo] * inverse).astype(BF)
-        vals = kv[pl.ds(pl.multiple_of(j * TILE, TILE), TILE), PAIR : 2 * PAIR]
+        prob = (s_scr[j] * inverse).astype(BF)
+        vals = kv[step_rows(lo, j), PAIR : 2 * PAIR]
         acc[...] += tn(vals, prob)
         return carry
 
-    lax.fori_loop(lo, hi, third, 0)
+    lax.fori_loop(0, steps, third, 0)
     for head in range(2):
         at = slice(head * TILE, (head + 1) * TILE)
         st_ref[head : head + 1, :] = peak[:, at]
@@ -268,8 +275,8 @@
                 pl.BlockSpec((8, TILE), lambda i, sc: (0, i)),
             ],
             scratch_shapes=[
-                pltpu.VMEM((near, 2 * PAIR), BF),
-                pltpu.VMEM((near // TILE, TILE, 2 * TILE), F32),
+                pltpu.VMEM((near + TILE, 2 * PAIR), BF),
+                pltpu.VMEM((near // STEP + 1, STEP, 2 * TILE), F32),
                 pltpu.VMEM((PAIR, 2 * TILE), F32),
                 pltpu.SemaphoreType.DMA((len(pieces),)),
             ],
@@ -299,7 +306,7 @@
 
     i = sc[0] ^ r
     lo = sc[1 + 2 * i]
-    hi = sc[2 + 2 * i]
+    steps = (sc[2 + 2 * i] - lo + 1) // 2
     start = se_ref[0:1, :]
     end = se_ref[1:2, :]
     start = twice(start)
@@ -310,29 +317,29 @@
     inverse = jnp.concatenate([st_ref[2:3, :], st_ref[3:4, :]], axis=1)
 
     def first(j, dot8):
-        score = scores_of(kv, head_query, j, start, end)
+        score = scores_of(kv, head_query, lo, j, start, end)
         weight = jnp.exp(score - peak) * inverse
-        vals = kv[pl.ds(pl.multiple_of(j * TILE, TILE), TILE), PAIR : 2 * PAIR]
+        vals = kv[step_rows(lo, j), PAIR : 2 * PAIR]
         grad_prob = nt(vals, head_grad)
-        w_scr[j - lo] = weight
-        g_scr[j - lo] = grad_prob
+        w_scr[j] = weight
+        g_scr[j] = grad_prob
         return dot8 + fold8(weight * grad_prob, jnp.sum)
 
-    dot8 = lax.fori_loop(lo, hi, first, jnp.zeros((8, 2 * TILE), F32))
+    dot8 = lax.fori_loop(0, steps, first, jnp.zeros((8, 2 * TILE), F32))
     rowdot = jnp.sum(dot8, axis=0, keepdims=True)
     dq_scr[...] = jnp.zeros(dq_scr.shape, F32)
 
     def second(j, carry):
-        weight = w_scr[j - lo]
-        grad_score = (weight * (g_scr[j - lo] - rowdot)).astype(BF)
+        weight = w_scr[j]
+        grad_score = (weight * (g_scr[j] - rowdot)).astype(BF)
         prob = weight.astype(BF)
-        at = pl.ds(pl.multiple_of(j * TILE, TILE), TILE)
+        at = step_rows(lo, j)
         acc[at, 0:PAIR] += nn(grad_score, head_query)
         acc[at, PAIR : 2 * PAIR] += nn(prob, head_grad)
         dq_scr[...] += tn(kv[at, 0:PAIR], grad_score)
         return carry
 
-    lax.fori_loop(lo, hi, second, 0)
+    lax.fori_loop(0, steps, second, 0)
     dq_ref[...] = (joined(dq_scr[...]).T * SCALE).astype(BF)
 
     @pl.when(r == pl.num_programs(0) - 1)
@@ -364,10 +371,10 @@
             out_specs=[pl.BlockSpec((TILE, PAIR), lambda r, sc: (sc[0] ^ r, 0))]
             + [whole(c) for c in counts],
             scratch_shapes=[
-                pltpu.VMEM((near, 2 * PAIR), BF),
-                pltpu.VMEM((near // TILE, TILE, 2 * TILE), F32),
-                pltpu.VMEM((near // TILE, TILE, 2 * TILE), F32),
-                pltpu.VMEM((near, 2 * PAIR), F32),
+                pltpu.VMEM((near + TILE, 2 * PAIR), BF),
+                pltpu.VMEM((near // STEP + 1, STEP, 2 * TILE), F32),
+                pltpu.VMEM((near // STEP + 1, STEP, 2 * TILE), F32),
+                pltpu.VMEM((near + TILE, 2 * PAIR), F32),
                 pltpu.VMEM((PAIR, 2 * TILE), F32),
                 pltpu.SemaphoreType.DMA((len(pieces),)),
             ],
@@ -807,12 +814,14 @@
     return pieces[0], px(pieces[1], 1), px(far, 2)
 
 
-def halved(blocks, s):
+def halved(blocks, s, early=None):
     for axis, bits, place in ((1, 2, 1), (1, 1, 0), (0, 4, 2)):
         mine = (s >> place) & 1
         keep = lax.dynamic_index_in_dim(blocks, mine, axis, keepdims=False)
         send = lax.dynamic_index_in_dim(blocks, 1 - mine, axis, keepdims=False)
         got = ps(send.astype(BF), bits)
+        if bits == 4 and early:
+            got, *early[:] = after(got, *early)
         blocks = keep.astype(F32) + got.astype(F32)
     return blocks
 
@@ -1027,11 +1036,16 @@
     gk = jnp.concatenate(grad_k, axis=1)
     gv = jnp.concatenate(grad_v, axis=1)
     gq = jnp.concatenate(grad_q, axis=1)
+    finals = [
+        proj_out.T.astype(F32),
+        fc_out[:, :units].T.astype(F32),
+        fc_out[:, units:].T.astype(F32),
+    ]
     if n_seq == 8:
         unit = width // 8
         blocks = qkvg_call(gq, gk, gv, normed1).reshape(2, 2, 2, 3, features, unit)
         blocks, gk = after(blocks, gk)
-        blocks = halved(blocks, s)
+        blocks = halved(blocks, s, finals)
         qkv_out = jnp.concatenate([blocks[k] for k in range(3)], axis=1)
     else:
         qkv_parts = [tn(g, normed1) for g in (gq, gk, gv)]
@@ -1072,9 +1086,7 @@
         block_output,
         input_grad,
         qkv_out,
-        proj_out.T.astype(F32),
-        fc_out[:, :units].T.astype(F32),
-        fc_out[:, units:].T.astype(F32),
+        *finals,
         own8[0],
         own8[1],
         q_bias_grad,

time: 443 us -> 442 us (level)
  Pallas kernels: 148 us -> 133 us
  starting transfers between devices: 107 us -> 114 us
  waiting for transfers between devices: 129 us -> 134 us
    pallas_call x2, Pallas kernels: 33.8 us -> 25.6 us  [fwd_call(): pl.pallas_call(functools.partial(fwd_kernel, offsets, counts), grid_spec=...]
    all_gather x1, waiting for transfers between devices: 7.28 us -> 14.6 us  [per_device(): others = lax.all_gather(stacked, 'seq', axis=1, tiled=True)]
    pallas_call x2, Pallas kernels: 43.5 us -> 36.4 us  [bwd_call(): pl.pallas_call(functools.partial(bwd_kernel, offsets, counts), grid_spec=...]
    ppermute x16, starting transfers between devices: 24 us -> 29.4 us  [ps(): return lax.ppermute(value, 'seq', pairs)]
  transfers between devices with their start and end apart: 79 -> 79, of which waited for: 32 -> 31; matrix products, arithmetic and copies ran while one was open for 7% -> 7% of each run, Pallas kernels for 28% -> 24%
where the time goes in v4:
time: 442 us; the launch traced here: 436 us
  waiting for transfers between devices  134 us (30%)
  Pallas kernels  133 us (30%)
  starting transfers between devices  114 us (26%)
  local copies, waits for them, and re-layouts  22.8 us (5%)
  other arithmetic  17 us (4%)
  between operations  15.7 us (4%)
    ppermute x16, starting transfers between devices, passed_along(): return lax.ppermute(block, 'seq', route)  57.4 us
    ppermute x45, waiting for transfers between devices, px(): return lax.ppermute(value, 'tensor', pairs)  54.6 us
    ppermute x16, waiting for transfers between devices, ps(): return lax.ppermute(value, 'seq', pairs)  40.1 us
    pallas_call x2, Pallas kernels, bwd_call(): pl.pallas_call(functools.partial(bwd_kernel, offsets, counts), grid_spec=...  36.4 us
    ppermute x16, starting transfers between devices, ps(): return lax.ppermute(value, 'seq', pairs)  29.4 us
    ppermute x45, starting transfers between devices, px(): return lax.ppermute(value, 'tensor', pairs)  26.7 us
    pallas_call x2, Pallas kernels, fwd_call(): pl.pallas_call(functools.partial(fwd_kernel, offsets, counts), grid_spec=...  25.6 us
    ppermute x16, waiting for transfers between devices, passed_along(): return lax.ppermute(block, 'seq', route)  24.3 us
  transfers between devices with their start and end apart: 79, of which 31 were waited for; matrix products, arithmetic and copies ran while one was open for 7% of the time, Pallas kernels for 24%

profile of v4, /device:TPU:0, one launch (start us, length us, event | category | flops | bytes accessed | tf_op | source)
XLA Modules:
  0.0 436.1 jit_solution(1242131054568372169)
XLA Ops:
  15.2 7.7 %collective-permute-done.10 = f32[8,256]{1,0:T(8,128)S(1)} collective-permute-done((f32[8,256]{1,0:T(8,128)S(1)}, f32[8,256]{1,0:T(8,128)S(1)}, u32[]{:S(2)}, u32[]{:S(2)}) %collective-permute-start.10) | collective-permute-done | bytes 8224 | tf_op jit(solution)/shard_map/ppermute | solution.py:28
  39.1 7.9 %collective-permute-done.6 = bf16[256,512]{1,0:T(8,128)(2,1)S(1)} collective-permute-done((bf16[256,512]{1,0:T(8,128)(2,1)S(1)}, bf16[256,512]{1,0:T(8,128)(2,1)S(1)}, u32[]{:S(2)}, u32[]{:S(2)}) %collective-permute-start.6) | collective-permute-done | bytes 262176 | tf_op jit(solution)/shard_map/ppermute | solution.py:33
  50.6 6.6 %collective-permute-done.7 = bf16[256,512]{1,0:T(8,128)(2,1)S(1)} collective-permute-done((bf16[256,512]{1,0:T(8,128)(2,1)S(1)}, bf16[256,512]{1,0:T(8,128)(2,1)S(1)}, u32[]{:S(2)}, u32[]{:S(2)}) %collective-permute-start.7) | collective-permute-done | bytes 262176 | tf_op jit(solution)/shard_map/ppermute | solution.py:33
  61.5 7.6 %qkv.1 = (bf16[1024,1024]{1,0:T(8,128)(2,1)}, bf16[1024,256]{1,0:T(8,128)(2,1)}, bf16[1024,256]{1,0:T(8,128)(2,1)}, bf16[1024,256]{1,0:T(8,128)(2,1)}, bf16[256,...) custom-call(s32[1]{0:T(128)} %bitcast.sc, bf16[1024,256]{1,0:T(8,128)(2,1)} %x0.7, ...), custom_call_target="tpu_custom_call" | custom-call | flops 7000000000 | bytes 1048576 | tf_op jit(solution)/shard_map/qkv/pallas_call | solution.py:138
  73.7 11.6 %collective-permute-start.17 = (bf16[384,256]{1,0:T(8,128)(2,1)S(1)}, bf16[384,256]{1,0:T(8,128)(2,1)S(1)}, u32[]{:S(2)}, u32[]{:S(2)}) collective-permute-start(bf16[384,256]{1,0:T(8,128)(2,1)S(1)} %get-tuple-element.328), channel_id=1, source_target_pairs={{0,8},{4,12},{8,16},{12,20},{16,24},{20,28},{1,9},{5,13},{9,17},{1... | collective-permute-start | bytes 589832 | tf_op jit(solution)/shard_map/ppermute | solution.py:39
  88.5 8.7 %collective-permute-done.20.refs_4_ = bf16[384,256]{1,0:T(8,128)(2,1)S(1)} collective-permute-done((bf16[384,256]{1,0:T(8,128)(2,1)S(1)}, bf16[384,256]{1,0:T(8,128)(2,1)S(1)}, u32[]{:S(2)}, u32[]{:S(2)}) %collective-permute-start.20) | collective-permute-done | bytes 196640 | tf_op jit(solution)/shard_map/ppermute | solution.py:39
  105.7 10.7 %collective-permute-start.13 = (bf16[384,256]{1,0:T(8,128)(2,1)S(1)}, bf16[384,256]{1,0:T(8,128)(2,1)S(1)}, u32[]{:S(2)}, u32[]{:S(2)}) collective-permute-start(bf16[384,256]{1,0:T(8,128)(2,1)S(1)} %get-tuple-element.330), channel_id=1, source_target_pairs={{0,8},{4,12},{8,16},{12,20},{16,24},{20,28},{1,9},{5,13},{9,17},{1... | collective-permute-start | bytes 589832 | tf_op jit(solution)/shard_map/ppermute | solution.py:39
  118.7 12.8 %attn_fwd.3 = (bf16[1024,128]{1,0:T(8,128)(2,1)}, f32[8,1024]{1,0:T(8,128)}) custom-call(s32[9]{0:T(128)} %pad_add_fusion.1.sc, bf16[1024,256]{1,0:T(8,128)(2,1)} %get-tuple-element.125.q_ref, s32[8,1024]{1,0:T(8,128)} %add_add_fusion.se_ref, bf16[384,256]{1,0:T(8,128)(2,1)} %copy-done.49, bf16[1024,256]{1,0:T(8,128)(2,1)} %copy-done.26, ...), custom_call_target="tpu_custom_call" | custom-call | flops 16999999488 | bytes 1048576 | tf_op jit(solution)/shard_map/attn_fwd/pallas_call | solution.py:263
  134.5 12.8 %attn_fwd.2 = (bf16[1024,128]{1,0:T(8,128)(2,1)}, f32[8,1024]{1,0:T(8,128)}) custom-call(s32[9]{0:T(128)} %pad_add_fusion.1.sc, bf16[1024,256]{1,0:T(8,128)(2,1)} %get-tuple-element.125.q_ref, s32[8,1024]{1,0:T(8,128)} %add_add_fusion.se_ref, bf16[384,256]{1,0:T(8,128)(2,1)} %copy-done.51, bf16[1024,256]{1,0:T(8,128)(2,1)} %copy-done.29, ...), custom_call_target="tpu_custom_call" | custom-call | flops 16999999488 | bytes 1048576 | tf_op jit(solution)/shard_map/attn_fwd/pallas_call | solution.py:263
  151.3 4.5 %collective-permute-done.31.c2 = bf16[256,256]{1,0:T(8,128)(2,1)S(1)} collective-permute-done((bf16[256,256]{1,0:T(8,128)(2,1)S(1)}, bf16[256,256]{1,0:T(8,128)(2,1)S(1)}, u32[]{:S(2)}, u32[]{:S(2)}) %collective-permute-start.31) | collective-permute-done | bytes 131104 | tf_op jit(solution)/shard_map/ppermute | solution.py:28
  158.3 4.3 proj.1
  163.4 13.9 %collective-permute-done.33.n0.n2 = bf16[256,1024]{1,0:T(8,128)(2,1)S(1)} collective-permute-done((bf16[256,1024]{1,0:T(8,128)(2,1)}, bf16[256,1024]{1,0:T(8,128)(2,1)S(1)}, u32[]{:S(2)}, u32[]{:S(2)}) %collective-permute-start.33) | collective-permute-done | bytes 524320 | tf_op jit(solution)/shard_map/ppermute | solution.py:28
  179.3 14.6 %all-gather.2.cloned.1.call-done.fc1.fc2 = bf16[2048,1024]{1,0:T(8,128)(2,1)} async-done(((bf16[2048,128]{1,0:T(8,128)(2,1)}), bf16[2048,1024]{1,0:T(8,128)(2,1)}) %all-gather.2.cloned.1.call-update) | async-done | bytes 4194320 | tf_op jit(solution)/shard_map/all_gather | solution.py:960
  193.9 10.2 %mlp.2 = (bf16[512,1024]{1,0:T(8,128)(2,1)}, bf16[512,1024]{1,0:T(8,128)(2,1)}, bf16[256,1024]{1,0:T(8,128)(2,1)}, bf16[256,1024]{1,0:T(8,128)(2,1)}, bf16[256,1...) custom-call(bf16[256,1024]{1,0:T(8,128)(2,1)} %copy-done.41, bf16[256,1024]{1,0:T(8,128)(2,1)} %copy-done.42, ...), custom_call_target="tpu_custom_call" | custom-call | flops 10000000000 | bytes 1048576 | tf_op jit(solution)/shard_map/mlp/pallas_call | solution.py:488
  208.3 10.3 %mlp.3 = (bf16[512,1024]{1,0:T(8,128)(2,1)}, bf16[512,1024]{1,0:T(8,128)(2,1)}, bf16[256,1024]{1,0:T(8,128)(2,1)}, bf16[256,1024]{1,0:T(8,128)(2,1)}, bf16[256,1...) custom-call(bf16[256,1024]{1,0:T(8,128)(2,1)} %get-tuple-element.143.n0, ...), custom_call_target="tpu_custom_call" | custom-call | flops 10000000000 | bytes 1048576 | tf_op jit(solution)/shard_map/mlp/pallas_call | solution.py:488
  220.3 9.3 %wgrads.1 = bf16[1024,2048]{1,0:T(8,128)(2,1)} custom-call(bf16[256,1024]{1,0:T(8,128)(2,1)} %get-tuple-element.143.n0, bf16[256,1024]{1,0:T(8,128)(2,1)} %copy-done.43, bf16[256,1024]{1,0:T(8,128)(2,1)} %copy-done.41, bf16[256,1024]{1,0:T(8,128)(2,1)} %copy-done.42, bf16[256,1024]{1,0:T(8,128)(2,1)} %copy-done.8, bf16[256,1024]{1,0:T(8,128)(2,1)} %copy-done.37, ...), custom_call_target="tpu_custom_call" | custom-call | flops 8999999488 | bytes 1048576 | tf_op jit(solution)/shard_map/wgrads/pallas_call | solution.py:530
  233.9 5.8 %mid.1 = (f32[256,1024]{1,0:T(8,128)}, bf16[256,1024]{1,0:T(8,128)(2,1)}, bf16[4,256,256]{2,1,0:T(8,128)(2,1)}, f32[8,1024]{1,0:T(8,128)}) custom-call(s32[1]{0:T(128)} %bitcast.sc, bf16[256,1024]{1,0:T(8,128)(2,1)} %get-tuple-element.152.a0, bf16[256,1024]{1,0:T(8,128)(2,1)} %copy-done.47, bf16[256,1024]{1,0:T(8,128)(2,1)} %copy-done.48, ...), custom_call_target="tpu_custom_call" | custom-call | flops 6000000000 | bytes 1048576 | tf_op jit(solution)/shard_map/mid/pallas_call | solution.py:589
  250.4 18.2 %attn_bwd.2 = (bf16[1024,128]{1,0:T(8,128)(2,1)}, bf16[384,256]{1,0:T(8,128)(2,1)}, bf16[1024,256]{1,0:T(8,128)(2,1)}, f32[1024,256]{1,0:T(8,128)}, bf16[1024,256]{1,0:T(8,128)(2,1)}, /*index=5*/bf16[384,256]{1,0:T(8,128)(2,1)}) custom-call(s32[9]{0:T(128)} %pad_add_fusion.1.sc, bf16[1024,256]{1,0:T(8,128)(2,1)} %get-tuple-element.125.q_ref, ...), custom_call_target="tpu_custom_call" | custom-call | flops 22000001024 | bytes 1048576 | tf_op jit(solution)/shard_map/attn_bwd/pallas_call | solution.py:359
  268.7 5.4 %collective-permute-start.57 = (bf16[1024,256]{1,0:T(8,128)(2,1)}, bf16[1024,256]{1,0:T(8,128)(2,1)S(1)}, u32[]{:S(2)}, u32[]{:S(2)}) collective-permute-start(bf16[1024,256]{1,0:T(8,128)(2,1)} %get-tuple-element.195), channel_id=1, source_target_pairs={{0,4},{4,8},{8,12},{12,16},{16,20},{20,24},{24,28},{1,5},{5,9},{9,... | collective-permute-start | bytes 1572872 | tf_op jit(solution)/shard_map/ppermute | solution.py:39
  280.5 18.2 %attn_bwd.3 = (bf16[1024,128]{1,0:T(8,128)(2,1)}, bf16[384,256]{1,0:T(8,128)(2,1)}, bf16[1024,256]{1,0:T(8,128)(2,1)}, f32[1024,256]{1,0:T(8,128)}, bf16[1024,256]{1,0:T(8,128)(2,1)}, /*index=5*/bf16[384,256]{1,0:T(8,128)(2,1)}) custom-call(s32[9]{0:T(128)} %pad_add_fusion.1.sc, bf16[1024,256]{1,0:T(8,128)(2,1)} %get-tuple-element.125.q_ref, ...), custom_call_target="tpu_custom_call" | custom-call | flops 22000001024 | bytes 1048576 | tf_op jit(solution)/shard_map/attn_bwd/pallas_call | solution.py:359
  300.5 7.3 %collective-permute-done.55 = bf16[384,256]{1,0:T(8,128)(2,1)S(1)} collective-permute-done((bf16[384,256]{1,0:T(8,128)(2,1)S(1)}, bf16[384,256]{1,0:T(8,128)(2,1)S(1)}, u32[]{:S(2)}, u32[]{:S(2)}) %collective-permute-start.55) | collective-permute-done | bytes 196640 | tf_op jit(solution)/shard_map/ppermute | solution.py:39
  311.2 5.3 %collective-permute-start.44 = (bf16[1024,256]{1,0:T(8,128)(2,1)}, bf16[1024,256]{1,0:T(8,128)(2,1)}, u32[]{:S(2)}, u32[]{:S(2)}) collective-permute-start(bf16[1024,256]{1,0:T(8,128)(2,1)} %get-tuple-element.173), channel_id=1, source_target_pairs={{0,4},{4,8},{8,12},{12,16},{16,20},{20,24},{24,28},{1,5},{5,9},{9,... | collective-permute-start | bytes 1572872 | tf_op jit(solution)/shard_map/ppermute | solution.py:39
  316.6 7.1 %collective-permute-done.48.a2 = bf16[256,1024]{1,0:T(8,128)(2,1)S(1)} collective-permute-done((bf16[256,1024]{1,0:T(8,128)(2,1)S(1)}, bf16[256,1024]{1,0:T(8,128)(2,1)S(1)}, u32[]{:S(2)}, u32[]{:S(2)}) %collective-permute-start.48) | collective-permute-done | bytes 524320 | tf_op jit(solution)/shard_map/ppermute | solution.py:28
  336.2 5.6 %collective-permute-start.45 = (bf16[384,256]{1,0:T(8,128)(2,1)}, bf16[384,256]{1,0:T(8,128)(2,1)S(1)}, u32[]{:S(2)}, u32[]{:S(2)}) collective-permute-start(bf16[384,256]{1,0:T(8,128)(2,1)} %get-tuple-element.174), channel_id=1, source_target_pairs={{0,8},{4,12},{8,16},{12,20},{16,24},{20,28},{1,9},{5,13},{9,17},{1... | collective-permute-start | bytes 589832 | tf_op jit(solution)/shard_map/ppermute | solution.py:39
  345.2 6.8 %collective-permute-done.42 = bf16[384,256]{1,0:T(8,128)(2,1)S(1)} collective-permute-done((bf16[384,256]{1,0:T(8,128)(2,1)}, bf16[384,256]{1,0:T(8,128)(2,1)S(1)}, u32[]{:S(2)}, u32[]{:S(2)}) %collective-permute-start.42) | collective-permute-done | bytes 196640 | tf_op jit(solution)/shard_map/ppermute | solution.py:39
  355.1 5.1 %qkv_grad.1 = bf16[24,256,128]{2,1,0:T(8,128)(2,1)} custom-call(bf16[1024,256]{1,0:T(8,128)(2,1)} %copy-done.2, bf16[1024,256]{1,0:T(8,128)(2,1)} %pad_maximum_fusion.3.gk, bf16[1024,256]{1,0:T(8,128)(2,1)} %pad_maximum_fusion.4.gv, bf16[1024,1024]{1,0:T(8,128)(2,1)} %get-tuple-element.202.n1), custom_call_target="tpu_custom_call" | custom-call | flops 5000000000 | bytes 1048576 | tf_op jit(solution)/shard_map/qkv_grad/pallas_call | solution.py:668
  360.2 6.1 %gn1.1 = (bf16[256,1024]{1,0:T(8,128)(2,1)}, bf16[256,1024]{1,0:T(8,128)(2,1)}, bf16[256,1024]{1,0:T(8,128)(2,1)}, bf16[256,1024]{1,0:T(8,128)(2,1)}) custom-call(s32[1]{0:T(128)} %bitcast.sc, bf16[1024,128]{1,0:T(8,128)(2,1)} %get-tuple-element.190.gq0, bf16[1024,128]{1,0:T(8,128)(2,1)} %get-tuple-element.191.gq1, bf16[1024,256]{1,0:T(8,128)(2,1)} %pad_maximum_fusion.3.gk, ...), custom_call_target="tpu_custom_call" | custom-call | flops 6000000000 | bytes 1048576 | tf_op jit(solution)/shard_map/gn1/pallas_call | solution.py:641
  366.7 5.7 %norm_sums.1 = f32[8,1024]{1,0:T(8,128)} custom-call(s32[1]{0:T(128)} %bitcast.sc, bf16[256,1024]{1,0:T(8,128)(2,1)} %get-tuple-element.205.a0, bf16[256,1024]{1,0:T(8,128)(2,1)} %get-tuple-element.206.a1, bf16[256,1024]{1,0:T(8,128)(2,1)} %get-tuple-element.207.a2, bf16[256,1024]{1,0:T(8,128)(2,1)} %get-tuple-element.208.a3, bf16[1024,256]{1,0:T(8,128)(2,1)} %x0.7, ...), custom_call_target="tpu_custom_call" | custom-call | flops 5000000000 | bytes 1048576 | tf_op jit(solution)/shard_map/norm_sums/pallas_call | solution.py:701
  384.2 4.6 %collective-permute-start.73 = (bf16[128,256]{0,1:T(8,128)(2,1)S(1)}, bf16[128,256]{0,1:T(8,128)(2,1)S(1)}, u32[]{:S(2)}, u32[]{:S(2)}) collective-permute-start(bf16[128,256]{0,1:T(8,128)(2,1)S(1)} %fusion.15), channel_id=1, source_target_pairs={{0,16},{4,20},{8,24},{12,28},{16,0},{20,4},{24,8},{28,12},{1,17},{... | collective-permute-start | bytes 196616 | tf_op jit(solution)/shard_map/ppermute | solution.py:33
  388.8 4.5 %collective-permute-done.64.a2 = bf16[256,1024]{1,0:T(8,128)(2,1)S(1)} collective-permute-done((bf16[256,1024]{1,0:T(8,128)(2,1)S(1)}, bf16[256,1024]{1,0:T(8,128)(2,1)S(1)}, u32[]{:S(2)}, u32[]{:S(2)}) %collective-permute-start.64) | collective-permute-done | bytes 524320 | tf_op jit(solution)/shard_map/ppermute | solution.py:28
  404.8 4.9 %collective-permute-start.76 = (f32[28,128]{1,0:T(8,128)S(1)}, f32[28,128]{1,0:T(8,128)S(1)}, u32[]{:S(2)}, u32[]{:S(2)}) collective-permute-start(f32[28,128]{1,0:T(8,128)S(1)} %add.249), channel_id=1, source_target_pairs={{0,16},{4,20},{8,24},{12,28},{16,0},{20,4},{24,8},{28,12},{1,17},{... | collective-permute-start | bytes 43016 | tf_op jit(solution)/shard_map/ppermute | solution.py:33
  421.0 5.1 %collective-permute-done.70 = bf16[3,256,128]{2,1,0:T(8,128)(2,1)S(1)} collective-permute-done((bf16[3,256,128]{2,1,0:T(8,128)(2,1)S(1)}, bf16[3,256,128]{2,1,0:T(8,128)(2,1)S(1)}, u32[]{:S(2)}, u32[]{:S(2)}) %collective-permute-start.70) | collective-permute-done | bytes 196640 | tf_op jit(solution)/shard_map/ppermute | solution.py:33
  (360 shorter events, 151.3 us)
Async XLA Ops:
  7.2 186.7 %all-gather.2.cloned.1.call-start = ((), (), s32[]{:S(2)}) async-start(), calls=%async_computation.1 | async-start | bytes 4718592 | tf_op jit(solution)/shard_map/all_gather | solution.py:960
  7.2 52.7 %collective-permute-start = (bf16[1024,256]{1,0:T(8,128)(2,1)}, bf16[1024,256]{1,0:T(8,128)(2,1)}, u32[]{:S(2)}, u32[]{:S(2)}) collective-permute-start(bf16[1024,256]{1,0:T(8,128)(2,1)} %x0.7), channel_id=1, source_target_pairs={{0,1},{1,0},{2,3},{3,2},{4,5},{5,4},{6,7},{7,6},{8,9},{9,8},{10,11... | collective-permute-start | bytes 1572872 | tf_op jit(solution)/shard_map/ppermute | solution.py:28
  7.8 41.0 %collective-permute-start.1 = (bf16[1024,256]{1,0:T(8,128)(2,1)}, bf16[1024,256]{1,0:T(8,128)(2,1)}, u32[]{:S(2)}, u32[]{:S(2)}) collective-permute-start(bf16[1024,256]{1,0:T(8,128)(2,1)} %x0.7), channel_id=1, source_target_pairs={{0,2},{1,3},{2,0},{3,1},{4,6},{5,7},{6,4},{7,5},{8,10},{9,11},{10,... | collective-permute-start | bytes 1572872 | tf_op jit(solution)/shard_map/ppermute | solution.py:28
  26.1 20.9 %collective-permute-start.6 = (bf16[256,512]{1,0:T(8,128)(2,1)S(1)}, bf16[256,512]{1,0:T(8,128)(2,1)S(1)}, u32[]{:S(2)}, u32[]{:S(2)}) collective-permute-start(bf16[256,512]{1,0:T(8,128)(2,1)S(1)} %constant_dynamic-update-slice_fusion), channel_id=1, source_target_pairs={{0,16},{4,20},{8,24},{12,28},{16,0},{20,4},{24,8},{28,12},{1,17},{... | collective-permute-start | bytes 786440 | tf_op jit(solution)/shard_map/ppermute | solution.py:33
  31.7 16.8 %collective-permute-start.8 = (bf16[256,512]{1,0:T(8,128)(2,1)S(1)}, bf16[256,512]{1,0:T(8,128)(2,1)S(1)}, u32[]{:S(2)}, u32[]{:S(2)}) collective-permute-start(bf16[256,512]{1,0:T(8,128)(2,1)S(1)} %constant_dynamic-update-slice_fusion), channel_id=1, source_target_pairs={{0,24},{4,28},{8,16},{12,20},{16,8},{20,12},{24,0},{28,4},{1,25},{... | collective-permute-start | bytes 786440 | tf_op jit(solution)/shard_map/ppermute | solution.py:33
  47.0 52.8 %collective-permute-start.25 = (bf16[256,256]{1,0:T(8,128)(2,1)S(1)}, bf16[256,256]{1,0:T(8,128)(2,1)S(1)}, u32[]{:S(2)}, u32[]{:S(2)}) collective-permute-start(bf16[256,256]{1,0:T(8,128)(2,1)S(1)} %get-tuple-element.325), channel_id=1, source_target_pairs={{0,2},{1,3},{2,0},{3,1},{4,6},{5,7},{6,4},{7,5},{8,10},{9,11},{10,... | collective-permute-start | bytes 393224 | tf_op jit(solution)/shard_map/ppermute | solution.py:28
  69.1 28.8 %collective-permute-start.18 = (bf16[1024,256]{1,0:T(8,128)(2,1)}, bf16[1024,256]{1,0:T(8,128)(2,1)S(1)}, u32[]{:S(2)}, u32[]{:S(2)}) collective-permute-start(bf16[1024,256]{1,0:T(8,128)(2,1)} %get-tuple-element.131.refs_2_), channel_id=1, source_target_pairs={{0,4},{4,8},{8,12},{12,16},{16,20},{20,24},{24,28},{1,5},{5,9},{9,... | collective-permute-start | bytes 1572872 | tf_op jit(solution)/shard_map/ppermute | solution.py:39
  71.3 26.6 %collective-permute-start.19 = (bf16[1024,256]{1,0:T(8,128)(2,1)}, bf16[1024,256]{1,0:T(8,128)(2,1)S(1)}, u32[]{:S(2)}, u32[]{:S(2)}) collective-permute-start(bf16[1024,256]{1,0:T(8,128)(2,1)} %get-tuple-element.131.refs_2_), channel_id=1, source_target_pairs={{4,0},{8,4},{12,8},{16,12},{20,16},{24,20},{28,24},{5,1},{9,5},{13... | collective-permute-start | bytes 1572872 | tf_op jit(solution)/shard_map/ppermute | solution.py:39
  73.7 14.8 %collective-permute-start.17 = (bf16[384,256]{1,0:T(8,128)(2,1)S(1)}, bf16[384,256]{1,0:T(8,128)(2,1)S(1)}, u32[]{:S(2)}, u32[]{:S(2)}) collective-permute-start(bf16[384,256]{1,0:T(8,128)(2,1)S(1)} %get-tuple-element.328), channel_id=1, source_target_pairs={{0,8},{4,12},{8,16},{12,20},{16,24},{20,28},{1,9},{5,13},{9,17},{1... | collective-permute-start | bytes 589832 | tf_op jit(solution)/shard_map/ppermute | solution.py:39
  98.0 321.9 %reduce-scatter.2.cloned.1.call-start = ((), (), s32[]{:S(2)}) async-start(), calls=%async_computation.2 | async-start | bytes 4718592 | tf_op jit(solution)/shard_map/reduce_scatter | solution.py:985
  100.1 18.0 %collective-permute-start.28 = (bf16[256,1024]{1,0:T(8,128)(2,1)S(1)}, bf16[256,1024]{1,0:T(8,128)(2,1)S(1)}, u32[]{:S(2)}, u32[]{:S(2)}) collective-permute-start(bf16[256,1024]{1,0:T(8,128)(2,1)S(1)} %multiply_convert_fusion.g0), channel_id=1, source_target_pairs={{0,2},{1,3},{2,0},{3,1},{4,6},{5,7},{6,4},{7,5},{8,10},{9,11},{10,... | collective-permute-start | bytes 1572872 | tf_op jit(solution)/shard_map/ppermute | solution.py:28
  103.0 30.0 %collective-permute-start.14 = (bf16[1024,256]{1,0:T(8,128)(2,1)S(1)}, bf16[1024,256]{1,0:T(8,128)(2,1)S(1)}, u32[]{:S(2)}, u32[]{:S(2)}) collective-permute-start(bf16[1024,256]{1,0:T(8,128)(2,1)S(1)} %copy-done.14), channel_id=1, source_target_pairs={{0,4},{4,8},{8,12},{12,16},{16,20},{20,24},{24,28},{1,5},{5,9},{9,... | collective-permute-start | bytes 1572872 | tf_op jit(solution)/shard_map/ppermute | solution.py:39
  104.3 29.2 %collective-permute-start.15 = (bf16[1024,256]{1,0:T(8,128)(2,1)S(1)}, bf16[1024,256]{1,0:T(8,128)(2,1)S(1)}, u32[]{:S(2)}, u32[]{:S(2)}) collective-permute-start(bf16[1024,256]{1,0:T(8,128)(2,1)S(1)} %copy-done.14), channel_id=1, source_target_pairs={{4,0},{8,4},{12,8},{16,12},{20,16},{24,20},{28,24},{5,1},{9,5},{13... | collective-permute-start | bytes 1572872 | tf_op jit(solution)/shard_map/ppermute | solution.py:39
  105.7 26.0 %collective-permute-start.13 = (bf16[384,256]{1,0:T(8,128)(2,1)S(1)}, bf16[384,256]{1,0:T(8,128)(2,1)S(1)}, u32[]{:S(2)}, u32[]{:S(2)}) collective-permute-start(bf16[384,256]{1,0:T(8,128)(2,1)S(1)} %get-tuple-element.330), channel_id=1, source_target_pairs={{0,8},{4,12},{8,16},{12,20},{16,24},{20,28},{1,9},{5,13},{9,17},{1... | collective-permute-start | bytes 589832 | tf_op jit(solution)/shard_map/ppermute | solution.py:39
  116.3 15.4 %collective-permute-start.16 = (bf16[384,256]{1,0:T(8,128)(2,1)S(1)}, bf16[384,256]{1,0:T(8,128)(2,1)S(1)}, u32[]{:S(2)}, u32[]{:S(2)}) collective-permute-start(bf16[384,256]{1,0:T(8,128)(2,1)S(1)} %get-tuple-element.329), channel_id=1, source_target_pairs={{8,0},{12,4},{16,8},{20,12},{24,16},{28,20},{9,1},{13,5},{17,9},{2... | collective-permute-start | bytes 589832 | tf_op jit(solution)/shard_map/ppermute | solution.py:39
  118.1 14.8 %collective-permute-start.22 = (bf16[256,1024]{1,0:T(8,128)(2,1)S(1)}, bf16[256,1024]{1,0:T(8,128)(2,1)S(1)}, u32[]{:S(2)}, u32[]{:S(2)}) collective-permute-start(bf16[256,1024]{1,0:T(8,128)(2,1)S(1)} %copy-done.28), channel_id=1, source_target_pairs={{0,2},{1,3},{2,0},{3,1},{4,6},{5,7},{6,4},{7,5},{8,10},{9,11},{10,... | collective-permute-start | bytes 1572872 | tf_op jit(solution)/shard_map/ppermute | solution.py:28
  131.7 15.7 %collective-permute-start.27 = (bf16[256,1024]{1,0:T(8,128)(2,1)S(1)}, bf16[256,1024]{1,0:T(8,128)(2,1)S(1)}, u32[]{:S(2)}, u32[]{:S(2)}) collective-permute-start(bf16[256,1024]{1,0:T(8,128)(2,1)S(1)} %multiply_convert_fusion.g0), channel_id=1, source_target_pairs={{0,1},{1,0},{2,3},{3,2},{4,5},{5,4},{6,7},{7,6},{8,9},{9,8},{10,11... | collective-permute-start | bytes 1572872 | tf_op jit(solution)/shard_map/ppermute | solution.py:28
  131.8 15.6 %collective-permute-start.29 = (bf16[256,1024]{1,0:T(8,128)(2,1)S(1)}, bf16[256,1024]{1,0:T(8,128)(2,1)S(1)}, u32[]{:S(2)}, u32[]{:S(2)}) collective-permute-start(bf16[256,1024]{1,0:T(8,128)(2,1)S(1)} %collective-permute-done.28.g0.g2), channel_id=1, source_target_pairs={{0,1},{1,0},{2,3},{3,2},{4,5},{5,4},{6,7},{7,6},{8,9},{9,8},{10,11... | collective-permute-start | bytes 1572872 | tf_op jit(solution)/shard_map/ppermute | solution.py:28
  268.6 30.1 %collective-permute-start.47 = (bf16[256,1024]{1,0:T(8,128)(2,1)S(1)}, bf16[256,1024]{1,0:T(8,128)(2,1)S(1)}, u32[]{:S(2)}, u32[]{:S(2)}) collective-permute-start(bf16[256,1024]{1,0:T(8,128)(2,1)S(1)} %copy-done.33), channel_id=1, source_target_pairs={{0,1},{1,0},{2,3},{3,2},{4,5},{5,4},{6,7},{7,6},{8,9},{9,8},{10,11... | collective-permute-start | bytes 1572872 | tf_op jit(solution)/shard_map/ppermute | solution.py:28
  268.7 40.5 %collective-permute-start.57 = (bf16[1024,256]{1,0:T(8,128)(2,1)}, bf16[1024,256]{1,0:T(8,128)(2,1)S(1)}, u32[]{:S(2)}, u32[]{:S(2)}) collective-permute-start(bf16[1024,256]{1,0:T(8,128)(2,1)} %get-tuple-element.195), channel_id=1, source_target_pairs={{0,4},{4,8},{8,12},{12,16},{16,20},{20,24},{24,28},{1,5},{5,9},{9,... | collective-permute-start | bytes 1572872 | tf_op jit(solution)/shard_map/ppermute | solution.py:39
  274.2 35.2 %collective-permute-start.56 = (bf16[1024,256]{1,0:T(8,128)(2,1)}, bf16[1024,256]{1,0:T(8,128)(2,1)S(1)}, u32[]{:S(2)}, u32[]{:S(2)}) collective-permute-start(bf16[1024,256]{1,0:T(8,128)(2,1)} %get-tuple-element.194), channel_id=1, source_target_pairs={{4,0},{8,4},{12,8},{16,12},{20,16},{24,20},{28,24},{5,1},{9,5},{13... | collective-permute-start | bytes 1572872 | tf_op jit(solution)/shard_map/ppermute | solution.py:39
  275.5 24.9 %collective-permute-start.58 = (bf16[384,256]{1,0:T(8,128)(2,1)}, bf16[384,256]{1,0:T(8,128)(2,1)S(1)}, u32[]{:S(2)}, u32[]{:S(2)}) collective-permute-start(bf16[384,256]{1,0:T(8,128)(2,1)} %get-tuple-element.196), channel_id=1, source_target_pairs={{0,8},{4,12},{8,16},{12,20},{16,24},{20,28},{1,9},{5,13},{9,17},{1... | collective-permute-start | bytes 589832 | tf_op jit(solution)/shard_map/ppermute | solution.py:39
  279.5 31.0 %collective-permute-start.53 = (bf16[256,1024]{1,0:T(8,128)(2,1)S(1)}, bf16[256,1024]{1,0:T(8,128)(2,1)S(1)}, u32[]{:S(2)}, u32[]{:S(2)}) collective-permute-start(bf16[256,1024]{1,0:T(8,128)(2,1)S(1)} %copy-done.6), channel_id=1, source_target_pairs={{0,2},{1,3},{2,0},{3,1},{4,6},{5,7},{6,4},{7,5},{8,10},{9,11},{10,... | collective-permute-start | bytes 1572872 | tf_op jit(solution)/shard_map/ppermute | solution.py:28
  300.4 27.6 %collective-permute-start.52 = (bf16[256,1024]{1,0:T(8,128)(2,1)S(1)}, bf16[256,1024]{1,0:T(8,128)(2,1)S(1)}, u32[]{:S(2)}, u32[]{:S(2)}) collective-permute-start(bf16[256,1024]{1,0:T(8,128)(2,1)S(1)} %copy-done.6), channel_id=1, source_target_pairs={{0,1},{1,0},{2,3},{3,2},{4,5},{5,4},{6,7},{7,6},{8,9},{9,8},{10,11... | collective-permute-start | bytes 1572872 | tf_op jit(solution)/shard_map/ppermute | solution.py:28
  307.7 44.3 %collective-permute-start.43 = (bf16[1024,256]{1,0:T(8,128)(2,1)}, bf16[1024,256]{1,0:T(8,128)(2,1)S(1)}, u32[]{:S(2)}, u32[]{:S(2)}) collective-permute-start(bf16[1024,256]{1,0:T(8,128)(2,1)} %get-tuple-element.172), channel_id=1, source_target_pairs={{4,0},{8,4},{12,8},{16,12},{20,16},{24,20},{28,24},{5,1},{9,5},{13... | collective-permute-start | bytes 1572872 | tf_op jit(solution)/shard_map/ppermute | solution.py:39
  310.5 18.5 %collective-permute-start.54 = (bf16[256,1024]{1,0:T(8,128)(2,1)S(1)}, bf16[256,1024]{1,0:T(8,128)(2,1)S(1)}, u32[]{:S(2)}, u32[]{:S(2)}) collective-permute-start(bf16[256,1024]{1,0:T(8,128)(2,1)S(1)} %collective-permute-done.53), channel_id=1, source_target_pairs={{0,1},{1,0},{2,3},{3,2},{4,5},{5,4},{6,7},{7,6},{8,9},{9,8},{10,11... | collective-permute-start | bytes 1572872 | tf_op jit(solution)/shard_map/ppermute | solution.py:28
  311.2 40.8 %collective-permute-start.44 = (bf16[1024,256]{1,0:T(8,128)(2,1)}, bf16[1024,256]{1,0:T(8,128)(2,1)}, u32[]{:S(2)}, u32[]{:S(2)}) collective-permute-start(bf16[1024,256]{1,0:T(8,128)(2,1)} %get-tuple-element.173), channel_id=1, source_target_pairs={{0,4},{4,8},{8,12},{12,16},{16,20},{20,24},{24,28},{1,5},{5,9},{9,... | collective-permute-start | bytes 1572872 | tf_op jit(solution)/shard_map/ppermute | solution.py:39
  333.9 18.1 %collective-permute-start.42 = (bf16[384,256]{1,0:T(8,128)(2,1)}, bf16[384,256]{1,0:T(8,128)(2,1)S(1)}, u32[]{:S(2)}, u32[]{:S(2)}) collective-permute-start(bf16[384,256]{1,0:T(8,128)(2,1)} %get-tuple-element.171), channel_id=1, source_target_pairs={{8,0},{12,4},{16,8},{20,12},{24,16},{28,20},{9,1},{13,5},{17,9},{2... | collective-permute-start | bytes 589832 | tf_op jit(solution)/shard_map/ppermute | solution.py:39
  336.2 15.8 %collective-permute-start.45 = (bf16[384,256]{1,0:T(8,128)(2,1)}, bf16[384,256]{1,0:T(8,128)(2,1)S(1)}, u32[]{:S(2)}, u32[]{:S(2)}) collective-permute-start(bf16[384,256]{1,0:T(8,128)(2,1)} %get-tuple-element.174), channel_id=1, source_target_pairs={{0,8},{4,12},{8,16},{12,20},{16,24},{20,28},{1,9},{5,13},{9,17},{1... | collective-permute-start | bytes 589832 | tf_op jit(solution)/shard_map/ppermute | solution.py:39
  341.8 33.5 %collective-permute-start.71 = (bf16[2,2,128,256]{2,3,0,1:T(8,128)(2,1)S(1)}, bf16[2,2,128,256]{2,3,0,1:T(8,128)(2,1)S(1)}, u32[]{:S(2)}, u32[]{:S(2)}) collective-permute-start(bf16[2,2,128,256]{2,3,0,1:T(8,128)(2,1)S(1)} %bitcast.132), channel_id=1, source_target_pairs={{0,8},{4,12},{8,0},{12,4},{16,24},{20,28},{24,16},{28,20},{1,9},{5... | collective-permute-start | bytes 786440 | tf_op jit(solution)/shard_map/ppermute | solution.py:33
  366.2 22.6 %collective-permute-start.62 = (bf16[256,1024]{1,0:T(8,128)(2,1)}, bf16[256,1024]{1,0:T(8,128)(2,1)S(1)}, u32[]{:S(2)}, u32[]{:S(2)}) collective-permute-start(bf16[256,1024]{1,0:T(8,128)(2,1)} %get-tuple-element.206.a1), channel_id=1, source_target_pairs={{0,1},{1,0},{2,3},{3,2},{4,5},{5,4},{6,7},{7,6},{8,9},{9,8},{10,11... | collective-permute-start | bytes 1572872 | tf_op jit(solution)/shard_map/ppermute | solution.py:28
  375.6 26.5 %collective-permute-start.68 = (bf16[2,2,3,256,128]{4,3,2,0,1:T(8,128)(2,1)S(1)}, bf16[2,2,3,256,128]{4,3,2,0,1:T(8,128)(2,1)S(1)}, u32[]{:S(2)}, u32[]{:S(2)}) collective-permute-start(bf16[2,2,3,256,128]{4,3,2,0,1:T(8,128)(2,1)S(1)} %copy_bitcast_fusion), channel_id=1, source_target_pairs={{0,8},{4,12},{8,0},{12,4},{16,24},{20,28},{24,16},{28,20},{1,9},{5... | collective-permute-start | bytes 2359304 | tf_op jit(solution)/shard_map/ppermute | solution.py:33
  (107 other events, 1161.0 us)
Sparse Core Ops, SparseCore 0:
  98.1 95.7 all-gather.1
  245.1 122.7 reduce-scatter.1
